TPU v7x, 128 devices: a whole 4x4x4 slice. The times are simulated.
128 devices in a mesh: section: 4 (over y), fsdp: 32 (over x, z, core).
Axes of the slice: x: 4, y: 4, z: 4, core: 2. Of those that a mesh axis runs over, the one named last changes fastest.
Arguments:
- inputs: bfloat16 [3, 128, 3072], P(None, 'fsdp'), may hold values from -6 to 6
- gain: float32 [4, 3072], P('section'), may hold values from 0.25 to 1.75
- w_gate: bfloat16 [4, 4, 3072, 8192], P('section', None, None, 'fsdp'), may hold values from -0.109375 to 0.109375
- w_up: bfloat16 [4, 4, 3072, 8192], P('section', None, None, 'fsdp'), may hold values from -0.109375 to 0.109375
- w_down: bfloat16 [4, 4, 8192, 3072], P('section', None, 'fsdp'), may hold values from -0.0625 to 0.0625
- routes: int32 [4, 3, 128, 2], P('section'), may hold values from 0 to 3, all different within a row
- shares: float32 [4, 3, 128, 2], P('section'), may hold values from 0.1 to 1
Outputs:
- hidden: bfloat16 [4, 3, 128, 3072], P('section', None, 'fsdp')
Inputs may be any that keep to these rules, and one draw needn't show every extreme that they name: `routes`: each token names 2 different experts, and every expert is named in each microbatch of each layer.
All inputs are finite; a program needn't handle non-finite values.
Results may differ from a plain program's by a relative error of at most 0.014.
Values may be sent and summed in bfloat16 or wider, within the bound.
A program may use at most 128 MiB of HBM per device.

v0:
```python
import jax
import jax.numpy as jnp
from jax import lax
from jax.sharding import PartitionSpec as P


def passed_along(array, axis, by):
    devices = lax.axis_size(axis)
    pairs = [(i, i + by) for i in range(devices) if 0 <= i + by < devices]
    return lax.ppermute(array, axis, pairs)


def sibling(array, axis):
    devices = lax.axis_size(axis)
    return lax.ppermute(array, axis, [(i, i ^ 1) for i in range(devices)])


def rms_norm(rows, gain_row):
    values = rows.astype(jnp.float32)
    scale = lax.rsqrt(jnp.mean(values * values, axis=-1, keepdims=True) + 1e-05)
    return (values * scale * gain_row[None, :]).astype(jnp.bfloat16)


def combine_weights(route_layer, share_layer, experts, shards):
    micro, tokens, top = route_layer.shape
    per = tokens // shards
    onehot = (route_layer[..., None] == jnp.arange(experts, dtype=route_layer.dtype)).astype(jnp.float32)
    coef = jnp.sum(onehot * share_layer[..., None], axis=2)
    return coef.reshape(micro, shards, per, experts).transpose(0, 3, 1, 2)


def expert_mix(rows, coef, gate_w, up_w, down_w):
    gate = jnp.einsum("fmd,edh->efmh", rows, gate_w, preferred_element_type=jnp.float32)
    upward = jnp.einsum("fmd,edh->efmh", rows, up_w, preferred_element_type=jnp.float32)
    gated = (jax.nn.silu(gate) * upward * coef[..., None]).astype(jnp.bfloat16)
    return jnp.einsum("efmh,ehd->fmd", gated, down_w, preferred_element_type=jnp.float32)


def on_device(inputs, gain, w_gate, w_up, w_down, routes, shares):
    sections = lax.axis_size("section")
    shards = lax.axis_size("fsdp")
    chips = shards // 2
    section_index = lax.axis_index("section")
    core = lax.axis_index("fsdp") % 2
    groups = [list(range(c, shards, 2)) for c in range(2)]
    micro, local, width = inputs.shape
    gain_row = gain[0]
    gate_w, up_w, down_w = w_gate[0], w_up[0], w_down[0]
    experts = gate_w.shape[0]
    coef = combine_weights(routes[0], shares[0], experts, shards)
    coef = coef.reshape(micro, experts, chips, 2, local)
    coef = jnp.concatenate(
        [
            lax.dynamic_index_in_dim(coef, core, 3, keepdims=False),
            lax.dynamic_index_in_dim(coef, 1 - core, 3, keepdims=False),
        ],
        axis=2,
    )
    output = jnp.zeros_like(inputs)
    carried = None
    for tick in range(micro + sections - 1):
        position = tick - section_index
        valid = jnp.logical_and(position >= 0, position < micro)
        clipped = jnp.clip(position, 0, micro - 1)
        entry = lax.dynamic_index_in_dim(inputs, clipped, 0, keepdims=False)
        coef_now = lax.dynamic_index_in_dim(coef, clipped, 0, keepdims=False)
        current = entry if carried is None else jnp.where(section_index == 0, entry, carried)
        normed = rms_norm(current, gain_row)
        spread = jnp.broadcast_to(normed[None], (chips,) + normed.shape)
        near = lax.all_to_all(spread, "fsdp", 0, 0, tiled=True, axis_index_groups=groups)
        rows = jnp.concatenate([near, sibling(near, "fsdp")], axis=0)
        partial_value = expert_mix(rows, coef_now, gate_w, up_w, down_w)
        chip_sum = partial_value[:chips] + sibling(partial_value[chips:], "fsdp")
        pieces = lax.all_to_all(
            chip_sum.astype(jnp.bfloat16), "fsdp", 0, 0, tiled=True, axis_index_groups=groups
        )
        mixed = jnp.sum(pieces.astype(jnp.float32), axis=0)
        result = (current.astype(jnp.float32) + mixed).astype(jnp.bfloat16)
        if tick + 1 < micro + sections - 1:
            carried = passed_along(result, "section", 1)
        updated = lax.dynamic_update_index_in_dim(output, result, clipped, 0)
        output = jnp.where(valid, updated, output)
    return output[None]


def solution(mesh):
    placed = (
        P(None, "fsdp", None),
        P("section", None),
        P("section", None, None, "fsdp"),
        P("section", None, None, "fsdp"),
        P("section", None, "fsdp", None),
        P("section", None, None, None),
        P("section", None, None, None),
    )
    return jax.shard_map(
        on_device,
        mesh=mesh,
        in_specs=placed,
        out_specs=P("section", None, "fsdp", None),
        check_vma=False,
    )
```

profile of v0, /device:TPU:24, one launch (start us, length us, event | category | flops | bytes accessed | tf_op | source)
XLA Modules:
  0.0 293.5 jit_solution(10684785438337031523)
XLA Ops:
  0.0 0.9 fusion.134
  0.9 0.8 fusion.165
  1.8 17.5 %all_to_all.60 = bf16[16,4,3072]{2,1,0:T(4,128)(2,1)S(1)} all-to-all(bf16[16,4,3072]{2,1,0:T(4,128)(2,1)S(1)} %broadcast_in_dim.39), channel_id=1, replica_groups={{0,2,4,6,8,10,12,14,16,18,20,22,24,26,28,30},{1,3,5,7,9,11,13,15,17,19,..., dimensions={0} | all-to-all | bytes 786432 | tf_op jit(solution)/shard_map/all_to_all | solution.py:70
  19.6 0.7 select_reduce_fusion
  21.3 3.8 %fusion.54 = f32[4,32,4,256]{3,1,0,2:T(8,128)S(1)} fusion(bf16[1,4,3072,256]{3,2,1,0:T(8,128)(2,1)} %param.9, bf16[16,4,3072]{2,0,1:T(8,128)(2,1)S(1)} %collective-permute-done, bf16[16,4,3072]{2,0,1:T(8,128)(2,1)S(1)} %copy.75), kind=kOutput, calls=%fused_computation.42 | convolution fusion | flops 806879232 | bytes 7602176 | tf_op jit(solution)/shard_map/fmd,edh->efmh/dot_general | solution.py:33
  25.1 6.6 %fusion.36 = f32[32,4,3072]{2,0,1:T(8,128)S(1)} fusion(bf16[1,4,256,3072]{3,2,1,0:T(8,128)(2,1)} %param.11, f32[4,32,4,256]{3,1,0,2:T(8,128)S(1)} %fusion.54, bf16[1,4,3072,256]{3,2,1,0:T(8,128)(2,1)} %param.10, bf16[16,4,3072]{2,0,1:T(8,128)(2,1)S(1)} %collective-permute-done, bf16[16,4,3072]{2,0,1:T(8,128)(2,1)S(1)} %copy.75, f32[4,32,4]{1,0,2:T(4,128)S(1)} %copy.78), kind=kOutput, calls=%fused_computation.36 | convolution fusion | flops 1613103104 | bytes 15468544 | tf_op jit(solution)/shard_map/efmh,ehd->fmd/dot_general | solution.py:36
  31.8 0.4 collective-permute-start.1
  32.2 1.9 collective-permute-done.1
  34.3 0.3 copy.79
  34.6 13.9 %all_to_all.61 = bf16[16,4,3072]{2,1,0:T(4,128)(2,1)S(1)} all-to-all(bf16[16,4,3072]{2,1,0:T(4,128)(2,1)S(1)} %copy.79), channel_id=1, replica_groups={{0,2,4,6,8,10,12,14,16,18,20,22,24,26,28,30},{1,3,5,7,9,11,13,15,17,19,..., dimensions={0} | all-to-all | bytes 786432 | tf_op jit(solution)/shard_map/all_to_all | solution.py:74
  48.6 1.3 collective-permute-start.2
  50.0 4.4 %collective-permute-done.2 = bf16[4,3072]{1,0:T(4,128)(2,1)S(1)} collective-permute-done((bf16[4,3072]{1,0:T(4,128)(2,1)S(1)}, bf16[4,3072]{1,0:T(4,128)(2,1)S(1)}, u32[]{:S(2)}, u32[]{:S(2)}) %collective-permute-start.2) | collective-permute-done | bytes 24608 | tf_op jit(solution)/shard_map/ppermute | solution.py:10
  54.7 12.6 %all_to_all.62 = bf16[16,4,3072]{2,1,0:T(4,128)(2,1)S(1)} all-to-all(bf16[16,4,3072]{2,1,0:T(4,128)(2,1)S(1)} %broadcast_in_dim.40), channel_id=1, replica_groups={{0,2,4,6,8,10,12,14,16,18,20,22,24,26,28,30},{1,3,5,7,9,11,13,15,17,19,..., dimensions={0} | all-to-all | bytes 786432 | tf_op jit(solution)/shard_map/all_to_all | solution.py:70
  67.6 1.7 collective-permute-done.3
  69.3 3.8 %fusion.57 = f32[4,32,4,256]{3,1,0,2:T(8,128)S(1)} fusion(bf16[1,4,3072,256]{3,2,1,0:T(8,128)(2,1)} %param.9, bf16[16,4,3072]{2,0,1:T(8,128)(2,1)S(1)} %collective-permute-done.3, bf16[16,4,3072]{2,0,1:T(8,128)(2,1)S(1)} %copy.81), kind=kOutput, calls=%fused_computation.43 | convolution fusion | flops 806879232 | bytes 7602176 | tf_op jit(solution)/shard_map/fmd,edh->efmh/dot_general | solution.py:33
  73.1 6.6 %fusion.39 = f32[32,4,3072]{2,0,1:T(8,128)S(1)} fusion(bf16[1,4,256,3072]{3,2,1,0:T(8,128)(2,1)} %param.11, f32[4,32,4,256]{3,1,0,2:T(8,128)S(1)} %fusion.57, bf16[1,4,3072,256]{3,2,1,0:T(8,128)(2,1)} %param.10, bf16[16,4,3072]{2,0,1:T(8,128)(2,1)S(1)} %collective-permute-done.3, bf16[16,4,3072]{2,0,1:T(8,128)(2,1)S(1)} %copy.81, f32[4,32,4]{1,0,2:T(4,128)S(1)} %copy.82), kind=kOutput, calls=%fused_computation.37 | convolution fusion | flops 1613103104 | bytes 15468544 | tf_op jit(solution)/shard_map/efmh,ehd->fmd/dot_general | solution.py:36
  80.0 2.2 collective-permute-done.4
  82.2 1.0 copy.83
  83.3 3.7 %all-to-all-start.3 = ((bf16[16,4,3072]{2,1,0:T(4,128)(2,1)}), bf16[16,4,3072]{2,1,0:T(4,128)(2,1)S(1)}, u32[]{:S(2)}, u32[]{:S(2)}) async-start(bf16[16,4,3072]{2,1,0:T(4,128)(2,1)} %copy.83), calls=%async_computation.3 | async-start | bytes 786432 | tf_op jit(solution)/shard_map/all_to_all | solution.py:74
  87.1 10.1 %all-to-all-done.3 = bf16[16,4,3072]{2,1,0:T(4,128)(2,1)S(1)} async-done(((bf16[16,4,3072]{2,1,0:T(4,128)(2,1)}), bf16[16,4,3072]{2,1,0:T(4,128)(2,1)S(1)}, u32[]{:S(2)}, u32[]{:S(2)}) %all-to-all-start.3) | async-done | bytes 393248 | tf_op jit(solution)/shard_map/all_to_all | solution.py:74
  97.4 1.3 collective-permute-start.5
  98.7 4.4 %collective-permute-done.5 = bf16[4,3072]{1,0:T(4,128)(2,1)S(1)} collective-permute-done((bf16[4,3072]{1,0:T(4,128)(2,1)S(1)}, bf16[4,3072]{1,0:T(4,128)(2,1)S(1)}, u32[]{:S(2)}, u32[]{:S(2)}) %collective-permute-start.5) | collective-permute-done | bytes 24608 | tf_op jit(solution)/shard_map/ppermute | solution.py:10
  103.5 12.7 %all_to_all.63 = bf16[16,4,3072]{2,1,0:T(4,128)(2,1)S(1)} all-to-all(bf16[16,4,3072]{2,1,0:T(4,128)(2,1)S(1)} %broadcast_in_dim.81), channel_id=1, replica_groups={{0,2,4,6,8,10,12,14,16,18,20,22,24,26,28,30},{1,3,5,7,9,11,13,15,17,19,..., dimensions={0} | all-to-all | bytes 786432 | tf_op jit(solution)/shard_map/all_to_all | solution.py:70
  116.3 0.3 collective-permute-start.6
  116.5 1.7 collective-permute-done.6
  118.2 3.8 %fusion.60 = f32[4,32,4,256]{3,1,0,2:T(8,128)S(1)} fusion(bf16[1,4,3072,256]{3,2,1,0:T(8,128)(2,1)} %param.9, bf16[16,4,3072]{2,0,1:T(8,128)(2,1)S(1)} %collective-permute-done.6, bf16[16,4,3072]{2,0,1:T(8,128)(2,1)S(1)} %copy.85), kind=kOutput, calls=%fused_computation.44 | convolution fusion | flops 806879232 | bytes 7602176 | tf_op jit(solution)/shard_map/fmd,edh->efmh/dot_general | solution.py:33
  122.0 6.6 %fusion.42 = f32[32,4,3072]{2,0,1:T(8,128)S(1)} fusion(bf16[1,4,256,3072]{3,2,1,0:T(8,128)(2,1)} %param.11, f32[4,32,4,256]{3,1,0,2:T(8,128)S(1)} %fusion.60, bf16[1,4,3072,256]{3,2,1,0:T(8,128)(2,1)} %param.10, bf16[16,4,3072]{2,0,1:T(8,128)(2,1)S(1)} %collective-permute-done.6, bf16[16,4,3072]{2,0,1:T(8,128)(2,1)S(1)} %copy.85, f32[4,32,4]{1,0,2:T(4,128)S(1)} %copy.86), kind=kOutput, calls=%fused_computation.38 | convolution fusion | flops 1613103104 | bytes 15468544 | tf_op jit(solution)/shard_map/efmh,ehd->fmd/dot_general | solution.py:36
  128.9 2.1 collective-permute-done.7
  131.2 1.0 copy.87
  132.2 3.7 %all-to-all-start.5 = ((bf16[16,4,3072]{2,1,0:T(4,128)(2,1)}), bf16[16,4,3072]{2,1,0:T(4,128)(2,1)S(1)}, u32[]{:S(2)}, u32[]{:S(2)}) async-start(bf16[16,4,3072]{2,1,0:T(4,128)(2,1)} %copy.87), calls=%async_computation.5 | async-start | bytes 786432 | tf_op jit(solution)/shard_map/all_to_all | solution.py:74
  136.0 10.2 %all-to-all-done.5 = bf16[16,4,3072]{2,1,0:T(4,128)(2,1)S(1)} async-done(((bf16[16,4,3072]{2,1,0:T(4,128)(2,1)}), bf16[16,4,3072]{2,1,0:T(4,128)(2,1)S(1)}, u32[]{:S(2)}, u32[]{:S(2)}) %all-to-all-start.5) | async-done | bytes 393248 | tf_op jit(solution)/shard_map/all_to_all | solution.py:74
  146.3 1.3 collective-permute-start.8
  147.6 4.4 %collective-permute-done.8 = bf16[4,3072]{1,0:T(4,128)(2,1)S(1)} collective-permute-done((bf16[4,3072]{1,0:T(4,128)(2,1)S(1)}, bf16[4,3072]{1,0:T(4,128)(2,1)S(1)}, u32[]{:S(2)}, u32[]{:S(2)}) %collective-permute-start.8) | collective-permute-done | bytes 24608 | tf_op jit(solution)/shard_map/ppermute | solution.py:10
  152.4 12.7 %all_to_all.64 = bf16[16,4,3072]{2,1,0:T(4,128)(2,1)S(1)} all-to-all(bf16[16,4,3072]{2,1,0:T(4,128)(2,1)S(1)} %broadcast_in_dim.83), channel_id=1, replica_groups={{0,2,4,6,8,10,12,14,16,18,20,22,24,26,28,30},{1,3,5,7,9,11,13,15,17,19,..., dimensions={0} | all-to-all | bytes 786432 | tf_op jit(solution)/shard_map/all_to_all | solution.py:70
  165.3 1.7 collective-permute-done.9
  167.0 3.8 %fusion.63 = f32[4,32,4,256]{3,1,0,2:T(8,128)S(1)} fusion(bf16[1,4,3072,256]{3,2,1,0:T(8,128)(2,1)} %param.9, bf16[16,4,3072]{2,0,1:T(8,128)(2,1)S(1)} %collective-permute-done.9, bf16[16,4,3072]{2,0,1:T(8,128)(2,1)S(1)} %copy.89), kind=kOutput, calls=%fused_computation.45 | convolution fusion | flops 806879232 | bytes 7602176 | tf_op jit(solution)/shard_map/fmd,edh->efmh/dot_general | solution.py:33
  170.8 6.6 %fusion.45 = f32[32,4,3072]{2,0,1:T(8,128)S(1)} fusion(bf16[1,4,256,3072]{3,2,1,0:T(8,128)(2,1)} %param.11, f32[4,32,4,256]{3,1,0,2:T(8,128)S(1)} %fusion.63, bf16[1,4,3072,256]{3,2,1,0:T(8,128)(2,1)} %param.10, bf16[16,4,3072]{2,0,1:T(8,128)(2,1)S(1)} %collective-permute-done.9, bf16[16,4,3072]{2,0,1:T(8,128)(2,1)S(1)} %copy.89, f32[4,32,4]{1,0,2:T(4,128)S(1)} %copy.90), kind=kOutput, calls=%fused_computation.39 | convolution fusion | flops 1613103104 | bytes 15468544 | tf_op jit(solution)/shard_map/efmh,ehd->fmd/dot_general | solution.py:36
  177.7 2.1 collective-permute-done.10
  180.0 1.0 copy.91
  181.0 3.7 %all-to-all-start.7 = ((bf16[16,4,3072]{2,1,0:T(4,128)(2,1)}), bf16[16,4,3072]{2,1,0:T(4,128)(2,1)S(1)}, u32[]{:S(2)}, u32[]{:S(2)}) async-start(bf16[16,4,3072]{2,1,0:T(4,128)(2,1)} %copy.91), calls=%async_computation.7 | async-start | bytes 786432 | tf_op jit(solution)/shard_map/all_to_all | solution.py:74
  184.8 10.2 %all-to-all-done.7 = bf16[16,4,3072]{2,1,0:T(4,128)(2,1)S(1)} async-done(((bf16[16,4,3072]{2,1,0:T(4,128)(2,1)}), bf16[16,4,3072]{2,1,0:T(4,128)(2,1)S(1)}, u32[]{:S(2)}, u32[]{:S(2)}) %all-to-all-start.7) | async-done | bytes 393248 | tf_op jit(solution)/shard_map/all_to_all | solution.py:74
  195.1 1.3 collective-permute-start.11
  196.4 4.4 %collective-permute-done.11 = bf16[4,3072]{1,0:T(4,128)(2,1)S(1)} collective-permute-done((bf16[4,3072]{1,0:T(4,128)(2,1)S(1)}, bf16[4,3072]{1,0:T(4,128)(2,1)S(1)}, u32[]{:S(2)}, u32[]{:S(2)}) %collective-permute-start.11) | collective-permute-done | bytes 24608 | tf_op jit(solution)/shard_map/ppermute | solution.py:10
  201.2 12.7 %all_to_all.65 = bf16[16,4,3072]{2,1,0:T(4,128)(2,1)S(1)} all-to-all(bf16[16,4,3072]{2,1,0:T(4,128)(2,1)S(1)} %broadcast_in_dim.85), channel_id=1, replica_groups={{0,2,4,6,8,10,12,14,16,18,20,22,24,26,28,30},{1,3,5,7,9,11,13,15,17,19,..., dimensions={0} | all-to-all | bytes 786432 | tf_op jit(solution)/shard_map/all_to_all | solution.py:70
  214.0 0.3 collective-permute-start.12
  214.3 1.7 collective-permute-done.12
  216.0 3.8 %fusion.66 = f32[4,32,4,256]{3,1,0,2:T(8,128)S(1)} fusion(bf16[1,4,3072,256]{3,2,1,0:T(8,128)(2,1)} %param.9, bf16[16,4,3072]{2,0,1:T(8,128)(2,1)S(1)} %collective-permute-done.12, bf16[16,4,3072]{2,0,1:T(8,128)(2,1)S(1)} %copy.93), kind=kOutput, calls=%fused_computation.46 | convolution fusion | flops 806879232 | bytes 7602176 | tf_op jit(solution)/shard_map/fmd,edh->efmh/dot_general | solution.py:33
  219.8 6.6 %fusion.48 = f32[32,4,3072]{2,0,1:T(8,128)S(1)} fusion(bf16[1,4,256,3072]{3,2,1,0:T(8,128)(2,1)} %param.11, f32[4,32,4,256]{3,1,0,2:T(8,128)S(1)} %fusion.66, bf16[1,4,3072,256]{3,2,1,0:T(8,128)(2,1)} %param.10, bf16[16,4,3072]{2,0,1:T(8,128)(2,1)S(1)} %collective-permute-done.12, bf16[16,4,3072]{2,0,1:T(8,128)(2,1)S(1)} %copy.93, f32[4,32,4]{1,0,2:T(4,128)S(1)} %copy.94), kind=kOutput, calls=%fused_computation.40 | convolution fusion | flops 1613103104 | bytes 15468544 | tf_op jit(solution)/shard_map/efmh,ehd->fmd/dot_general | solution.py:36
  226.7 2.2 collective-permute-done.13
  229.0 1.0 copy.95
  230.0 3.7 %all-to-all-start.9 = ((bf16[16,4,3072]{2,1,0:T(4,128)(2,1)}), bf16[16,4,3072]{2,1,0:T(4,128)(2,1)S(1)}, u32[]{:S(2)}, u32[]{:S(2)}) async-start(bf16[16,4,3072]{2,1,0:T(4,128)(2,1)} %copy.95), calls=%async_computation.9 | async-start | bytes 786432 | tf_op jit(solution)/shard_map/all_to_all | solution.py:74
  233.8 10.2 %all-to-all-done.9 = bf16[16,4,3072]{2,1,0:T(4,128)(2,1)S(1)} async-done(((bf16[16,4,3072]{2,1,0:T(4,128)(2,1)}), bf16[16,4,3072]{2,1,0:T(4,128)(2,1)S(1)}, u32[]{:S(2)}, u32[]{:S(2)}) %all-to-all-start.9) | async-done | bytes 393248 | tf_op jit(solution)/shard_map/all_to_all | solution.py:74
  244.1 1.3 collective-permute-start.14
  245.4 4.4 %collective-permute-done.14 = bf16[4,3072]{1,0:T(4,128)(2,1)S(1)} collective-permute-done((bf16[4,3072]{1,0:T(4,128)(2,1)S(1)}, bf16[4,3072]{1,0:T(4,128)(2,1)S(1)}, u32[]{:S(2)}, u32[]{:S(2)}) %collective-permute-start.14) | collective-permute-done | bytes 24608 | tf_op jit(solution)/shard_map/ppermute | solution.py:10
  250.2 12.7 %all_to_all.66 = bf16[16,4,3072]{2,1,0:T(4,128)(2,1)S(1)} all-to-all(bf16[16,4,3072]{2,1,0:T(4,128)(2,1)S(1)} %broadcast_in_dim.88), channel_id=1, replica_groups={{0,2,4,6,8,10,12,14,16,18,20,22,24,26,28,30},{1,3,5,7,9,11,13,15,17,19,..., dimensions={0} | all-to-all | bytes 786432 | tf_op jit(solution)/shard_map/all_to_all | solution.py:70
  263.1 1.7 collective-permute-done.15
  264.8 3.8 %fusion.69 = f32[4,32,4,256]{3,1,0,2:T(8,128)S(1)} fusion(bf16[1,4,3072,256]{3,2,1,0:T(8,128)(2,1)} %param.9, bf16[16,4,3072]{2,0,1:T(8,128)(2,1)S(1)} %collective-permute-done.15, bf16[16,4,3072]{2,0,1:T(8,128)(2,1)S(1)} %copy.97), kind=kOutput, calls=%fused_computation.47 | convolution fusion | flops 806879232 | bytes 7602176 | tf_op jit(solution)/shard_map/fmd,edh->efmh/dot_general | solution.py:33
  268.6 6.6 %fusion.51 = f32[32,4,3072]{2,0,1:T(8,128)S(1)} fusion(bf16[1,4,256,3072]{3,2,1,0:T(8,128)(2,1)} %param.11, f32[4,32,4,256]{3,1,0,2:T(8,128)S(1)} %fusion.69, bf16[1,4,3072,256]{3,2,1,0:T(8,128)(2,1)} %param.10, bf16[16,4,3072]{2,0,1:T(8,128)(2,1)S(1)} %collective-permute-done.15, bf16[16,4,3072]{2,0,1:T(8,128)(2,1)S(1)} %copy.97, f32[4,32,4]{1,0,2:T(4,128)S(1)} %copy.98), kind=kOutput, calls=%fused_computation.41 | convolution fusion | flops 1613103104 | bytes 15468544 | tf_op jit(solution)/shard_map/efmh,ehd->fmd/dot_general | solution.py:36
  275.5 2.1 collective-permute-done.16
  277.7 1.0 copy.99
  278.8 3.7 %all-to-all-start.11 = ((bf16[16,4,3072]{2,1,0:T(4,128)(2,1)}), bf16[16,4,3072]{2,1,0:T(4,128)(2,1)S(1)}, u32[]{:S(2)}, u32[]{:S(2)}) async-start(bf16[16,4,3072]{2,1,0:T(4,128)(2,1)} %copy.99), calls=%async_computation.11 | async-start | bytes 786432 | tf_op jit(solution)/shard_map/all_to_all | solution.py:74
  282.5 0.6 copy.117
  283.2 9.5 %all-to-all-done.11 = bf16[16,4,3072]{2,1,0:T(4,128)(2,1)S(1)} async-done(((bf16[16,4,3072]{2,1,0:T(4,128)(2,1)}), bf16[16,4,3072]{2,1,0:T(4,128)(2,1)S(1)}, u32[]{:S(2)}, u32[]{:S(2)}) %all-to-all-start.11) | async-done | bytes 393248 | tf_op jit(solution)/shard_map/all_to_all | solution.py:74
  292.9 0.6 fusion.162
  (78 shorter events, 7.1 us)
Async XLA Ops:
  19.5 1.8 collective-permute-start
  25.1 23.6 %copy-start = (bf16[3,4,3072]{2,1,0:T(4,128)(2,1)S(1)}, bf16[3,4,3072]{2,1,0:T(4,128)(2,1)}, u32[]{:S(2)}) copy-start(bf16[3,4,3072]{2,1,0:T(4,128)(2,1)} %param.7) | copy-start | bytes 221188
  25.1 29.5 %copy-start.1 = (f32[1,3072]{1,0:T(1,128)S(1)}, f32[1,3072]{1,0:T(1,128)}, u32[]{:S(2)}) copy-start(f32[1,3072]{1,0:T(1,128)} %param.8) | copy-start | bytes 36868
  31.8 2.4 collective-permute-start.1
  48.6 5.7 %collective-permute-start.2 = (bf16[4,3072]{1,0:T(4,128)(2,1)S(1)}, bf16[4,3072]{1,0:T(4,128)(2,1)S(1)}, u32[]{:S(2)}, u32[]{:S(2)}) collective-permute-start(bf16[4,3072]{1,0:T(4,128)(2,1)S(1)} %fusion.135), channel_id=1, source_target_pairs={{0,32},{32,64},{64,96},{1,33},{33,65},{65,97},{2,34},{34,66},{66,9... | collective-permute-start | bytes 73736 | tf_op jit(solution)/shard_map/ppermute | solution.py:10
  67.5 1.8 collective-permute-start.3
  79.8 2.4 collective-permute-start.4
  83.3 13.9 %all-to-all-start.3 = ((bf16[16,4,3072]{2,1,0:T(4,128)(2,1)}), bf16[16,4,3072]{2,1,0:T(4,128)(2,1)S(1)}, u32[]{:S(2)}, u32[]{:S(2)}) async-start(bf16[16,4,3072]{2,1,0:T(4,128)(2,1)} %copy.83), calls=%async_computation.3 | async-start | bytes 786432 | tf_op jit(solution)/shard_map/all_to_all | solution.py:74
  97.4 5.7 %collective-permute-start.5 = (bf16[4,3072]{1,0:T(4,128)(2,1)S(1)}, bf16[4,3072]{1,0:T(4,128)(2,1)S(1)}, u32[]{:S(2)}, u32[]{:S(2)}) collective-permute-start(bf16[4,3072]{1,0:T(4,128)(2,1)S(1)} %get-tuple-element.20), channel_id=1, source_target_pairs={{0,32},{32,64},{64,96},{1,33},{33,65},{65,97},{2,34},{34,66},{66,9... | collective-permute-start | bytes 73736 | tf_op jit(solution)/shard_map/ppermute | solution.py:10
  116.3 2.0 collective-permute-start.6
  128.7 2.4 collective-permute-start.7
  132.2 13.9 %all-to-all-start.5 = ((bf16[16,4,3072]{2,1,0:T(4,128)(2,1)}), bf16[16,4,3072]{2,1,0:T(4,128)(2,1)S(1)}, u32[]{:S(2)}, u32[]{:S(2)}) async-start(bf16[16,4,3072]{2,1,0:T(4,128)(2,1)} %copy.87), calls=%async_computation.5 | async-start | bytes 786432 | tf_op jit(solution)/shard_map/all_to_all | solution.py:74
  146.3 5.7 %collective-permute-start.8 = (bf16[4,3072]{1,0:T(4,128)(2,1)S(1)}, bf16[4,3072]{1,0:T(4,128)(2,1)S(1)}, u32[]{:S(2)}, u32[]{:S(2)}) collective-permute-start(bf16[4,3072]{1,0:T(4,128)(2,1)S(1)} %get-tuple-element.16), channel_id=1, source_target_pairs={{0,32},{32,64},{64,96},{1,33},{33,65},{65,97},{2,34},{34,66},{66,9... | collective-permute-start | bytes 73736 | tf_op jit(solution)/shard_map/ppermute | solution.py:10
  165.2 1.8 collective-permute-start.9
  177.5 2.4 collective-permute-start.10
  181.0 13.9 %all-to-all-start.7 = ((bf16[16,4,3072]{2,1,0:T(4,128)(2,1)}), bf16[16,4,3072]{2,1,0:T(4,128)(2,1)S(1)}, u32[]{:S(2)}, u32[]{:S(2)}) async-start(bf16[16,4,3072]{2,1,0:T(4,128)(2,1)} %copy.91), calls=%async_computation.7 | async-start | bytes 786432 | tf_op jit(solution)/shard_map/all_to_all | solution.py:74
  195.1 5.7 %collective-permute-start.11 = (bf16[4,3072]{1,0:T(4,128)(2,1)S(1)}, bf16[4,3072]{1,0:T(4,128)(2,1)S(1)}, u32[]{:S(2)}, u32[]{:S(2)}) collective-permute-start(bf16[4,3072]{1,0:T(4,128)(2,1)S(1)} %get-tuple-element.12), channel_id=1, source_target_pairs={{0,32},{32,64},{64,96},{1,33},{33,65},{65,97},{2,34},{34,66},{66,9... | collective-permute-start | bytes 73736 | tf_op jit(solution)/shard_map/ppermute | solution.py:10
  214.0 2.0 collective-permute-start.12
  226.5 2.4 collective-permute-start.13
  230.0 13.9 %all-to-all-start.9 = ((bf16[16,4,3072]{2,1,0:T(4,128)(2,1)}), bf16[16,4,3072]{2,1,0:T(4,128)(2,1)S(1)}, u32[]{:S(2)}, u32[]{:S(2)}) async-start(bf16[16,4,3072]{2,1,0:T(4,128)(2,1)} %copy.95), calls=%async_computation.9 | async-start | bytes 786432 | tf_op jit(solution)/shard_map/all_to_all | solution.py:74
  244.1 5.7 %collective-permute-start.14 = (bf16[4,3072]{1,0:T(4,128)(2,1)S(1)}, bf16[4,3072]{1,0:T(4,128)(2,1)S(1)}, u32[]{:S(2)}, u32[]{:S(2)}) collective-permute-start(bf16[4,3072]{1,0:T(4,128)(2,1)S(1)} %get-tuple-element.8), channel_id=1, source_target_pairs={{0,32},{32,64},{64,96},{1,33},{33,65},{65,97},{2,34},{34,66},{66,9... | collective-permute-start | bytes 73736 | tf_op jit(solution)/shard_map/ppermute | solution.py:10
  263.0 1.8 collective-permute-start.15
  275.3 2.4 collective-permute-start.16
  278.8 13.9 %all-to-all-start.11 = ((bf16[16,4,3072]{2,1,0:T(4,128)(2,1)}), bf16[16,4,3072]{2,1,0:T(4,128)(2,1)S(1)}, u32[]{:S(2)}, u32[]{:S(2)}) async-start(bf16[16,4,3072]{2,1,0:T(4,128)(2,1)} %copy.99), calls=%async_computation.11 | async-start | bytes 786432 | tf_op jit(solution)/shard_map/all_to_all | solution.py:74
where the time goes:
time: 295 us; the launch traced here: 294 us
  blocking collectives  94.7 us (32%)
  waiting for transfers between devices  93.6 us (32%)
  matrix products  62.4 us (21%)
  starting transfers between devices  27.5 us (9%)
  local copies, waits for them, and re-layouts  8.59 us (3%)
  other arithmetic  6.2 us (2%)
    all_to_all x6, blocking collectives, on_device(): lax.all_to_all(spread, 'fsdp', 0, 0, tiled=True, axis_index_groups=groups)  80.8 us
    all_to_all x5, waiting for transfers between devices, on_device(): lax.all_to_all(chip_sum.astype(jnp.bfloat16), 'fsdp', 0, 0, tiled=True, a...  50.2 us
    dot_general x6, matrix products, expert_mix(): jnp.einsum('efmh,ehd->fmd', gated, down_w, preferred_element_type=jnp.flo...  39.7 us
    dot_general x6, matrix products, expert_mix(): jnp.einsum('fmd,edh->efmh', rows, gate_w, preferred_element_type=jnp.floa...  22.7 us
    ppermute x5, waiting for transfers between devices, passed_along(): return lax.ppermute(array, axis, pairs)  22.1 us
    ppermute x12, waiting for transfers between devices, sibling(): return lax.ppermute(array, axis, [(i, i ^ 1) for i in range(devices)])  21.3 us
    all_to_all x5, starting transfers between devices, on_device(): lax.all_to_all(chip_sum.astype(jnp.bfloat16), 'fsdp', 0, 0, tiled=True, a...  18.6 us
    all_to_all x1, blocking collectives, on_device(): lax.all_to_all(chip_sum.astype(jnp.bfloat16), 'fsdp', 0, 0, tiled=True, a...  13.9 us
  transfers between devices with their start and end apart: 22, of which 22 were waited for; matrix products, arithmetic and copies ran while one was open for 1% of the time, Pallas kernels for 0%

commit v1 on v0

--- a/solution.py
+++ b/solution.py
@@ -1,7 +1,55 @@
 import jax
 import jax.numpy as jnp
 from jax import lax
+from jax.experimental import pallas as pl
+from jax.experimental.pallas import tpu as pltpu
 from jax.sharding import PartitionSpec as P
+
+MESH = pl.DeviceIdType.MESH
+
+
+def exchange(src, shards, same, collective_id):
+    rows, width = src.shape[-2:]
+
+    def kernel(src_ref, out_ref, send_sem, recv_sem, local_sem):
+        me = lax.axis_index("fsdp")
+        section = lax.axis_index("section")
+        barrier = pltpu.get_barrier_semaphore()
+        for j in range(1, shards):
+            peer = lax.rem(me + j, shards)
+            pl.semaphore_signal(barrier, 1, device_id=(section, peer), device_id_type=MESH)
+        pl.semaphore_wait(barrier, shards - 1)
+        local = pltpu.make_async_copy(src_ref if same else src_ref.at[me], out_ref.at[me], local_sem)
+        local.start()
+        copies = []
+        for j in range(1, shards):
+            peer = lax.rem(me + j, shards)
+            copy = pltpu.make_async_remote_copy(
+                src_ref=src_ref if same else src_ref.at[peer],
+                dst_ref=out_ref.at[me],
+                send_sem=send_sem.at[j],
+                recv_sem=recv_sem.at[j],
+                device_id=(section, peer),
+                device_id_type=MESH,
+            )
+            copy.start()
+            copies.append(copy)
+        local.wait()
+        for copy in copies:
+            copy.wait()
+
+    return pl.pallas_call(
+        kernel,
+        out_shape=jax.ShapeDtypeStruct((shards, rows, width), src.dtype),
+        in_specs=[pl.BlockSpec(memory_space=pl.ANY)],
+        out_specs=pl.BlockSpec(memory_space=pl.ANY),
+        scratch_shapes=[
+            pltpu.SemaphoreType.DMA((shards,)),
+            pltpu.SemaphoreType.DMA((shards,)),
+            pltpu.SemaphoreType.DMA(()),
+        ],
+        compiler_params=pltpu.CompilerParams(collective_id=collective_id, has_side_effects=True),
+    )(src)
 
 
 def passed_along(array, axis, by):
@@ -41,21 +89,11 @@
     shards = lax.axis_size("fsdp")
     chips = shards // 2
     section_index = lax.axis_index("section")
-    core = lax.axis_index("fsdp") % 2
-    groups = [list(range(c, shards, 2)) for c in range(2)]
     micro, local, width = inputs.shape
     gain_row = gain[0]
     gate_w, up_w, down_w = w_gate[0], w_up[0], w_down[0]
     experts = gate_w.shape[0]
     coef = combine_weights(routes[0], shares[0], experts, shards)
-    coef = coef.reshape(micro, experts, chips, 2, local)
-    coef = jnp.concatenate(
-        [
-            lax.dynamic_index_in_dim(coef, core, 3, keepdims=False),
-            lax.dynamic_index_in_dim(coef, 1 - core, 3, keepdims=False),
-        ],
-        axis=2,
-    )
     output = jnp.zeros_like(inputs)
     carried = None
     for tick in range(micro + sections - 1):
@@ -66,15 +104,12 @@
         coef_now = lax.dynamic_index_in_dim(coef, clipped, 0, keepdims=False)
         current = entry if carried is None else jnp.where(section_index == 0, entry, carried)
         normed = rms_norm(current, gain_row)
-        spread = jnp.broadcast_to(normed[None], (chips,) + normed.shape)
-        near = lax.all_to_all(spread, "fsdp", 0, 0, tiled=True, axis_index_groups=groups)
-        rows = jnp.concatenate([near, sibling(near, "fsdp")], axis=0)
+        lanes = local * width // 128
+        rows = exchange(normed.reshape(lanes, 128), shards, True, 0).reshape(shards, local, width)
         partial_value = expert_mix(rows, coef_now, gate_w, up_w, down_w)
-        chip_sum = partial_value[:chips] + sibling(partial_value[chips:], "fsdp")
-        pieces = lax.all_to_all(
-            chip_sum.astype(jnp.bfloat16), "fsdp", 0, 0, tiled=True, axis_index_groups=groups
-        )
-        mixed = jnp.sum(pieces.astype(jnp.float32), axis=0)
+        sent = partial_value.astype(jnp.bfloat16).reshape(shards, lanes, 128)
+        pieces = exchange(sent, shards, False, 1)
+        mixed = jnp.sum(pieces.astype(jnp.float32), axis=0).reshape(local, width)
         result = (current.astype(jnp.float32) + mixed).astype(jnp.bfloat16)
         if tick + 1 < micro + sections - 1:
             carried = passed_along(result, "section", 1)

time: 295 us -> 351 us (1.19)
  the two profiles are of different devices: /device:TPU:24 before, /device:TPU:19 now
where the time goes in v1:
time: 351 us; the launch traced here: 345 us
  Pallas kernels  220 us (63%)
  matrix products  63.3 us (18%)
  local copies, waits for them, and re-layouts  26.1 us (7%)
  starting transfers between devices  16.1 us (5%)
  other arithmetic  13.3 us (4%)
  waiting for transfers between devices  5.43 us (2%)
    pallas_call x12, Pallas kernels, exchange(): pl.pallas_call(kernel, out_shape=jax.ShapeDtypeStruct((shards, rows, widt...  220 us
    dot_general x6, matrix products, expert_mix(): jnp.einsum('efmh,ehd->fmd', gated, down_w, preferred_element_type=jnp.flo...  40.2 us
    dot_general x6, matrix products, expert_mix(): jnp.einsum('fmd,edh->efmh', rows, gate_w, preferred_element_type=jnp.floa...  23.1 us
    ppermute x5, starting transfers between devices, passed_along(): return lax.ppermute(array, axis, pairs)  16.1 us
    reshape x6, local copies, waits for them, and re-layouts, on_device(): exchange(normed.reshape(lanes, 128), shards, True, 0)  10.5 us
    reduce_sum x6, other arithmetic, on_device(): mixed = jnp.sum(pieces.astype(jnp.float32), axis=0).reshape(local, width)  7.54 us
    reshape x6, local copies, waits for them, and re-layouts, on_device(): sent = partial_value.astype(jnp.bfloat16).reshape(shards, lanes, 128)  7.03 us
  transfers between devices with their start and end apart: 5, of which 5 were waited for; matrix products, arithmetic and copies ran while one was open for 0% of the time, Pallas kernels for 0%

profile of v1, /device:TPU:19, one launch (start us, length us, event | category | flops | bytes accessed | tf_op | source)
XLA Modules:
  0.0 344.6 jit_solution(17454723074293621436)
XLA Ops:
  0.0 0.9 fusion.255
  0.9 0.7 dynamic-slice_convert_fusion
  1.8 0.7 select_reduce_fusion
  2.9 1.4 fusion.254.src_ref
  4.3 19.1 %shard_map.73 = bf16[32,96,128]{2,1,0:T(8,128)(2,1)} custom-call(bf16[96,128]{1,0:T(8,128)(2,1)} %fusion.254.src_ref), custom_call_target="tpu_custom_call" | custom-call | tf_op jit(solution)/shard_map/pallas_call | solution.py:41
  23.4 1.7 reshape.149
  25.2 3.9 %fusion.72 = f32[4,32,4,256]{3,1,0,2:T(8,128)S(1)} fusion(bf16[1,4,3072,256]{3,2,1,0:T(8,128)(2,1)} %param.9, bf16[32,4,3072,1]{2,1,0,3:T(4,128)(2,1)S(1)} %bitcast.338), kind=kOutput, calls=%fused_computation.54 | convolution fusion | flops 805306368 | bytes 7602176 | tf_op jit(solution)/shard_map/fmd,edh->efmh/dot_general | solution.py:81
  29.1 6.7 %fusion.69 = bf16[32,4,3072]{2,0,1:T(8,128)(2,1)S(1)} fusion(bf16[1,4,256,3072]{3,2,1,0:T(8,128)(2,1)} %param.11, bf16[1,4,3072,256]{3,2,1,0:T(8,128)(2,1)} %param.10, bf16[32,4,3072,1]{2,1,0,3:T(4,128)(2,1)S(1)} %bitcast.339, f32[4,32,4,256]{3,1,0,2:T(8,128)S(1)} %fusion.72, f32[4,32,4]{1,0,2:T(4,128)S(1)} %copy.44), kind=kOutput, calls=%fused_computation.47 | convolution fusion | flops 1611923456 | bytes 14682112 | tf_op jit(solution)/shard_map/efmh,ehd->fmd/dot_general | solution.py:84
  36.4 1.2 reshape.151.src_ref
  37.6 18.0 %shard_map.74 = bf16[32,96,128]{2,1,0:T(8,128)(2,1)} custom-call(bf16[32,96,128]{2,1,0:T(8,128)(2,1)} %reshape.151.src_ref), custom_call_target="tpu_custom_call" | custom-call | tf_op jit(solution)/shard_map/pallas_call | solution.py:41
  55.6 1.3 convert_reduce_fusion.5
  56.9 3.2 collective-permute-start
  60.3 1.2 collective-permute-done
  61.7 0.6 reshape.154.src_ref
  62.4 18.5 %shard_map.75 = bf16[32,96,128]{2,1,0:T(8,128)(2,1)} custom-call(bf16[96,128]{1,0:T(8,128)(2,1)} %reshape.154.src_ref), custom_call_target="tpu_custom_call" | custom-call | tf_op jit(solution)/shard_map/pallas_call | solution.py:41
  80.9 1.7 reshape.155
  82.6 3.9 %fusion.75 = f32[4,32,4,256]{3,1,0,2:T(8,128)S(1)} fusion(bf16[1,4,3072,256]{3,2,1,0:T(8,128)(2,1)} %param.9, bf16[32,4,3072,1]{2,1,0,3:T(4,128)(2,1)S(1)} %bitcast.340), kind=kOutput, calls=%fused_computation.55 | convolution fusion | flops 805306368 | bytes 7602176 | tf_op jit(solution)/shard_map/fmd,edh->efmh/dot_general | solution.py:81
  86.5 6.7 %fusion.66 = bf16[32,4,3072]{2,0,1:T(8,128)(2,1)S(1)} fusion(bf16[1,4,256,3072]{3,2,1,0:T(8,128)(2,1)} %param.11, bf16[1,4,3072,256]{3,2,1,0:T(8,128)(2,1)} %param.10, bf16[32,4,3072,1]{2,1,0,3:T(4,128)(2,1)S(1)} %bitcast.341, f32[4,32,4,256]{3,1,0,2:T(8,128)S(1)} %fusion.75, f32[4,32,4]{1,0,2:T(4,128)S(1)} %copy.48), kind=kOutput, calls=%fused_computation.46 | convolution fusion | flops 1611923456 | bytes 14682112 | tf_op jit(solution)/shard_map/efmh,ehd->fmd/dot_general | solution.py:84
  93.8 1.2 reshape.156.src_ref
  95.0 18.0 %shard_map.76 = bf16[32,96,128]{2,1,0:T(8,128)(2,1)} custom-call(bf16[32,96,128]{2,1,0:T(8,128)(2,1)} %reshape.156.src_ref), custom_call_target="tpu_custom_call" | custom-call | tf_op jit(solution)/shard_map/pallas_call | solution.py:41
  113.0 1.3 convert_reduce_fusion.4
  114.3 3.2 collective-permute-start.1
  117.7 1.2 collective-permute-done.1
  119.1 0.6 reshape.158.src_ref
  119.7 18.5 %shard_map.77 = bf16[32,96,128]{2,1,0:T(8,128)(2,1)} custom-call(bf16[96,128]{1,0:T(8,128)(2,1)} %reshape.158.src_ref), custom_call_target="tpu_custom_call" | custom-call | tf_op jit(solution)/shard_map/pallas_call | solution.py:41
  138.3 1.7 reshape.159
  140.0 3.9 %fusion.78 = f32[4,32,4,256]{3,1,0,2:T(8,128)S(1)} fusion(bf16[1,4,3072,256]{3,2,1,0:T(8,128)(2,1)} %param.9, bf16[32,4,3072,1]{2,1,0,3:T(4,128)(2,1)S(1)} %bitcast.342), kind=kOutput, calls=%fused_computation.56 | convolution fusion | flops 805306368 | bytes 7602176 | tf_op jit(solution)/shard_map/fmd,edh->efmh/dot_general | solution.py:81
  143.9 6.7 %fusion.63 = bf16[32,4,3072]{2,0,1:T(8,128)(2,1)S(1)} fusion(bf16[1,4,256,3072]{3,2,1,0:T(8,128)(2,1)} %param.11, bf16[1,4,3072,256]{3,2,1,0:T(8,128)(2,1)} %param.10, bf16[32,4,3072,1]{2,1,0,3:T(4,128)(2,1)S(1)} %bitcast.343, f32[4,32,4,256]{3,1,0,2:T(8,128)S(1)} %fusion.78, f32[4,32,4]{1,0,2:T(4,128)S(1)} %copy.52), kind=kOutput, calls=%fused_computation.45 | convolution fusion | flops 1611923456 | bytes 14682112 | tf_op jit(solution)/shard_map/efmh,ehd->fmd/dot_general | solution.py:84
  151.2 1.2 reshape.160.src_ref
  152.4 18.0 %shard_map.78 = bf16[32,96,128]{2,1,0:T(8,128)(2,1)} custom-call(bf16[32,96,128]{2,1,0:T(8,128)(2,1)} %reshape.160.src_ref), custom_call_target="tpu_custom_call" | custom-call | tf_op jit(solution)/shard_map/pallas_call | solution.py:41
  170.4 1.3 convert_reduce_fusion.3
  171.7 3.5 %collective-permute-start.2 = (bf16[4,3072]{1,0:T(4,128)(2,1)S(1)}, bf16[4,3072]{1,0:T(4,128)(2,1)S(1)}, u32[]{:S(2)}, u32[]{:S(2)}) collective-permute-start(bf16[4,3072]{1,0:T(4,128)(2,1)S(1)} %get-tuple-element.16), channel_id=1, source_target_pairs={{0,32},{32,64},{64,96},{1,33},{33,65},{65,97},{2,34},{34,66},{66,9... | collective-permute-start | bytes 73736 | tf_op jit(solution)/shard_map/ppermute | solution.py:58
  175.3 1.0 collective-permute-done.2
  176.5 0.6 reshape.162.src_ref
  177.1 18.5 %shard_map.79 = bf16[32,96,128]{2,1,0:T(8,128)(2,1)} custom-call(bf16[96,128]{1,0:T(8,128)(2,1)} %reshape.162.src_ref), custom_call_target="tpu_custom_call" | custom-call | tf_op jit(solution)/shard_map/pallas_call | solution.py:41
  195.6 1.7 reshape.163
  197.4 3.9 %fusion.81 = f32[4,32,4,256]{3,1,0,2:T(8,128)S(1)} fusion(bf16[1,4,3072,256]{3,2,1,0:T(8,128)(2,1)} %param.9, bf16[32,4,3072,1]{2,1,0,3:T(4,128)(2,1)S(1)} %bitcast.344), kind=kOutput, calls=%fused_computation.57 | convolution fusion | flops 805306368 | bytes 7602176 | tf_op jit(solution)/shard_map/fmd,edh->efmh/dot_general | solution.py:81
  201.3 6.7 %fusion.60 = bf16[32,4,3072]{2,0,1:T(8,128)(2,1)S(1)} fusion(bf16[1,4,256,3072]{3,2,1,0:T(8,128)(2,1)} %param.11, bf16[1,4,3072,256]{3,2,1,0:T(8,128)(2,1)} %param.10, bf16[32,4,3072,1]{2,1,0,3:T(4,128)(2,1)S(1)} %bitcast.345, f32[4,32,4,256]{3,1,0,2:T(8,128)S(1)} %fusion.81, f32[4,32,4]{1,0,2:T(4,128)S(1)} %copy.56), kind=kOutput, calls=%fused_computation.44 | convolution fusion | flops 1611923456 | bytes 14682112 | tf_op jit(solution)/shard_map/efmh,ehd->fmd/dot_general | solution.py:84
  208.0 0.6 copy.57
  208.6 1.2 reshape.164.src_ref
  209.7 18.0 %shard_map.80 = bf16[32,96,128]{2,1,0:T(8,128)(2,1)} custom-call(bf16[32,96,128]{2,1,0:T(8,128)(2,1)} %reshape.164.src_ref), custom_call_target="tpu_custom_call" | custom-call | tf_op jit(solution)/shard_map/pallas_call | solution.py:41
  227.7 1.3 convert_reduce_fusion.2
  229.0 3.1 collective-permute-start.3
  232.2 1.4 collective-permute-done.3
  233.9 0.6 reshape.166.src_ref
  234.5 18.5 %shard_map.81 = bf16[32,96,128]{2,1,0:T(8,128)(2,1)} custom-call(bf16[96,128]{1,0:T(8,128)(2,1)} %reshape.166.src_ref), custom_call_target="tpu_custom_call" | custom-call | tf_op jit(solution)/shard_map/pallas_call | solution.py:41
  253.0 1.7 reshape.167
  254.8 3.9 %fusion.84 = f32[4,32,4,256]{3,1,0,2:T(8,128)S(1)} fusion(bf16[1,4,3072,256]{3,2,1,0:T(8,128)(2,1)} %param.9, bf16[32,4,3072,1]{2,1,0,3:T(4,128)(2,1)S(1)} %bitcast.346), kind=kOutput, calls=%fused_computation.58 | convolution fusion | flops 805306368 | bytes 7602176 | tf_op jit(solution)/shard_map/fmd,edh->efmh/dot_general | solution.py:81
  258.6 6.7 %fusion.57 = bf16[32,4,3072]{2,0,1:T(8,128)(2,1)S(1)} fusion(bf16[1,4,256,3072]{3,2,1,0:T(8,128)(2,1)} %param.11, bf16[1,4,3072,256]{3,2,1,0:T(8,128)(2,1)} %param.10, bf16[32,4,3072,1]{2,1,0,3:T(4,128)(2,1)S(1)} %bitcast.347, f32[4,32,4,256]{3,1,0,2:T(8,128)S(1)} %fusion.84, f32[4,32,4]{1,0,2:T(4,128)S(1)} %copy.60), kind=kOutput, calls=%fused_computation.43 | convolution fusion | flops 1611923456 | bytes 14682112 | tf_op jit(solution)/shard_map/efmh,ehd->fmd/dot_general | solution.py:84
  265.9 1.2 reshape.168.src_ref
  267.1 18.0 %shard_map.82 = bf16[32,96,128]{2,1,0:T(8,128)(2,1)} custom-call(bf16[32,96,128]{2,1,0:T(8,128)(2,1)} %reshape.168.src_ref), custom_call_target="tpu_custom_call" | custom-call | tf_op jit(solution)/shard_map/pallas_call | solution.py:41
  285.1 1.3 convert_reduce_fusion.1
  286.4 3.1 collective-permute-start.4
  289.6 0.6 copy.143
  290.3 0.7 collective-permute-done.4
  291.2 0.6 reshape.170.src_ref
  291.8 18.5 %shard_map.83 = bf16[32,96,128]{2,1,0:T(8,128)(2,1)} custom-call(bf16[96,128]{1,0:T(8,128)(2,1)} %reshape.170.src_ref), custom_call_target="tpu_custom_call" | custom-call | tf_op jit(solution)/shard_map/pallas_call | solution.py:41
  310.4 1.7 reshape.171
  312.1 3.9 %fusion.87 = f32[4,32,4,256]{3,1,0,2:T(8,128)S(1)} fusion(bf16[1,4,3072,256]{3,2,1,0:T(8,128)(2,1)} %param.9, bf16[32,4,3072,1]{2,1,0,3:T(4,128)(2,1)S(1)} %bitcast.348), kind=kOutput, calls=%fused_computation.59 | convolution fusion | flops 805306368 | bytes 7602176 | tf_op jit(solution)/shard_map/fmd,edh->efmh/dot_general | solution.py:81
  316.0 6.7 %fusion.54 = bf16[32,4,3072]{2,0,1:T(8,128)(2,1)S(1)} fusion(bf16[1,4,256,3072]{3,2,1,0:T(8,128)(2,1)} %param.11, bf16[1,4,3072,256]{3,2,1,0:T(8,128)(2,1)} %param.10, bf16[32,4,3072,1]{2,1,0,3:T(4,128)(2,1)S(1)} %bitcast.349, f32[4,32,4,256]{3,1,0,2:T(8,128)S(1)} %fusion.87, f32[4,32,4]{1,0,2:T(4,128)S(1)} %copy.64), kind=kOutput, calls=%fused_computation.42 | convolution fusion | flops 1611923456 | bytes 14682112 | tf_op jit(solution)/shard_map/efmh,ehd->fmd/dot_general | solution.py:84
  323.3 1.2 reshape.172.src_ref
  324.5 18.0 %shard_map.84 = bf16[32,96,128]{2,1,0:T(8,128)(2,1)} custom-call(bf16[32,96,128]{2,1,0:T(8,128)(2,1)} %reshape.172.src_ref), custom_call_target="tpu_custom_call" | custom-call | tf_op jit(solution)/shard_map/pallas_call | solution.py:41
  342.4 1.3 convert_reduce_fusion
  343.7 0.6 fusion.262
  (50 shorter events, 5.6 us)
Async XLA Ops:
  29.0 27.9 %copy-start = (bf16[3,4,3072]{2,1,0:T(4,128)(2,1)S(1)}, bf16[3,4,3072]{2,1,0:T(4,128)(2,1)}, u32[]{:S(2)}) copy-start(bf16[3,4,3072]{2,1,0:T(4,128)(2,1)} %param.7) | copy-start | bytes 221188
  29.0 32.6 %copy-start.1 = (f32[1,3072]{1,0:T(1,128)S(1)}, f32[1,3072]{1,0:T(1,128)}, u32[]{:S(2)}) copy-start(f32[1,3072]{1,0:T(1,128)} %param.8) | copy-start | bytes 36868
  56.9 4.6 %collective-permute-start = (bf16[4,3072]{1,0:T(4,128)(2,1)S(1)}, bf16[4,3072]{1,0:T(4,128)(2,1)S(1)}, u32[]{:S(2)}, u32[]{:S(2)}) collective-permute-start(bf16[4,3072]{1,0:T(4,128)(2,1)S(1)} %fusion.256), channel_id=1, source_target_pairs={{0,32},{32,64},{64,96},{1,33},{33,65},{65,97},{2,34},{34,66},{66,9... | collective-permute-start | bytes 73736 | tf_op jit(solution)/shard_map/ppermute | solution.py:58
  114.3 4.6 %collective-permute-start.1 = (bf16[4,3072]{1,0:T(4,128)(2,1)S(1)}, bf16[4,3072]{1,0:T(4,128)(2,1)S(1)}, u32[]{:S(2)}, u32[]{:S(2)}) collective-permute-start(bf16[4,3072]{1,0:T(4,128)(2,1)S(1)} %get-tuple-element.20), channel_id=1, source_target_pairs={{0,32},{32,64},{64,96},{1,33},{33,65},{65,97},{2,34},{34,66},{66,9... | collective-permute-start | bytes 73736 | tf_op jit(solution)/shard_map/ppermute | solution.py:58
  171.7 4.6 %collective-permute-start.2 = (bf16[4,3072]{1,0:T(4,128)(2,1)S(1)}, bf16[4,3072]{1,0:T(4,128)(2,1)S(1)}, u32[]{:S(2)}, u32[]{:S(2)}) collective-permute-start(bf16[4,3072]{1,0:T(4,128)(2,1)S(1)} %get-tuple-element.16), channel_id=1, source_target_pairs={{0,32},{32,64},{64,96},{1,33},{33,65},{65,97},{2,34},{34,66},{66,9... | collective-permute-start | bytes 73736 | tf_op jit(solution)/shard_map/ppermute | solution.py:58
  229.0 4.6 %collective-permute-start.3 = (bf16[4,3072]{1,0:T(4,128)(2,1)S(1)}, bf16[4,3072]{1,0:T(4,128)(2,1)S(1)}, u32[]{:S(2)}, u32[]{:S(2)}) collective-permute-start(bf16[4,3072]{1,0:T(4,128)(2,1)S(1)} %get-tuple-element.12), channel_id=1, source_target_pairs={{0,32},{32,64},{64,96},{1,33},{33,65},{65,97},{2,34},{34,66},{66,9... | collective-permute-start | bytes 73736 | tf_op jit(solution)/shard_map/ppermute | solution.py:58
  286.4 4.6 %collective-permute-start.4 = (bf16[4,3072]{1,0:T(4,128)(2,1)S(1)}, bf16[4,3072]{1,0:T(4,128)(2,1)S(1)}, u32[]{:S(2)}, u32[]{:S(2)}) collective-permute-start(bf16[4,3072]{1,0:T(4,128)(2,1)S(1)} %get-tuple-element.8), channel_id=1, source_target_pairs={{0,32},{32,64},{64,96},{1,33},{33,65},{65,97},{2,34},{34,66},{66,9... | collective-permute-start | bytes 73736 | tf_op jit(solution)/shard_map/ppermute | solution.py:58

commit v2 on v1

--- a/solution.py
+++ b/solution.py
@@ -1,35 +1,36 @@
 import jax
 import jax.numpy as jnp
 from jax import lax
+from jax.sharding import PartitionSpec as P
 from jax.experimental import pallas as pl
 from jax.experimental.pallas import tpu as pltpu
-from jax.sharding import PartitionSpec as P
 
 MESH = pl.DeviceIdType.MESH
 
 
-def exchange(src, shards, same, collective_id):
+def exchange(src, chips, same, collective_id):
     rows, width = src.shape[-2:]
 
     def kernel(src_ref, out_ref, send_sem, recv_sem, local_sem):
         me = lax.axis_index("fsdp")
         section = lax.axis_index("section")
+        chip, core = me // 2, me % 2
         barrier = pltpu.get_barrier_semaphore()
-        for j in range(1, shards):
-            peer = lax.rem(me + j, shards)
-            pl.semaphore_signal(barrier, 1, device_id=(section, peer), device_id_type=MESH)
-        pl.semaphore_wait(barrier, shards - 1)
-        local = pltpu.make_async_copy(src_ref if same else src_ref.at[me], out_ref.at[me], local_sem)
+        for j in range(1, chips):
+            peer = lax.rem(chip + j, chips)
+            pl.semaphore_signal(barrier, 1, device_id=(section, peer * 2 + core), device_id_type=MESH)
+        pl.semaphore_wait(barrier, chips - 1)
+        local = pltpu.make_async_copy(src_ref if same else src_ref.at[chip], out_ref.at[chip], local_sem)
         local.start()
         copies = []
-        for j in range(1, shards):
-            peer = lax.rem(me + j, shards)
+        for j in range(1, chips):
+            peer = lax.rem(chip + j, chips)
             copy = pltpu.make_async_remote_copy(
                 src_ref=src_ref if same else src_ref.at[peer],
-                dst_ref=out_ref.at[me],
+                dst_ref=out_ref.at[chip],
                 send_sem=send_sem.at[j],
                 recv_sem=recv_sem.at[j],
-                device_id=(section, peer),
+                device_id=(section, peer * 2 + core),
                 device_id_type=MESH,
             )
             copy.start()
@@ -40,12 +41,12 @@
 
     return pl.pallas_call(
         kernel,
-        out_shape=jax.ShapeDtypeStruct((shards, rows, width), src.dtype),
+        out_shape=jax.ShapeDtypeStruct((chips, rows, width), src.dtype),
         in_specs=[pl.BlockSpec(memory_space=pl.ANY)],
         out_specs=pl.BlockSpec(memory_space=pl.ANY),
         scratch_shapes=[
-            pltpu.SemaphoreType.DMA((shards,)),
-            pltpu.SemaphoreType.DMA((shards,)),
+            pltpu.SemaphoreType.DMA((chips,)),
+            pltpu.SemaphoreType.DMA((chips,)),
             pltpu.SemaphoreType.DMA(()),
         ],
         compiler_params=pltpu.CompilerParams(collective_id=collective_id, has_side_effects=True),
@@ -89,11 +90,20 @@
     shards = lax.axis_size("fsdp")
     chips = shards // 2
     section_index = lax.axis_index("section")
+    core = lax.axis_index("fsdp") % 2
     micro, local, width = inputs.shape
     gain_row = gain[0]
     gate_w, up_w, down_w = w_gate[0], w_up[0], w_down[0]
     experts = gate_w.shape[0]
     coef = combine_weights(routes[0], shares[0], experts, shards)
+    coef = coef.reshape(micro, experts, chips, 2, local)
+    coef = jnp.concatenate(
+        [
+            lax.dynamic_index_in_dim(coef, core, 3, keepdims=False),
+            lax.dynamic_index_in_dim(coef, 1 - core, 3, keepdims=False),
+        ],
+        axis=2,
+    )
     output = jnp.zeros_like(inputs)
     carried = None
     for tick in range(micro + sections - 1):
@@ -105,10 +115,12 @@
         current = entry if carried is None else jnp.where(section_index == 0, entry, carried)
         normed = rms_norm(current, gain_row)
         lanes = local * width // 128
-        rows = exchange(normed.reshape(lanes, 128), shards, True, 0).reshape(shards, local, width)
+        near = exchange(normed.reshape(lanes, 128), chips, True, 0)
+        rows = jnp.concatenate([near, sibling(near, "fsdp")], axis=0).reshape(shards, local, width)
         partial_value = expert_mix(rows, coef_now, gate_w, up_w, down_w)
-        sent = partial_value.astype(jnp.bfloat16).reshape(shards, lanes, 128)
-        pieces = exchange(sent, shards, False, 1)
+        chip_sum = partial_value[:chips] + sibling(partial_value[chips:], "fsdp")
+        sent = chip_sum.astype(jnp.bfloat16).reshape(chips, lanes, 128)
+        pieces = exchange(sent, chips, False, 1)
         mixed = jnp.sum(pieces.astype(jnp.float32), axis=0).reshape(local, width)
         result = (current.astype(jnp.float32) + mixed).astype(jnp.bfloat16)
         if tick + 1 < micro + sections - 1:

time: 351 us -> 285 us (0.81)
  the two profiles are of different devices: /device:TPU:19 before, /device:TPU:24 now
where the time goes in v2:
time: 285 us; the launch traced here: 284 us
  Pallas kernels  135 us (47%)
  matrix products  63.2 us (22%)
  waiting for transfers between devices  43.9 us (15%)
  other arithmetic  19.2 us (7%)
  local copies, waits for them, and re-layouts  13.4 us (5%)
  starting transfers between devices  8.69 us (3%)
    pallas_call x12, Pallas kernels, exchange(): pl.pallas_call(kernel, out_shape=jax.ShapeDtypeStruct((chips, rows, width...  135 us
    dot_general x6, matrix products, expert_mix(): jnp.einsum('efmh,ehd->fmd', gated, down_w, preferred_element_type=jnp.flo...  40.1 us
    dot_general x6, matrix products, expert_mix(): jnp.einsum('fmd,edh->efmh', rows, gate_w, preferred_element_type=jnp.floa...  23.1 us
    ppermute x12, waiting for transfers between devices, sibling(): return lax.ppermute(array, axis, [(i, i ^ 1) for i in range(devices)])  22 us
    ppermute x5, waiting for transfers between devices, passed_along(): return lax.ppermute(array, axis, pairs)  21.9 us
    ppermute x5, starting transfers between devices, passed_along(): return lax.ppermute(array, axis, pairs)  6.64 us
    concatenate x6, other arithmetic, on_device(): jnp.concatenate([near, sibling(near, 'fsdp')], axis=0)  6.39 us
    reduce_sum x6, other arithmetic, on_device(): mixed = jnp.sum(pieces.astype(jnp.float32), axis=0).reshape(local, width)  6.36 us
  transfers between devices with their start and end apart: 17, of which 17 were waited for; matrix products, arithmetic and copies ran while one was open for 1% of the time, Pallas kernels for 0%

profile of v2, /device:TPU:24, one launch (start us, length us, event | category | flops | bytes accessed | tf_op | source)
XLA Modules:
  0.0 283.7 jit_solution(4945464350390419428)
XLA Ops:
  1.8 1.4 fusion.242.src_ref
  3.2 13.3 %shard_map.73 = bf16[16,96,128]{2,1,0:T(8,128)(2,1)} custom-call(bf16[96,128]{1,0:T(8,128)(2,1)} %fusion.242.src_ref), custom_call_target="tpu_custom_call" | custom-call | tf_op jit(solution)/shard_map/pallas_call | solution.py:42
  18.6 1.1 pad_maximum_fusion
  19.8 3.9 %fusion.54 = f32[4,32,4,256]{3,1,0,2:T(8,128)S(1)} fusion(bf16[1,4,3072,256]{3,2,1,0:T(8,128)(2,1)} %param.9, bf16[32,4,3072,1]{2,1,0,3:T(4,128)(2,1)S(1)} %bitcast.306), kind=kOutput, calls=%fused_computation.42 | convolution fusion | flops 805306368 | bytes 7602176 | tf_op jit(solution)/shard_map/fmd,edh->efmh/dot_general | solution.py:82
  23.7 6.7 %fusion.36 = f32[32,4,3072]{2,0,1:T(8,128)S(1)} fusion(bf16[1,4,256,3072]{3,2,1,0:T(8,128)(2,1)} %param.11, bf16[1,4,3072,256]{3,2,1,0:T(8,128)(2,1)} %param.10, bf16[32,4,3072,1]{2,1,0,3:T(4,128)(2,1)S(1)} %bitcast.307, f32[4,32,4,256]{3,1,0,2:T(8,128)S(1)} %fusion.54, f32[4,32,4]{1,0,2:T(4,128)S(1)} %copy.120), kind=kOutput, calls=%fused_computation.36 | convolution fusion | flops 1611530240 | bytes 15468544 | tf_op jit(solution)/shard_map/efmh,ehd->fmd/dot_general | solution.py:85
  30.7 2.1 collective-permute-done.1
  33.2 0.9 reshape.155.src_ref
  34.1 11.7 %shard_map.74 = bf16[16,96,128]{2,1,0:T(8,128)(2,1)} custom-call(bf16[16,96,128]{2,1,0:T(8,128)(2,1)} %reshape.155.src_ref), custom_call_target="tpu_custom_call" | custom-call | tf_op jit(solution)/shard_map/pallas_call | solution.py:42
  45.8 1.1 convert_reduce_fusion.5
  46.9 1.3 collective-permute-start.2
  48.2 4.4 %collective-permute-done.2 = bf16[4,3072]{1,0:T(4,128)(2,1)S(1)} collective-permute-done((bf16[4,3072]{1,0:T(4,128)(2,1)S(1)}, bf16[4,3072]{1,0:T(4,128)(2,1)S(1)}, u32[]{:S(2)}, u32[]{:S(2)}) %collective-permute-start.2) | collective-permute-done | bytes 24608 | tf_op jit(solution)/shard_map/ppermute | solution.py:59
  53.5 10.6 %shard_map.75 = bf16[16,96,128]{2,1,0:T(8,128)(2,1)} custom-call(bf16[96,128]{1,0:T(8,128)(2,1)} %reshape.158.src_ref), custom_call_target="tpu_custom_call" | custom-call | tf_op jit(solution)/shard_map/pallas_call | solution.py:42
  64.2 1.9 collective-permute-done.3
  66.1 1.1 pad_maximum_fusion.1
  67.4 3.9 %fusion.57 = f32[4,32,4,256]{3,1,0,2:T(8,128)S(1)} fusion(bf16[1,4,3072,256]{3,2,1,0:T(8,128)(2,1)} %param.9, bf16[32,4,3072,1]{2,1,0,3:T(4,128)(2,1)S(1)} %bitcast.308), kind=kOutput, calls=%fused_computation.43 | convolution fusion | flops 805306368 | bytes 7602176 | tf_op jit(solution)/shard_map/fmd,edh->efmh/dot_general | solution.py:82
  71.2 6.7 %fusion.39 = f32[32,4,3072]{2,0,1:T(8,128)S(1)} fusion(bf16[1,4,256,3072]{3,2,1,0:T(8,128)(2,1)} %param.11, bf16[1,4,3072,256]{3,2,1,0:T(8,128)(2,1)} %param.10, bf16[32,4,3072,1]{2,1,0,3:T(4,128)(2,1)S(1)} %bitcast.309, f32[4,32,4,256]{3,1,0,2:T(8,128)S(1)} %fusion.57, f32[4,32,4]{1,0,2:T(4,128)S(1)} %copy.124), kind=kOutput, calls=%fused_computation.37 | convolution fusion | flops 1611530240 | bytes 15468544 | tf_op jit(solution)/shard_map/efmh,ehd->fmd/dot_general | solution.py:85
  78.3 2.1 collective-permute-done.4
  80.7 0.9 reshape.160.src_ref
  81.6 11.5 %shard_map.76 = bf16[16,96,128]{2,1,0:T(8,128)(2,1)} custom-call(bf16[16,96,128]{2,1,0:T(8,128)(2,1)} %reshape.160.src_ref), custom_call_target="tpu_custom_call" | custom-call | tf_op jit(solution)/shard_map/pallas_call | solution.py:42
  93.2 1.1 convert_reduce_fusion.4
  94.3 1.5 collective-permute-start.5
  95.8 4.2 %collective-permute-done.5 = bf16[4,3072]{1,0:T(4,128)(2,1)S(1)} collective-permute-done((bf16[4,3072]{1,0:T(4,128)(2,1)S(1)}, bf16[4,3072]{1,0:T(4,128)(2,1)S(1)}, u32[]{:S(2)}, u32[]{:S(2)}) %collective-permute-start.5) | collective-permute-done | bytes 24608 | tf_op jit(solution)/shard_map/ppermute | solution.py:59
  100.9 10.3 %shard_map.77 = bf16[16,96,128]{2,1,0:T(8,128)(2,1)} custom-call(bf16[96,128]{1,0:T(8,128)(2,1)} %reshape.162.src_ref), custom_call_target="tpu_custom_call" | custom-call | tf_op jit(solution)/shard_map/pallas_call | solution.py:42
  111.3 1.9 collective-permute-done.6
  113.2 1.1 pad_maximum_fusion.2
  114.5 3.9 %fusion.60 = f32[4,32,4,256]{3,1,0,2:T(8,128)S(1)} fusion(bf16[1,4,3072,256]{3,2,1,0:T(8,128)(2,1)} %param.9, bf16[32,4,3072,1]{2,1,0,3:T(4,128)(2,1)S(1)} %bitcast.310), kind=kOutput, calls=%fused_computation.44 | convolution fusion | flops 805306368 | bytes 7602176 | tf_op jit(solution)/shard_map/fmd,edh->efmh/dot_general | solution.py:82
  118.3 6.7 %fusion.42 = f32[32,4,3072]{2,0,1:T(8,128)S(1)} fusion(bf16[1,4,256,3072]{3,2,1,0:T(8,128)(2,1)} %param.11, bf16[1,4,3072,256]{3,2,1,0:T(8,128)(2,1)} %param.10, bf16[32,4,3072,1]{2,1,0,3:T(4,128)(2,1)S(1)} %bitcast.311, f32[4,32,4,256]{3,1,0,2:T(8,128)S(1)} %fusion.60, f32[4,32,4]{1,0,2:T(4,128)S(1)} %copy.128), kind=kOutput, calls=%fused_computation.38 | convolution fusion | flops 1611530240 | bytes 15468544 | tf_op jit(solution)/shard_map/efmh,ehd->fmd/dot_general | solution.py:85
  125.3 2.1 collective-permute-done.7
  127.9 0.9 reshape.164.src_ref
  128.8 11.5 %shard_map.78 = bf16[16,96,128]{2,1,0:T(8,128)(2,1)} custom-call(bf16[16,96,128]{2,1,0:T(8,128)(2,1)} %reshape.164.src_ref), custom_call_target="tpu_custom_call" | custom-call | tf_op jit(solution)/shard_map/pallas_call | solution.py:42
  140.3 1.1 convert_reduce_fusion.3
  141.4 1.3 collective-permute-start.8
  142.7 4.4 %collective-permute-done.8 = bf16[4,3072]{1,0:T(4,128)(2,1)S(1)} collective-permute-done((bf16[4,3072]{1,0:T(4,128)(2,1)S(1)}, bf16[4,3072]{1,0:T(4,128)(2,1)S(1)}, u32[]{:S(2)}, u32[]{:S(2)}) %collective-permute-start.8) | collective-permute-done | bytes 24608 | tf_op jit(solution)/shard_map/ppermute | solution.py:59
  148.0 10.4 %shard_map.79 = bf16[16,96,128]{2,1,0:T(8,128)(2,1)} custom-call(bf16[96,128]{1,0:T(8,128)(2,1)} %reshape.166.src_ref), custom_call_target="tpu_custom_call" | custom-call | tf_op jit(solution)/shard_map/pallas_call | solution.py:42
  158.5 1.9 collective-permute-done.9
  160.4 1.1 pad_maximum_fusion.3
  161.6 3.9 %fusion.63 = f32[4,32,4,256]{3,1,0,2:T(8,128)S(1)} fusion(bf16[1,4,3072,256]{3,2,1,0:T(8,128)(2,1)} %param.9, bf16[32,4,3072,1]{2,1,0,3:T(4,128)(2,1)S(1)} %bitcast.312), kind=kOutput, calls=%fused_computation.45 | convolution fusion | flops 805306368 | bytes 7602176 | tf_op jit(solution)/shard_map/fmd,edh->efmh/dot_general | solution.py:82
  165.5 6.7 %fusion.45 = f32[32,4,3072]{2,0,1:T(8,128)S(1)} fusion(bf16[1,4,256,3072]{3,2,1,0:T(8,128)(2,1)} %param.11, bf16[1,4,3072,256]{3,2,1,0:T(8,128)(2,1)} %param.10, bf16[32,4,3072,1]{2,1,0,3:T(4,128)(2,1)S(1)} %bitcast.313, f32[4,32,4,256]{3,1,0,2:T(8,128)S(1)} %fusion.63, f32[4,32,4]{1,0,2:T(4,128)S(1)} %copy.132), kind=kOutput, calls=%fused_computation.39 | convolution fusion | flops 1611530240 | bytes 15468544 | tf_op jit(solution)/shard_map/efmh,ehd->fmd/dot_general | solution.py:85
  172.5 2.1 collective-permute-done.10
  175.0 0.9 reshape.168.src_ref
  175.9 11.6 %shard_map.80 = bf16[16,96,128]{2,1,0:T(8,128)(2,1)} custom-call(bf16[16,96,128]{2,1,0:T(8,128)(2,1)} %reshape.168.src_ref), custom_call_target="tpu_custom_call" | custom-call | tf_op jit(solution)/shard_map/pallas_call | solution.py:42
  187.5 1.1 convert_reduce_fusion.2
  188.6 1.3 collective-permute-start.11
  189.9 4.4 %collective-permute-done.11 = bf16[4,3072]{1,0:T(4,128)(2,1)S(1)} collective-permute-done((bf16[4,3072]{1,0:T(4,128)(2,1)S(1)}, bf16[4,3072]{1,0:T(4,128)(2,1)S(1)}, u32[]{:S(2)}, u32[]{:S(2)}) %collective-permute-start.11) | collective-permute-done | bytes 24608 | tf_op jit(solution)/shard_map/ppermute | solution.py:59
  195.2 10.3 %shard_map.81 = bf16[16,96,128]{2,1,0:T(8,128)(2,1)} custom-call(bf16[96,128]{1,0:T(8,128)(2,1)} %reshape.170.src_ref), custom_call_target="tpu_custom_call" | custom-call | tf_op jit(solution)/shard_map/pallas_call | solution.py:42
  205.9 1.9 collective-permute-done.12
  207.8 1.1 pad_maximum_fusion.4
  209.0 3.9 %fusion.66 = f32[4,32,4,256]{3,1,0,2:T(8,128)S(1)} fusion(bf16[1,4,3072,256]{3,2,1,0:T(8,128)(2,1)} %param.9, bf16[32,4,3072,1]{2,1,0,3:T(4,128)(2,1)S(1)} %bitcast.314), kind=kOutput, calls=%fused_computation.46 | convolution fusion | flops 805306368 | bytes 7602176 | tf_op jit(solution)/shard_map/fmd,edh->efmh/dot_general | solution.py:82
  212.9 6.7 %fusion.48 = f32[32,4,3072]{2,0,1:T(8,128)S(1)} fusion(bf16[1,4,256,3072]{3,2,1,0:T(8,128)(2,1)} %param.11, bf16[1,4,3072,256]{3,2,1,0:T(8,128)(2,1)} %param.10, bf16[32,4,3072,1]{2,1,0,3:T(4,128)(2,1)S(1)} %bitcast.315, f32[4,32,4,256]{3,1,0,2:T(8,128)S(1)} %fusion.66, f32[4,32,4]{1,0,2:T(4,128)S(1)} %copy.136), kind=kOutput, calls=%fused_computation.40 | convolution fusion | flops 1611530240 | bytes 15468544 | tf_op jit(solution)/shard_map/efmh,ehd->fmd/dot_general | solution.py:85
  219.9 2.1 collective-permute-done.13
  222.4 0.9 reshape.172.src_ref
  223.3 11.5 %shard_map.82 = bf16[16,96,128]{2,1,0:T(8,128)(2,1)} custom-call(bf16[16,96,128]{2,1,0:T(8,128)(2,1)} %reshape.172.src_ref), custom_call_target="tpu_custom_call" | custom-call | tf_op jit(solution)/shard_map/pallas_call | solution.py:42
  234.8 1.1 convert_reduce_fusion.1
  235.9 1.3 collective-permute-start.14
  237.2 4.4 %collective-permute-done.14 = bf16[4,3072]{1,0:T(4,128)(2,1)S(1)} collective-permute-done((bf16[4,3072]{1,0:T(4,128)(2,1)S(1)}, bf16[4,3072]{1,0:T(4,128)(2,1)S(1)}, u32[]{:S(2)}, u32[]{:S(2)}) %collective-permute-start.14) | collective-permute-done | bytes 24608 | tf_op jit(solution)/shard_map/ppermute | solution.py:59
  242.5 10.4 %shard_map.83 = bf16[16,96,128]{2,1,0:T(8,128)(2,1)} custom-call(bf16[96,128]{1,0:T(8,128)(2,1)} %reshape.174.src_ref), custom_call_target="tpu_custom_call" | custom-call | tf_op jit(solution)/shard_map/pallas_call | solution.py:42
  253.0 1.9 collective-permute-done.15
  254.9 1.1 pad_maximum_fusion.5
  256.2 3.9 %fusion.69 = f32[4,32,4,256]{3,1,0,2:T(8,128)S(1)} fusion(bf16[1,4,3072,256]{3,2,1,0:T(8,128)(2,1)} %param.9, bf16[32,4,3072,1]{2,1,0,3:T(4,128)(2,1)S(1)} %bitcast.316), kind=kOutput, calls=%fused_computation.47 | convolution fusion | flops 805306368 | bytes 7602176 | tf_op jit(solution)/shard_map/fmd,edh->efmh/dot_general | solution.py:82
  260.0 6.7 %fusion.51 = f32[32,4,3072]{2,0,1:T(8,128)S(1)} fusion(bf16[1,4,256,3072]{3,2,1,0:T(8,128)(2,1)} %param.11, bf16[1,4,3072,256]{3,2,1,0:T(8,128)(2,1)} %param.10, bf16[32,4,3072,1]{2,1,0,3:T(4,128)(2,1)S(1)} %bitcast.317, f32[4,32,4,256]{3,1,0,2:T(8,128)S(1)} %fusion.69, f32[4,32,4]{1,0,2:T(4,128)S(1)} %copy.140), kind=kOutput, calls=%fused_computation.41 | convolution fusion | flops 1611530240 | bytes 15468544 | tf_op jit(solution)/shard_map/efmh,ehd->fmd/dot_general | solution.py:85
  267.6 1.5 collective-permute-done.16
  269.6 0.9 reshape.176.src_ref
  270.5 11.5 %shard_map.84 = bf16[16,96,128]{2,1,0:T(8,128)(2,1)} custom-call(bf16[16,96,128]{2,1,0:T(8,128)(2,1)} %reshape.176.src_ref), custom_call_target="tpu_custom_call" | custom-call | tf_op jit(solution)/shard_map/pallas_call | solution.py:42
  282.0 1.1 convert_reduce_fusion
  (95 shorter events, 15.5 us)
Async XLA Ops:
  16.6 2.0 collective-permute-start
  30.4 16.5 %copy-start = (bf16[3,4,3072]{2,1,0:T(4,128)(2,1)S(1)}, bf16[3,4,3072]{2,1,0:T(4,128)(2,1)}, u32[]{:S(2)}) copy-start(bf16[3,4,3072]{2,1,0:T(4,128)(2,1)} %param.7) | copy-start | bytes 221188
  30.4 22.4 %copy-start.1 = (f32[1,3072]{1,0:T(1,128)S(1)}, f32[1,3072]{1,0:T(1,128)}, u32[]{:S(2)}) copy-start(f32[1,3072]{1,0:T(1,128)} %param.8) | copy-start | bytes 36868
  30.5 2.4 collective-permute-start.1
  46.9 5.7 %collective-permute-start.2 = (bf16[4,3072]{1,0:T(4,128)(2,1)S(1)}, bf16[4,3072]{1,0:T(4,128)(2,1)S(1)}, u32[]{:S(2)}, u32[]{:S(2)}) collective-permute-start(bf16[4,3072]{1,0:T(4,128)(2,1)S(1)} %fusion.244), channel_id=1, source_target_pairs={{0,32},{32,64},{64,96},{1,33},{33,65},{65,97},{2,34},{34,66},{66,9... | collective-permute-start | bytes 73736 | tf_op jit(solution)/shard_map/ppermute | solution.py:59
  64.1 2.0 collective-permute-start.3
  78.0 2.4 collective-permute-start.4
  94.3 5.7 %collective-permute-start.5 = (bf16[4,3072]{1,0:T(4,128)(2,1)S(1)}, bf16[4,3072]{1,0:T(4,128)(2,1)S(1)}, u32[]{:S(2)}, u32[]{:S(2)}) collective-permute-start(bf16[4,3072]{1,0:T(4,128)(2,1)S(1)} %get-tuple-element.20), channel_id=1, source_target_pairs={{0,32},{32,64},{64,96},{1,33},{33,65},{65,97},{2,34},{34,66},{66,9... | collective-permute-start | bytes 73736 | tf_op jit(solution)/shard_map/ppermute | solution.py:59
  111.2 2.0 collective-permute-start.6
  125.1 2.4 collective-permute-start.7
  141.4 5.7 %collective-permute-start.8 = (bf16[4,3072]{1,0:T(4,128)(2,1)S(1)}, bf16[4,3072]{1,0:T(4,128)(2,1)S(1)}, u32[]{:S(2)}, u32[]{:S(2)}) collective-permute-start(bf16[4,3072]{1,0:T(4,128)(2,1)S(1)} %get-tuple-element.16), channel_id=1, source_target_pairs={{0,32},{32,64},{64,96},{1,33},{33,65},{65,97},{2,34},{34,66},{66,9... | collective-permute-start | bytes 73736 | tf_op jit(solution)/shard_map/ppermute | solution.py:59
  158.4 2.0 collective-permute-start.9
  172.3 2.4 collective-permute-start.10
  188.6 5.7 %collective-permute-start.11 = (bf16[4,3072]{1,0:T(4,128)(2,1)S(1)}, bf16[4,3072]{1,0:T(4,128)(2,1)S(1)}, u32[]{:S(2)}, u32[]{:S(2)}) collective-permute-start(bf16[4,3072]{1,0:T(4,128)(2,1)S(1)} %get-tuple-element.12), channel_id=1, source_target_pairs={{0,32},{32,64},{64,96},{1,33},{33,65},{65,97},{2,34},{34,66},{66,9... | collective-permute-start | bytes 73736 | tf_op jit(solution)/shard_map/ppermute | solution.py:59
  205.5 2.2 collective-permute-start.12
  219.6 2.4 collective-permute-start.13
  235.9 5.7 %collective-permute-start.14 = (bf16[4,3072]{1,0:T(4,128)(2,1)S(1)}, bf16[4,3072]{1,0:T(4,128)(2,1)S(1)}, u32[]{:S(2)}, u32[]{:S(2)}) collective-permute-start(bf16[4,3072]{1,0:T(4,128)(2,1)S(1)} %get-tuple-element.8), channel_id=1, source_target_pairs={{0,32},{32,64},{64,96},{1,33},{33,65},{65,97},{2,34},{34,66},{66,9... | collective-permute-start | bytes 73736 | tf_op jit(solution)/shard_map/ppermute | solution.py:59
  252.9 2.0 collective-permute-start.15
  266.8 2.4 collective-permute-start.16

commit v3 on v2

--- a/solution.py
+++ b/solution.py
@@ -78,11 +78,44 @@
     return coef.reshape(micro, shards, per, experts).transpose(0, 3, 1, 2)
 
 
+def expert_kernel(rows_ref, coef_ref, gate_ref, up_ref, down_ref, out_ref):
+    expert = pl.program_id(0)
+
+    @pl.when(expert == 0)
+    def _():
+        out_ref[...] = jnp.zeros_like(out_ref)
+
+    rows = rows_ref[...]
+    gate = jnp.dot(rows, gate_ref[0], preferred_element_type=jnp.float32)
+    upward = jnp.dot(rows, up_ref[0], preferred_element_type=jnp.float32)
+    gated = (jax.nn.silu(gate) * upward * coef_ref[0]).astype(jnp.bfloat16)
+    out_ref[...] += jnp.dot(gated, down_ref[0], preferred_element_type=jnp.float32)
+
+
 def expert_mix(rows, coef, gate_w, up_w, down_w):
-    gate = jnp.einsum("fmd,edh->efmh", rows, gate_w, preferred_element_type=jnp.float32)
-    upward = jnp.einsum("fmd,edh->efmh", rows, up_w, preferred_element_type=jnp.float32)
-    gated = (jax.nn.silu(gate) * upward * coef[..., None]).astype(jnp.bfloat16)
-    return jnp.einsum("efmh,ehd->fmd", gated, down_w, preferred_element_type=jnp.float32)
+    tokens, width = rows.shape
+    experts, _, hidden = gate_w.shape
+    flops = 6 * tokens * width * hidden * experts
+    weight_bytes = 3 * experts * width * hidden * 2
+    return pl.pallas_call(
+        expert_kernel,
+        grid=(experts,),
+        out_shape=jax.ShapeDtypeStruct((tokens, width), jnp.float32),
+        in_specs=[
+            pl.BlockSpec((tokens, width), lambda e: (0, 0)),
+            pl.BlockSpec((1, tokens, 1), lambda e: (e, 0, 0)),
+            pl.BlockSpec((1, width, hidden), lambda e: (e, 0, 0)),
+            pl.BlockSpec((1, width, hidden), lambda e: (e, 0, 0)),
+            pl.BlockSpec((1, hidden, width), lambda e: (e, 0, 0)),
+        ],
+        out_specs=pl.BlockSpec((tokens, width), lambda e: (0, 0)),
+        compiler_params=pltpu.CompilerParams(dimension_semantics=("arbitrary",)),
+        cost_estimate=pl.CostEstimate(
+            flops=flops,
+            transcendentals=tokens * hidden * experts,
+            bytes_accessed=weight_bytes + tokens * width * 6,
+        ),
+    )(rows, coef, gate_w, up_w, down_w)
 
 
 def on_device(inputs, gain, w_gate, w_up, w_down, routes, shares):
@@ -104,6 +137,7 @@
         ],
         axis=2,
     )
+    coef = coef.reshape(micro, experts, shards * local, 1)
     output = jnp.zeros_like(inputs)
     carried = None
     for tick in range(micro + sections - 1):
@@ -116,8 +150,8 @@
         normed = rms_norm(current, gain_row)
         lanes = local * width // 128
         near = exchange(normed.reshape(lanes, 128), chips, True, 0)
-        rows = jnp.concatenate([near, sibling(near, "fsdp")], axis=0).reshape(shards, local, width)
-        partial_value = expert_mix(rows, coef_now, gate_w, up_w, down_w)
+        rows = jnp.concatenate([near, sibling(near, "fsdp")], axis=0).reshape(shards * local, width)
+        partial_value = expert_mix(rows, coef_now, gate_w, up_w, down_w).reshape(shards, local, width)
         chip_sum = partial_value[:chips] + sibling(partial_value[chips:], "fsdp")
         sent = chip_sum.astype(jnp.bfloat16).reshape(chips, lanes, 128)
         pieces = exchange(sent, chips, False, 1)

time: 285 us -> 298 us (1.046)
  matrix products: 63.2 us -> 0 us
  Pallas kernels: 135 us -> 196 us
  local copies, waits for them, and re-layouts: 13.4 us -> 34.5 us
  waiting for transfers between devices: 43.9 us -> 37.9 us
    dot_general x12 -> x0, matrix products: 63.2 us -> none  [the longest x6 40.1 us: expert_mix(): jnp.einsum('efmh,ehd->fmd', gated, down_w, preferred_element_type=jnp.flo...]
    pallas_call x0 -> x6, Pallas kernels: none -> 60.7 us  [expert_mix(): pl.pallas_call(expert_kernel, grid=(experts,), out_shape=jax.ShapeDtypeSt...]
    slice x6 -> x18, local copies, waits for them, and re-layouts: 0.32 us -> 11.6 us  [on_device(): chip_sum = partial_value[:chips] + sibling(partial_value[chips:], 'fsdp')]
    reshape x6, local copies, waits for them, and re-layouts: 1.07 us -> 7.34 us  [on_device(): jnp.concatenate([near, sibling(near, 'fsdp')], axis=0)]
    ppermute x12, waiting for transfers between devices: 22 us -> 15.8 us  [sibling(): return lax.ppermute(array, axis, [(i, i ^ 1) for i in range(devices)])]
    squeeze x0 -> x7, local copies, waits for them, and re-layouts: none -> 5.18 us  [on_device(): coef_now = lax.dynamic_index_in_dim(coef, clipped, 0, keepdims=False)]
  transfers between devices with their start and end apart: 17 -> 17, of which waited for: 17 -> 16; matrix products, arithmetic and copies ran while one was open for 1% -> 3% of each run, Pallas kernels for 0% -> 0%
where the time goes in v3:
time: 298 us; the launch traced here: 297 us
  Pallas kernels  196 us (66%)
  waiting for transfers between devices  37.9 us (13%)
  local copies, waits for them, and re-layouts  34.5 us (12%)
  other arithmetic  18.9 us (6%)
  starting transfers between devices  9 us (3%)
    pallas_call x12, Pallas kernels, exchange(): pl.pallas_call(kernel, out_shape=jax.ShapeDtypeStruct((chips, rows, width...  135 us
    pallas_call x6, Pallas kernels, expert_mix(): pl.pallas_call(expert_kernel, grid=(experts,), out_shape=jax.ShapeDtypeSt...  60.7 us
    ppermute x5, waiting for transfers between devices, passed_along(): return lax.ppermute(array, axis, pairs)  22.1 us
    ppermute x12, waiting for transfers between devices, sibling(): return lax.ppermute(array, axis, [(i, i ^ 1) for i in range(devices)])  15.8 us
    slice x18, local copies, waits for them, and re-layouts, on_device(): chip_sum = partial_value[:chips] + sibling(partial_value[chips:], 'fsdp')  11.6 us
    reshape x6, local copies, waits for them, and re-layouts, on_device(): jnp.concatenate([near, sibling(near, 'fsdp')], axis=0)  7.34 us
    ppermute x5, starting transfers between devices, passed_along(): return lax.ppermute(array, axis, pairs)  6.46 us
    reduce_sum x6, other arithmetic, on_device(): mixed = jnp.sum(pieces.astype(jnp.float32), axis=0).reshape(local, width)  6.36 us
  transfers between devices with their start and end apart: 17, of which 16 were waited for; matrix products, arithmetic and copies ran while one was open for 3% of the time, Pallas kernels for 0%

profile of v3, /device:TPU:24, one launch (start us, length us, event | category | flops | bytes accessed | tf_op | source)
XLA Modules:
  0.0 296.7 jit_solution(7377764302585097215)
XLA Ops:
  1.8 1.4 fusion.20.src_ref
  3.2 13.3 %shard_map.73 = bf16[16,96,128]{2,1,0:T(8,128)(2,1)} custom-call(bf16[96,128]{1,0:T(8,128)(2,1)} %fusion.20.src_ref), custom_call_target="tpu_custom_call" | custom-call | tf_op jit(solution)/shard_map/pallas_call | solution.py:42
  19.5 1.2 reshape.161.rows_ref
  20.8 10.1 %shard_map.74 = f32[128,3072]{1,0:T(8,128)} custom-call(bf16[128,3072]{1,0:T(8,128)(2,1)} %reshape.161.rows_ref, f32[4,128,1]{2,1,0:T(8,128)} %copy.49.coef_ref, bf16[4,3072,256]{2,1,0:T(8,128)(2,1)} %bitcast.83, bf16[4,3072,256]{2,1,0:T(8,128)(2,1)} %bitcast.89, bf16[4,256,3072]{2,1,0:T(8,128)(2,1)} %bitcast.95), custom_call_target="tpu_custom_call" | custom-call | flops 2415919104 | bytes 21233664 | tf_op jit(solution)/shard_map/pallas_call | solution.py:100
  30.9 1.5 fusion.49
  33.4 1.7 collective-permute-done.1
  36.2 11.6 %shard_map.75 = bf16[16,96,128]{2,1,0:T(8,128)(2,1)} custom-call(bf16[16,96,128]{2,1,0:T(8,128)(2,1)} %reshape.165.src_ref), custom_call_target="tpu_custom_call" | custom-call | tf_op jit(solution)/shard_map/pallas_call | solution.py:42
  47.8 1.1 convert_reduce_fusion.5
  49.0 1.3 collective-permute-start.2
  50.3 4.4 %collective-permute-done.2 = bf16[4,3072]{1,0:T(4,128)(2,1)S(1)} collective-permute-done((bf16[4,3072]{1,0:T(4,128)(2,1)S(1)}, bf16[4,3072]{1,0:T(4,128)(2,1)S(1)}, u32[]{:S(2)}, u32[]{:S(2)}) %collective-permute-start.2) | collective-permute-done | bytes 24608 | tf_op jit(solution)/shard_map/ppermute | solution.py:59
  55.6 10.8 %shard_map.76 = bf16[16,96,128]{2,1,0:T(8,128)(2,1)} custom-call(bf16[96,128]{1,0:T(8,128)(2,1)} %reshape.168.src_ref), custom_call_target="tpu_custom_call" | custom-call | tf_op jit(solution)/shard_map/pallas_call | solution.py:42
  67.4 1.1 collective-permute-done.3
  68.4 1.1 pad_maximum_fusion.1
  69.5 1.2 reshape.169.rows_ref
  70.7 10.1 %shard_map.77 = f32[128,3072]{1,0:T(8,128)} custom-call(bf16[128,3072]{1,0:T(8,128)(2,1)} %reshape.169.rows_ref, f32[4,128,1]{2,1,0:T(8,128)} %copy.50.coef_ref, bf16[4,3072,256]{2,1,0:T(8,128)(2,1)} %bitcast.84, bf16[4,3072,256]{2,1,0:T(8,128)(2,1)} %bitcast.90, bf16[4,256,3072]{2,1,0:T(8,128)(2,1)} %bitcast.96), custom_call_target="tpu_custom_call" | custom-call | flops 2415919104 | bytes 21233664 | tf_op jit(solution)/shard_map/pallas_call | solution.py:100
  80.8 1.5 fusion.48
  83.1 1.8 collective-permute-done.4
  86.0 11.8 %shard_map.78 = bf16[16,96,128]{2,1,0:T(8,128)(2,1)} custom-call(bf16[16,96,128]{2,1,0:T(8,128)(2,1)} %reshape.170.src_ref), custom_call_target="tpu_custom_call" | custom-call | tf_op jit(solution)/shard_map/pallas_call | solution.py:42
  97.8 1.1 convert_reduce_fusion.4
  98.9 1.3 collective-permute-start.5
  100.2 4.4 %collective-permute-done.5 = bf16[4,3072]{1,0:T(4,128)(2,1)S(1)} collective-permute-done((bf16[4,3072]{1,0:T(4,128)(2,1)S(1)}, bf16[4,3072]{1,0:T(4,128)(2,1)S(1)}, u32[]{:S(2)}, u32[]{:S(2)}) %collective-permute-start.5) | collective-permute-done | bytes 24608 | tf_op jit(solution)/shard_map/ppermute | solution.py:59
  105.5 10.2 %shard_map.79 = bf16[16,96,128]{2,1,0:T(8,128)(2,1)} custom-call(bf16[96,128]{1,0:T(8,128)(2,1)} %reshape.172.src_ref), custom_call_target="tpu_custom_call" | custom-call | tf_op jit(solution)/shard_map/pallas_call | solution.py:42
  116.6 1.1 collective-permute-done.6
  117.7 1.1 pad_maximum_fusion.2
  118.8 1.2 reshape.173.rows_ref
  120.0 10.1 %shard_map.80 = f32[128,3072]{1,0:T(8,128)} custom-call(bf16[128,3072]{1,0:T(8,128)(2,1)} %reshape.173.rows_ref, f32[4,128,1]{2,1,0:T(8,128)} %copy.51.coef_ref, bf16[4,3072,256]{2,1,0:T(8,128)(2,1)} %bitcast.85, bf16[4,3072,256]{2,1,0:T(8,128)(2,1)} %bitcast.91, bf16[4,256,3072]{2,1,0:T(8,128)(2,1)} %bitcast.97), custom_call_target="tpu_custom_call" | custom-call | flops 2415919104 | bytes 21233664 | tf_op jit(solution)/shard_map/pallas_call | solution.py:100
  130.1 1.5 fusion.47
  132.5 1.9 collective-permute-done.7
  134.6 0.9 reshape.174.src_ref
  135.5 11.5 %shard_map.81 = bf16[16,96,128]{2,1,0:T(8,128)(2,1)} custom-call(bf16[16,96,128]{2,1,0:T(8,128)(2,1)} %reshape.174.src_ref), custom_call_target="tpu_custom_call" | custom-call | tf_op jit(solution)/shard_map/pallas_call | solution.py:42
  147.0 1.1 convert_reduce_fusion.3
  148.1 1.3 collective-permute-start.8
  149.4 4.4 %collective-permute-done.8 = bf16[4,3072]{1,0:T(4,128)(2,1)S(1)} collective-permute-done((bf16[4,3072]{1,0:T(4,128)(2,1)S(1)}, bf16[4,3072]{1,0:T(4,128)(2,1)S(1)}, u32[]{:S(2)}, u32[]{:S(2)}) %collective-permute-start.8) | collective-permute-done | bytes 24608 | tf_op jit(solution)/shard_map/ppermute | solution.py:59
  154.7 10.4 %shard_map.82 = bf16[16,96,128]{2,1,0:T(8,128)(2,1)} custom-call(bf16[96,128]{1,0:T(8,128)(2,1)} %reshape.176.src_ref), custom_call_target="tpu_custom_call" | custom-call | tf_op jit(solution)/shard_map/pallas_call | solution.py:42
  166.0 1.1 collective-permute-done.9
  167.1 1.1 pad_maximum_fusion.3
  168.2 1.2 reshape.177.rows_ref
  169.4 10.1 %shard_map.83 = f32[128,3072]{1,0:T(8,128)} custom-call(bf16[128,3072]{1,0:T(8,128)(2,1)} %reshape.177.rows_ref, f32[4,128,1]{2,1,0:T(8,128)} %copy.52.coef_ref, bf16[4,3072,256]{2,1,0:T(8,128)(2,1)} %bitcast.86, bf16[4,3072,256]{2,1,0:T(8,128)(2,1)} %bitcast.92, bf16[4,256,3072]{2,1,0:T(8,128)(2,1)} %bitcast.98), custom_call_target="tpu_custom_call" | custom-call | flops 2415919104 | bytes 21233664 | tf_op jit(solution)/shard_map/pallas_call | solution.py:100
  179.5 1.5 fusion.46
  181.7 1.9 collective-permute-done.10
  184.7 11.6 %shard_map.84 = bf16[16,96,128]{2,1,0:T(8,128)(2,1)} custom-call(bf16[16,96,128]{2,1,0:T(8,128)(2,1)} %reshape.178.src_ref), custom_call_target="tpu_custom_call" | custom-call | tf_op jit(solution)/shard_map/pallas_call | solution.py:42
  196.3 1.1 convert_reduce_fusion.2
  197.4 1.3 collective-permute-start.11
  198.7 4.4 %collective-permute-done.11 = bf16[4,3072]{1,0:T(4,128)(2,1)S(1)} collective-permute-done((bf16[4,3072]{1,0:T(4,128)(2,1)S(1)}, bf16[4,3072]{1,0:T(4,128)(2,1)S(1)}, u32[]{:S(2)}, u32[]{:S(2)}) %collective-permute-start.11) | collective-permute-done | bytes 24608 | tf_op jit(solution)/shard_map/ppermute | solution.py:59
  204.0 10.3 %shard_map.85 = bf16[16,96,128]{2,1,0:T(8,128)(2,1)} custom-call(bf16[96,128]{1,0:T(8,128)(2,1)} %reshape.180.src_ref), custom_call_target="tpu_custom_call" | custom-call | tf_op jit(solution)/shard_map/pallas_call | solution.py:42
  215.3 1.1 collective-permute-done.12
  216.3 1.1 pad_maximum_fusion.4
  217.4 1.2 reshape.181.rows_ref
  218.6 10.1 %shard_map.86 = f32[128,3072]{1,0:T(8,128)} custom-call(bf16[128,3072]{1,0:T(8,128)(2,1)} %reshape.181.rows_ref, f32[4,128,1]{2,1,0:T(8,128)} %copy.53.coef_ref, bf16[4,3072,256]{2,1,0:T(8,128)(2,1)} %bitcast.87, bf16[4,3072,256]{2,1,0:T(8,128)(2,1)} %bitcast.93, bf16[4,256,3072]{2,1,0:T(8,128)(2,1)} %bitcast.99), custom_call_target="tpu_custom_call" | custom-call | flops 2415919104 | bytes 21233664 | tf_op jit(solution)/shard_map/pallas_call | solution.py:100
  228.7 1.5 fusion.45
  230.9 1.9 collective-permute-done.13
  233.9 11.5 %shard_map.87 = bf16[16,96,128]{2,1,0:T(8,128)(2,1)} custom-call(bf16[16,96,128]{2,1,0:T(8,128)(2,1)} %reshape.182.src_ref), custom_call_target="tpu_custom_call" | custom-call | tf_op jit(solution)/shard_map/pallas_call | solution.py:42
  245.4 1.1 convert_reduce_fusion.1
  246.5 1.3 collective-permute-start.14
  247.8 4.4 %collective-permute-done.14 = bf16[4,3072]{1,0:T(4,128)(2,1)S(1)} collective-permute-done((bf16[4,3072]{1,0:T(4,128)(2,1)S(1)}, bf16[4,3072]{1,0:T(4,128)(2,1)S(1)}, u32[]{:S(2)}, u32[]{:S(2)}) %collective-permute-start.14) | collective-permute-done | bytes 24608 | tf_op jit(solution)/shard_map/ppermute | solution.py:59
  253.1 10.4 %shard_map.88 = bf16[16,96,128]{2,1,0:T(8,128)(2,1)} custom-call(bf16[96,128]{1,0:T(8,128)(2,1)} %reshape.184.src_ref), custom_call_target="tpu_custom_call" | custom-call | tf_op jit(solution)/shard_map/pallas_call | solution.py:42
  264.7 1.1 collective-permute-done.15
  265.8 1.1 pad_maximum_fusion.5
  266.8 1.2 reshape.185.rows_ref
  268.1 10.1 %shard_map.89 = f32[128,3072]{1,0:T(8,128)} custom-call(bf16[128,3072]{1,0:T(8,128)(2,1)} %reshape.185.rows_ref, f32[4,128,1]{2,1,0:T(8,128)} %copy.54.coef_ref, bf16[4,3072,256]{2,1,0:T(8,128)(2,1)} %bitcast.88, bf16[4,3072,256]{2,1,0:T(8,128)(2,1)} %bitcast.94, bf16[4,256,3072]{2,1,0:T(8,128)(2,1)} %bitcast.100), custom_call_target="tpu_custom_call" | custom-call | flops 2415919104 | bytes 21233664 | tf_op jit(solution)/shard_map/pallas_call | solution.py:100
  278.2 1.5 fusion.44
  281.0 1.3 collective-permute-done.16
  283.4 11.6 %shard_map.90 = bf16[16,96,128]{2,1,0:T(8,128)(2,1)} custom-call(bf16[16,96,128]{2,1,0:T(8,128)(2,1)} %reshape.186.src_ref), custom_call_target="tpu_custom_call" | custom-call | tf_op jit(solution)/shard_map/pallas_call | solution.py:42
  294.9 1.1 convert_reduce_fusion
  (100 shorter events, 25.8 us)
Async XLA Ops:
  16.6 2.9 copy-start
  16.6 2.9 collective-permute-start
  32.6 2.5 collective-permute-start.1
  33.4 15.5 %copy-start.1 = (bf16[3,4,3072]{2,1,0:T(4,128)(2,1)S(1)}, bf16[3,4,3072]{2,1,0:T(4,128)(2,1)}, u32[]{:S(2)}) copy-start(bf16[3,4,3072]{2,1,0:T(4,128)(2,1)} %param.7) | copy-start | bytes 221188
  35.3 19.6 %copy-start.2 = (f32[1,3072]{1,0:T(1,128)S(1)}, f32[1,3072]{1,0:T(1,128)}, u32[]{:S(2)}) copy-start(f32[1,3072]{1,0:T(1,128)} %param.8) | copy-start | bytes 36868
  49.0 5.7 %collective-permute-start.2 = (bf16[4,3072]{1,0:T(4,128)(2,1)S(1)}, bf16[4,3072]{1,0:T(4,128)(2,1)S(1)}, u32[]{:S(2)}, u32[]{:S(2)}) collective-permute-start(bf16[4,3072]{1,0:T(4,128)(2,1)S(1)} %fusion.22), channel_id=1, source_target_pairs={{0,32},{32,64},{64,96},{1,33},{33,65},{65,97},{2,34},{34,66},{66,9... | collective-permute-start | bytes 73736 | tf_op jit(solution)/shard_map/ppermute | solution.py:59
  66.4 2.0 collective-permute-start.3
  82.6 2.4 collective-permute-start.4
  98.9 5.7 %collective-permute-start.5 = (bf16[4,3072]{1,0:T(4,128)(2,1)S(1)}, bf16[4,3072]{1,0:T(4,128)(2,1)S(1)}, u32[]{:S(2)}, u32[]{:S(2)}) collective-permute-start(bf16[4,3072]{1,0:T(4,128)(2,1)S(1)} %get-tuple-element.20), channel_id=1, source_target_pairs={{0,32},{32,64},{64,96},{1,33},{33,65},{65,97},{2,34},{34,66},{66,9... | collective-permute-start | bytes 73736 | tf_op jit(solution)/shard_map/ppermute | solution.py:59
  115.7 2.0 collective-permute-start.6
  131.8 2.5 collective-permute-start.7
  148.1 5.7 %collective-permute-start.8 = (bf16[4,3072]{1,0:T(4,128)(2,1)S(1)}, bf16[4,3072]{1,0:T(4,128)(2,1)S(1)}, u32[]{:S(2)}, u32[]{:S(2)}) collective-permute-start(bf16[4,3072]{1,0:T(4,128)(2,1)S(1)} %get-tuple-element.16), channel_id=1, source_target_pairs={{0,32},{32,64},{64,96},{1,33},{33,65},{65,97},{2,34},{34,66},{66,9... | collective-permute-start | bytes 73736 | tf_op jit(solution)/shard_map/ppermute | solution.py:59
  165.1 2.0 collective-permute-start.9
  181.2 2.4 collective-permute-start.10
  197.4 5.7 %collective-permute-start.11 = (bf16[4,3072]{1,0:T(4,128)(2,1)S(1)}, bf16[4,3072]{1,0:T(4,128)(2,1)S(1)}, u32[]{:S(2)}, u32[]{:S(2)}) collective-permute-start(bf16[4,3072]{1,0:T(4,128)(2,1)S(1)} %get-tuple-element.12), channel_id=1, source_target_pairs={{0,32},{32,64},{64,96},{1,33},{33,65},{65,97},{2,34},{34,66},{66,9... | collective-permute-start | bytes 73736 | tf_op jit(solution)/shard_map/ppermute | solution.py:59
  214.3 2.0 collective-permute-start.12
  230.5 2.4 collective-permute-start.13
  246.5 5.7 %collective-permute-start.14 = (bf16[4,3072]{1,0:T(4,128)(2,1)S(1)}, bf16[4,3072]{1,0:T(4,128)(2,1)S(1)}, u32[]{:S(2)}, u32[]{:S(2)}) collective-permute-start(bf16[4,3072]{1,0:T(4,128)(2,1)S(1)} %get-tuple-element.8), channel_id=1, source_target_pairs={{0,32},{32,64},{64,96},{1,33},{33,65},{65,97},{2,34},{34,66},{66,9... | collective-permute-start | bytes 73736 | tf_op jit(solution)/shard_map/ppermute | solution.py:59
  263.5 2.2 collective-permute-start.15
  279.9 2.4 collective-permute-start.16

commit v4 on v2

--- a/solution.py
+++ b/solution.py
@@ -51,6 +51,87 @@
         ],
         compiler_params=pltpu.CompilerParams(collective_id=collective_id, has_side_effects=True),
     )(src)
+
+
+def reduce_relay(sent, current, chips, sections, collective_id):
+    _, rows, width = sent.shape
+
+    def kernel(sent_ref, current_ref, result_ref, carried_ref, pieces, send_sem, recv_sem,
+               local_sem, relay_send, relay_recv):
+        me = lax.axis_index("fsdp")
+        section = lax.axis_index("section")
+        chip, core = me // 2, me % 2
+        barrier = pltpu.get_barrier_semaphore()
+        for j in range(1, chips):
+            peer = lax.rem(chip + j, chips)
+            pl.semaphore_signal(barrier, 1, device_id=(section, peer * 2 + core), device_id_type=MESH)
+
+        @pl.when(section > 0)
+        def _():
+            pl.semaphore_signal(barrier, 1, device_id=(section - 1, me), device_id_type=MESH)
+
+        has_next = (sections - 1 - section + sections - 2) // (sections - 1)
+        pl.semaphore_wait(barrier, chips - 1 + has_next)
+
+        local = pltpu.make_async_copy(sent_ref.at[chip], pieces.at[chip], local_sem)
+        local.start()
+        copies = []
+        for j in range(1, chips):
+            peer = lax.rem(chip + j, chips)
+            copy = pltpu.make_async_remote_copy(
+                src_ref=sent_ref.at[peer],
+                dst_ref=pieces.at[chip],
+                send_sem=send_sem.at[j],
+                recv_sem=recv_sem.at[j],
+                device_id=(section, peer * 2 + core),
+                device_id_type=MESH,
+            )
+            copy.start()
+            copies.append(copy)
+        local.wait()
+        for copy in copies:
+            copy.wait()
+        mixed = pieces[0].astype(jnp.float32)
+        for k in range(1, chips):
+            mixed = mixed + pieces[k].astype(jnp.float32)
+        result_ref[...] = (current_ref[...].astype(jnp.float32) + mixed).astype(result_ref.dtype)
+        relay = pltpu.make_async_remote_copy(
+            src_ref=result_ref,
+            dst_ref=carried_ref,
+            send_sem=relay_send,
+            recv_sem=relay_recv,
+            device_id=(section + 1, me),
+            device_id_type=MESH,
+        )
+
+        @pl.when(section < sections - 1)
+        def _():
+            relay.start()
+            relay.wait_send()
+
+        @pl.when(section > 0)
+        def _():
+            relay.wait_recv()
+
+    vmem = pl.BlockSpec(memory_space=pltpu.VMEM)
+    return pl.pallas_call(
+        kernel,
+        out_shape=(
+            jax.ShapeDtypeStruct((rows, width), current.dtype),
+            jax.ShapeDtypeStruct((rows, width), current.dtype),
+        ),
+        in_specs=[pl.BlockSpec(memory_space=pl.ANY), vmem],
+        out_specs=(vmem, vmem),
+        scratch_shapes=[
+            pltpu.VMEM((chips, rows, width), sent.dtype),
+            pltpu.SemaphoreType.DMA((chips,)),
+            pltpu.SemaphoreType.DMA((chips,)),
+            pltpu.SemaphoreType.DMA(()),
+            pltpu.SemaphoreType.DMA(()),
+            pltpu.SemaphoreType.DMA(()),
+        ],
+        compiler_params=pltpu.CompilerParams(collective_id=collective_id, has_side_effects=True),
+    )(sent, current)
 
 
 def passed_along(array, axis, by):
@@ -120,11 +201,9 @@
         partial_value = expert_mix(rows, coef_now, gate_w, up_w, down_w)
         chip_sum = partial_value[:chips] + sibling(partial_value[chips:], "fsdp")
         sent = chip_sum.astype(jnp.bfloat16).reshape(chips, lanes, 128)
-        pieces = exchange(sent, chips, False, 1)
-        mixed = jnp.sum(pieces.astype(jnp.float32), axis=0).reshape(local, width)
-        result = (current.astype(jnp.float32) + mixed).astype(jnp.bfloat16)
-        if tick + 1 < micro + sections - 1:
-            carried = passed_along(result, "section", 1)
+        result, carried = reduce_relay(sent, current.reshape(lanes, 128), chips, sections, 1)
+        result = result.reshape(local, width)
+        carried = carried.reshape(local, width)
         updated = lax.dynamic_update_index_in_dim(output, result, clipped, 0)
         output = jnp.where(valid, updated, output)
     return output[None]

time: 285 us -> 278 us (0.975)
  waiting for transfers between devices: 43.9 us -> 21.7 us
  Pallas kernels: 135 us -> 154 us
  starting transfers between devices: 8.69 us -> 2.02 us
    pallas_call x0 -> x6, Pallas kernels: none -> 89.1 us  [reduce_relay(): pl.pallas_call(kernel, out_shape=(jax.ShapeDtypeStruct((rows, width), cur...]
    pallas_call x12 -> x6, Pallas kernels: 135 us -> 65.1 us  [exchange(): pl.pallas_call(kernel, out_shape=jax.ShapeDtypeStruct((chips, rows, width...]
    ppermute x5 -> x0, waiting for transfers between devices: 21.9 us -> none  [passed_along(): return lax.ppermute(array, axis, pairs)]
    convert_element_type x6, other arithmetic: 1.83 us -> 8.56 us  [rms_norm(): return (values * scale * gain_row[None, :]).astype(jnp.bfloat16)]
    ppermute x5 -> x0, starting transfers between devices: 6.64 us -> none  [passed_along(): return lax.ppermute(array, axis, pairs)]
    reduce_sum x6 -> x0, other arithmetic: 6.36 us -> none  [on_device(): mixed = jnp.sum(pieces.astype(jnp.float32), axis=0).reshape(local, width)]
  transfers between devices with their start and end apart: 17 -> 12, of which waited for: 17 -> 12; matrix products, arithmetic and copies ran while one was open for 1% -> 1% of each run, Pallas kernels for 0% -> 0%
where the time goes in v4:
time: 278 us; the launch traced here: 276 us
  Pallas kernels  154 us (55%)
  matrix products  63.2 us (23%)
  waiting for transfers between devices  21.7 us (8%)
  other arithmetic  18.7 us (7%)
  local copies, waits for them, and re-layouts  15.7 us (6%)
    pallas_call x6, Pallas kernels, reduce_relay(): pl.pallas_call(kernel, out_shape=(jax.ShapeDtypeStruct((rows, width), cur...  89.1 us
    pallas_call x6, Pallas kernels, exchange(): pl.pallas_call(kernel, out_shape=jax.ShapeDtypeStruct((chips, rows, width...  65.1 us
    dot_general x6, matrix products, expert_mix(): jnp.einsum('efmh,ehd->fmd', gated, down_w, preferred_element_type=jnp.flo...  40 us
    dot_general x6, matrix products, expert_mix(): jnp.einsum('fmd,edh->efmh', rows, gate_w, preferred_element_type=jnp.floa...  23.1 us
    ppermute x12, waiting for transfers between devices, sibling(): return lax.ppermute(array, axis, [(i, i ^ 1) for i in range(devices)])  21.7 us
    convert_element_type x6, other arithmetic, rms_norm(): return (values * scale * gain_row[None, :]).astype(jnp.bfloat16)  8.56 us
    concatenate x6, other arithmetic, on_device(): jnp.concatenate([near, sibling(near, 'fsdp')], axis=0)  6.39 us
  transfers between devices with their start and end apart: 12, of which 12 were waited for; matrix products, arithmetic and copies ran while one was open for 1% of the time, Pallas kernels for 0%

profile of v4, /device:TPU:24, one launch (start us, length us, event | category | flops | bytes accessed | tf_op | source)
XLA Modules:
  0.0 276.3 jit_solution(16350864030048874301)
XLA Ops:
  0.0 0.9 multiply_reduce_fusion.5
  1.1 1.4 fusion.222.src_ref
  2.5 13.3 %shard_map.73 = bf16[16,96,128]{2,1,0:T(8,128)(2,1)} custom-call(bf16[96,128]{1,0:T(8,128)(2,1)} %fusion.222.src_ref), custom_call_target="tpu_custom_call" | custom-call | tf_op jit(solution)/shard_map/pallas_call | solution.py:42
  15.9 0.7 select_reduce_fusion
  17.5 0.3 collective-permute-done
  17.8 1.1 pad_maximum_fusion
  19.1 3.9 %fusion.54 = f32[4,32,4,256]{3,1,0,2:T(8,128)S(1)} fusion(bf16[1,4,3072,256]{3,2,1,0:T(8,128)(2,1)} %param.9, bf16[32,4,3072,1]{2,1,0,3:T(4,128)(2,1)S(1)} %bitcast.292), kind=kOutput, calls=%fused_computation.42 | convolution fusion | flops 805306368 | bytes 7602176 | tf_op jit(solution)/shard_map/fmd,edh->efmh/dot_general | solution.py:163
  23.0 6.7 %fusion.36 = f32[32,4,3072]{2,0,1:T(8,128)S(1)} fusion(bf16[1,4,256,3072]{3,2,1,0:T(8,128)(2,1)} %param.11, bf16[1,4,3072,256]{3,2,1,0:T(8,128)(2,1)} %param.10, bf16[32,4,3072,1]{2,1,0,3:T(4,128)(2,1)S(1)} %bitcast.293, f32[4,32,4,256]{3,1,0,2:T(8,128)S(1)} %fusion.54, f32[4,32,4]{1,0,2:T(4,128)S(1)} %copy.120), kind=kOutput, calls=%fused_computation.36 | convolution fusion | flops 1611530240 | bytes 15468544 | tf_op jit(solution)/shard_map/efmh,ehd->fmd/dot_general | solution.py:166
  30.0 2.1 collective-permute-done.1
  32.5 0.9 reshape.198.sent_ref
  33.4 15.6 %shard_map.74 = (bf16[96,128]{1,0:T(8,128)(2,1)}, bf16[96,128]{1,0:T(8,128)(2,1)}) custom-call(bf16[16,96,128]{2,1,0:T(8,128)(2,1)} %reshape.198.sent_ref, bf16[96,128]{1,0:T(8,128)(2,1)} %copy-done.2), custom_call_target="tpu_custom_call" | custom-call | tf_op jit(solution)/shard_map/pallas_call | solution.py:117
  49.0 0.8 reshape.199
  50.1 1.4 fusion.223
  51.5 10.6 %shard_map.75 = bf16[16,96,128]{2,1,0:T(8,128)(2,1)} custom-call(bf16[96,128]{1,0:T(8,128)(2,1)} %get-tuple-element.43.src_ref), custom_call_target="tpu_custom_call" | custom-call | tf_op jit(solution)/shard_map/pallas_call | solution.py:42
  62.2 1.9 collective-permute-done.2
  64.1 1.1 pad_maximum_fusion.1
  65.4 3.9 %fusion.57 = f32[4,32,4,256]{3,1,0,2:T(8,128)S(1)} fusion(bf16[1,4,3072,256]{3,2,1,0:T(8,128)(2,1)} %param.9, bf16[32,4,3072,1]{2,1,0,3:T(4,128)(2,1)S(1)} %bitcast.294), kind=kOutput, calls=%fused_computation.43 | convolution fusion | flops 805306368 | bytes 7602176 | tf_op jit(solution)/shard_map/fmd,edh->efmh/dot_general | solution.py:163
  69.2 6.7 %fusion.39 = f32[32,4,3072]{2,0,1:T(8,128)S(1)} fusion(bf16[1,4,256,3072]{3,2,1,0:T(8,128)(2,1)} %param.11, bf16[1,4,3072,256]{3,2,1,0:T(8,128)(2,1)} %param.10, bf16[32,4,3072,1]{2,1,0,3:T(4,128)(2,1)S(1)} %bitcast.295, f32[4,32,4,256]{3,1,0,2:T(8,128)S(1)} %fusion.57, f32[4,32,4]{1,0,2:T(4,128)S(1)} %copy.124), kind=kOutput, calls=%fused_computation.37 | convolution fusion | flops 1611530240 | bytes 15468544 | tf_op jit(solution)/shard_map/efmh,ehd->fmd/dot_general | solution.py:166
  76.2 2.2 collective-permute-done.3
  78.7 0.9 reshape.201.sent_ref
  79.6 15.1 %shard_map.76 = (bf16[96,128]{1,0:T(8,128)(2,1)}, bf16[96,128]{1,0:T(8,128)(2,1)}) custom-call(bf16[16,96,128]{2,1,0:T(8,128)(2,1)} %reshape.201.sent_ref, bf16[96,128]{1,0:T(8,128)(2,1)} %get-tuple-element.44.current_ref), custom_call_target="tpu_custom_call" | custom-call | tf_op jit(solution)/shard_map/pallas_call | solution.py:117
  94.8 0.8 reshape.202
  95.8 1.4 fusion.224
  97.3 10.3 %shard_map.77 = bf16[16,96,128]{2,1,0:T(8,128)(2,1)} custom-call(bf16[96,128]{1,0:T(8,128)(2,1)} %get-tuple-element.39.src_ref), custom_call_target="tpu_custom_call" | custom-call | tf_op jit(solution)/shard_map/pallas_call | solution.py:42
  107.6 1.9 collective-permute-done.4
  109.5 1.1 pad_maximum_fusion.2
  110.8 3.9 %fusion.60 = f32[4,32,4,256]{3,1,0,2:T(8,128)S(1)} fusion(bf16[1,4,3072,256]{3,2,1,0:T(8,128)(2,1)} %param.9, bf16[32,4,3072,1]{2,1,0,3:T(4,128)(2,1)S(1)} %bitcast.296), kind=kOutput, calls=%fused_computation.44 | convolution fusion | flops 805306368 | bytes 7602176 | tf_op jit(solution)/shard_map/fmd,edh->efmh/dot_general | solution.py:163
  114.7 6.7 %fusion.42 = f32[32,4,3072]{2,0,1:T(8,128)S(1)} fusion(bf16[1,4,256,3072]{3,2,1,0:T(8,128)(2,1)} %param.11, bf16[1,4,3072,256]{3,2,1,0:T(8,128)(2,1)} %param.10, bf16[32,4,3072,1]{2,1,0,3:T(4,128)(2,1)S(1)} %bitcast.297, f32[4,32,4,256]{3,1,0,2:T(8,128)S(1)} %fusion.60, f32[4,32,4]{1,0,2:T(4,128)S(1)} %copy.128), kind=kOutput, calls=%fused_computation.38 | convolution fusion | flops 1611530240 | bytes 15468544 | tf_op jit(solution)/shard_map/efmh,ehd->fmd/dot_general | solution.py:166
  121.6 2.1 collective-permute-done.5
  124.1 0.9 reshape.204.sent_ref
  125.0 15.1 %shard_map.78 = (bf16[96,128]{1,0:T(8,128)(2,1)}, bf16[96,128]{1,0:T(8,128)(2,1)}) custom-call(bf16[16,96,128]{2,1,0:T(8,128)(2,1)} %reshape.204.sent_ref, bf16[96,128]{1,0:T(8,128)(2,1)} %get-tuple-element.40.current_ref), custom_call_target="tpu_custom_call" | custom-call | tf_op jit(solution)/shard_map/pallas_call | solution.py:117
  140.1 0.8 reshape.205
  141.2 1.4 fusion.225
  142.6 10.4 %shard_map.79 = bf16[16,96,128]{2,1,0:T(8,128)(2,1)} custom-call(bf16[96,128]{1,0:T(8,128)(2,1)} %get-tuple-element.35.src_ref), custom_call_target="tpu_custom_call" | custom-call | tf_op jit(solution)/shard_map/pallas_call | solution.py:42
  153.2 1.9 collective-permute-done.6
  155.1 1.1 pad_maximum_fusion.3
  156.3 3.9 %fusion.63 = f32[4,32,4,256]{3,1,0,2:T(8,128)S(1)} fusion(bf16[1,4,3072,256]{3,2,1,0:T(8,128)(2,1)} %param.9, bf16[32,4,3072,1]{2,1,0,3:T(4,128)(2,1)S(1)} %bitcast.298), kind=kOutput, calls=%fused_computation.45 | convolution fusion | flops 805306368 | bytes 7602176 | tf_op jit(solution)/shard_map/fmd,edh->efmh/dot_general | solution.py:163
  160.2 6.7 %fusion.45 = f32[32,4,3072]{2,0,1:T(8,128)S(1)} fusion(bf16[1,4,256,3072]{3,2,1,0:T(8,128)(2,1)} %param.11, bf16[1,4,3072,256]{3,2,1,0:T(8,128)(2,1)} %param.10, bf16[32,4,3072,1]{2,1,0,3:T(4,128)(2,1)S(1)} %bitcast.299, f32[4,32,4,256]{3,1,0,2:T(8,128)S(1)} %fusion.63, f32[4,32,4]{1,0,2:T(4,128)S(1)} %copy.132), kind=kOutput, calls=%fused_computation.39 | convolution fusion | flops 1611530240 | bytes 15468544 | tf_op jit(solution)/shard_map/efmh,ehd->fmd/dot_general | solution.py:166
  167.1 2.2 collective-permute-done.7
  169.7 0.9 reshape.207.sent_ref
  170.6 14.5 %shard_map.80 = (bf16[96,128]{1,0:T(8,128)(2,1)}, bf16[96,128]{1,0:T(8,128)(2,1)}) custom-call(bf16[16,96,128]{2,1,0:T(8,128)(2,1)} %reshape.207.sent_ref, bf16[96,128]{1,0:T(8,128)(2,1)} %get-tuple-element.36.current_ref), custom_call_target="tpu_custom_call" | custom-call | tf_op jit(solution)/shard_map/pallas_call | solution.py:117
  185.1 0.8 reshape.208
  186.2 1.4 fusion.226
  187.7 10.3 %shard_map.81 = bf16[16,96,128]{2,1,0:T(8,128)(2,1)} custom-call(bf16[96,128]{1,0:T(8,128)(2,1)} %get-tuple-element.31.src_ref), custom_call_target="tpu_custom_call" | custom-call | tf_op jit(solution)/shard_map/pallas_call | solution.py:42
  198.4 1.8 collective-permute-done.8
  200.2 1.1 pad_maximum_fusion.4
  201.4 3.9 %fusion.66 = f32[4,32,4,256]{3,1,0,2:T(8,128)S(1)} fusion(bf16[1,4,3072,256]{3,2,1,0:T(8,128)(2,1)} %param.9, bf16[32,4,3072,1]{2,1,0,3:T(4,128)(2,1)S(1)} %bitcast.300), kind=kOutput, calls=%fused_computation.46 | convolution fusion | flops 805306368 | bytes 7602176 | tf_op jit(solution)/shard_map/fmd,edh->efmh/dot_general | solution.py:163
  205.3 6.7 %fusion.48 = f32[32,4,3072]{2,0,1:T(8,128)S(1)} fusion(bf16[1,4,256,3072]{3,2,1,0:T(8,128)(2,1)} %param.11, bf16[1,4,3072,256]{3,2,1,0:T(8,128)(2,1)} %param.10, bf16[32,4,3072,1]{2,1,0,3:T(4,128)(2,1)S(1)} %bitcast.301, f32[4,32,4,256]{3,1,0,2:T(8,128)S(1)} %fusion.66, f32[4,32,4]{1,0,2:T(4,128)S(1)} %copy.136), kind=kOutput, calls=%fused_computation.40 | convolution fusion | flops 1611530240 | bytes 15468544 | tf_op jit(solution)/shard_map/efmh,ehd->fmd/dot_general | solution.py:166
  212.4 2.0 collective-permute-done.9
  214.8 0.9 reshape.210.sent_ref
  215.7 14.4 %shard_map.82 = (bf16[96,128]{1,0:T(8,128)(2,1)}, bf16[96,128]{1,0:T(8,128)(2,1)}) custom-call(bf16[16,96,128]{2,1,0:T(8,128)(2,1)} %reshape.210.sent_ref, bf16[96,128]{1,0:T(8,128)(2,1)} %get-tuple-element.32.current_ref), custom_call_target="tpu_custom_call" | custom-call | tf_op jit(solution)/shard_map/pallas_call | solution.py:117
  230.1 0.8 reshape.211
  231.2 1.4 fusion.227
  232.6 10.3 %shard_map.83 = bf16[16,96,128]{2,1,0:T(8,128)(2,1)} custom-call(bf16[96,128]{1,0:T(8,128)(2,1)} %get-tuple-element.27.src_ref), custom_call_target="tpu_custom_call" | custom-call | tf_op jit(solution)/shard_map/pallas_call | solution.py:42
  243.1 1.9 collective-permute-done.10
  245.0 1.1 pad_maximum_fusion.5
  246.2 3.9 %fusion.69 = f32[4,32,4,256]{3,1,0,2:T(8,128)S(1)} fusion(bf16[1,4,3072,256]{3,2,1,0:T(8,128)(2,1)} %param.9, bf16[32,4,3072,1]{2,1,0,3:T(4,128)(2,1)S(1)} %bitcast.302), kind=kOutput, calls=%fused_computation.47 | convolution fusion | flops 805306368 | bytes 7602176 | tf_op jit(solution)/shard_map/fmd,edh->efmh/dot_general | solution.py:163
  250.1 6.7 %fusion.51 = f32[32,4,3072]{2,0,1:T(8,128)S(1)} fusion(bf16[1,4,256,3072]{3,2,1,0:T(8,128)(2,1)} %param.11, bf16[1,4,3072,256]{3,2,1,0:T(8,128)(2,1)} %param.10, bf16[32,4,3072,1]{2,1,0,3:T(4,128)(2,1)S(1)} %bitcast.303, f32[4,32,4,256]{3,1,0,2:T(8,128)S(1)} %fusion.69, f32[4,32,4]{1,0,2:T(4,128)S(1)} %copy.140), kind=kOutput, calls=%fused_computation.41 | convolution fusion | flops 1611530240 | bytes 15468544 | tf_op jit(solution)/shard_map/efmh,ehd->fmd/dot_general | solution.py:166
  257.1 0.6 copy.219
  257.8 1.4 collective-permute-done.11
  259.6 0.9 reshape.213.sent_ref
  260.5 14.4 %shard_map.84 = (bf16[96,128]{1,0:T(8,128)(2,1)}, bf16[96,128]{1,0:T(8,128)(2,1)}) custom-call(bf16[16,96,128]{2,1,0:T(8,128)(2,1)} %reshape.213.sent_ref, bf16[96,128]{1,0:T(8,128)(2,1)} %get-tuple-element.28.current_ref), custom_call_target="tpu_custom_call" | custom-call | tf_op jit(solution)/shard_map/pallas_call | solution.py:117
  274.9 0.8 broadcast_in_dim.44
  275.7 0.6 bitcast_dynamic-update-slice_fusion
  (104 shorter events, 8.6 us)
Async XLA Ops:
  0.9 22.1 %copy-start.2 = (bf16[96,128]{1,0:T(8,128)(2,1)}, bf16[96,128]{1,0:T(8,128)(2,1)S(1)}, u32[]{:S(2)}) copy-start(bf16[96,128]{1,0:T(8,128)(2,1)S(1)} %squeeze.52.current_ref) | copy-start | bytes 73732
  15.8 2.0 collective-permute-start
  23.0 26.8 %copy-start.1 = (bf16[3,4,3072]{2,1,0:T(4,128)(2,1)S(1)}, bf16[3,4,3072]{2,1,0:T(4,128)(2,1)}, u32[]{:S(2)}) copy-start(bf16[3,4,3072]{2,1,0:T(4,128)(2,1)} %param.7) | copy-start | bytes 221188
  23.0 27.1 %copy-start = (f32[1,3072]{1,0:T(1,128)S(1)}, f32[1,3072]{1,0:T(1,128)}, u32[]{:S(2)}) copy-start(f32[1,3072]{1,0:T(1,128)} %param.8) | copy-start | bytes 36868
  29.7 2.4 collective-permute-start.1
  62.1 2.0 collective-permute-start.2
  75.9 2.4 collective-permute-start.3
  107.5 2.0 collective-permute-start.4
  121.4 2.4 collective-permute-start.5
  153.1 2.0 collective-permute-start.6
  166.9 31.5 %copy-start.3 = (bf16[96,128]{1,0:T(8,128)(2,1)S(1)}, bf16[96,128]{1,0:T(8,128)(2,1)}, u32[]{:S(2)}) copy-start(bf16[96,128]{1,0:T(8,128)(2,1)} %get-tuple-element.16) | copy-start | bytes 73732
  166.9 2.4 collective-permute-start.7
  197.9 2.2 collective-permute-start.8
  205.3 7.0 %copy-start.4 = (bf16[96,128]{1,0:T(8,128)(2,1)S(1)}, bf16[96,128]{1,0:T(8,128)(2,1)}, u32[]{:S(2)}) copy-start(bf16[96,128]{1,0:T(8,128)(2,1)} %get-tuple-element.18) | copy-start | bytes 73732
  205.3 7.1 %copy-start.5 = (bf16[96,128]{1,0:T(8,128)(2,1)S(1)}, bf16[96,128]{1,0:T(8,128)(2,1)}, u32[]{:S(2)}) copy-start(bf16[96,128]{1,0:T(8,128)(2,1)} %get-tuple-element.20) | copy-start | bytes 73732
  212.0 31.1 %copy-start.6 = (bf16[96,128]{1,0:T(8,128)(2,1)S(1)}, bf16[96,128]{1,0:T(8,128)(2,1)}, u32[]{:S(2)}) copy-start(bf16[96,128]{1,0:T(8,128)(2,1)} %get-tuple-element.22) | copy-start | bytes 73732
  212.0 2.4 collective-permute-start.9
  242.9 2.0 collective-permute-start.10
  250.1 7.0 %copy-start.7 = (bf16[96,128]{1,0:T(8,128)(2,1)S(1)}, bf16[96,128]{1,0:T(8,128)(2,1)}, u32[]{:S(2)}) copy-start(bf16[96,128]{1,0:T(8,128)(2,1)} %get-tuple-element.24) | copy-start | bytes 73732
  256.8 2.4 collective-permute-start.11

commit v5 on v4

--- a/solution.py
+++ b/solution.py
@@ -45,6 +45,81 @@
         in_specs=[pl.BlockSpec(memory_space=pl.ANY)],
         out_specs=pl.BlockSpec(memory_space=pl.ANY),
         scratch_shapes=[
+            pltpu.SemaphoreType.DMA((chips,)),
+            pltpu.SemaphoreType.DMA((chips,)),
+            pltpu.SemaphoreType.DMA(()),
+        ],
+        compiler_params=pltpu.CompilerParams(collective_id=collective_id, has_side_effects=True),
+    )(src)
+
+
+def gather_rows(src, chips, collective_id):
+    rows, width = src.shape
+
+    def kernel(src_ref, out_ref, send_sem, recv_sem, pass_send, pass_recv, local_sem):
+        me = lax.axis_index("fsdp")
+        section = lax.axis_index("section")
+        chip, core = me // 2, me % 2
+        partner = chip * 2 + 1 - core
+        barrier = pltpu.get_barrier_semaphore()
+        for j in range(1, chips):
+            peer = lax.rem(chip + j, chips)
+            pl.semaphore_signal(barrier, 1, device_id=(section, peer * 2 + core), device_id_type=MESH)
+        pl.semaphore_signal(barrier, 1, device_id=(section, partner), device_id_type=MESH)
+        pl.semaphore_wait(barrier, chips)
+        local = pltpu.make_async_copy(src_ref, out_ref.at[chip], local_sem)
+        local.start()
+        copies = []
+        for j in range(1, chips):
+            peer = lax.rem(chip + j, chips)
+            copy = pltpu.make_async_remote_copy(
+                src_ref=src_ref,
+                dst_ref=out_ref.at[chip],
+                send_sem=send_sem.at[j],
+                recv_sem=recv_sem.at[j],
+                device_id=(section, peer * 2 + core),
+                device_id_type=MESH,
+            )
+            copy.start()
+            copies.append(copy)
+        passes = []
+        own = pltpu.make_async_remote_copy(
+            src_ref=src_ref,
+            dst_ref=out_ref.at[chips + chip],
+            send_sem=pass_send.at[0],
+            recv_sem=pass_recv.at[0],
+            device_id=(section, partner),
+            device_id_type=MESH,
+        )
+        own.start()
+        passes.append(own)
+        for j in range(1, chips):
+            source = lax.rem(chip - j + chips, chips)
+            copies[j - 1].wait_recv()
+            onward = pltpu.make_async_remote_copy(
+                src_ref=out_ref.at[source],
+                dst_ref=out_ref.at[chips + source],
+                send_sem=pass_send.at[j],
+                recv_sem=pass_recv.at[j],
+                device_id=(section, partner),
+                device_id_type=MESH,
+            )
+            onward.start()
+            passes.append(onward)
+        local.wait()
+        for copy in copies:
+            copy.wait_send()
+        for onward in passes:
+            onward.wait()
+
+    return pl.pallas_call(
+        kernel,
+        out_shape=jax.ShapeDtypeStruct((2 * chips, rows, width), src.dtype),
+        in_specs=[pl.BlockSpec(memory_space=pl.ANY)],
+        out_specs=pl.BlockSpec(memory_space=pl.ANY),
+        scratch_shapes=[
+            pltpu.SemaphoreType.DMA((chips,)),
+            pltpu.SemaphoreType.DMA((chips,)),
             pltpu.SemaphoreType.DMA((chips,)),
             pltpu.SemaphoreType.DMA((chips,)),
             pltpu.SemaphoreType.DMA(()),
@@ -196,8 +271,7 @@
         current = entry if carried is None else jnp.where(section_index == 0, entry, carried)
         normed = rms_norm(current, gain_row)
         lanes = local * width // 128
-        near = exchange(normed.reshape(lanes, 128), chips, True, 0)
-        rows = jnp.concatenate([near, sibling(near, "fsdp")], axis=0).reshape(shards, local, width)
+        rows = gather_rows(normed.reshape(lanes, 128), chips, 0).reshape(shards, local, width)
         partial_value = expert_mix(rows, coef_now, gate_w, up_w, down_w)
         chip_sum = partial_value[:chips] + sibling(partial_value[chips:], "fsdp")
         sent = chip_sum.astype(jnp.bfloat16).reshape(chips, lanes, 128)

time: 278 us -> 282 us (1.014)
  Pallas kernels: 154 us -> 166 us
  waiting for transfers between devices: 21.7 us -> 10.5 us
  local copies, waits for them, and re-layouts: 15.7 us -> 25 us
  other arithmetic: 18.7 us -> 12.3 us
    pallas_call x6, Pallas kernels: 65.1 us -> 77.1 us  [gather_rows(): pl.pallas_call(kernel, out_shape=jax.ShapeDtypeStruct((2 * chips, rows, w...]
    ppermute x12 -> x6, waiting for transfers between devices: 21.7 us -> 10.5 us  [sibling(): return lax.ppermute(array, axis, [(i, i ^ 1) for i in range(devices)])]
    reshape x6, local copies, waits for them, and re-layouts: 1.07 us -> 10.5 us  [on_device(): gather_rows(normed.reshape(lanes, 128), chips, 0)]
    concatenate x6 -> x0, other arithmetic: 6.39 us -> none  [on_device(): jnp.concatenate([near, sibling(near, 'fsdp')], axis=0)]
  transfers between devices with their start and end apart: 12 -> 6, of which waited for: 12 -> 6; matrix products, arithmetic and copies ran while one was open for 1% -> 0% of each run, Pallas kernels for 0% -> 0%
where the time goes in v5:
time: 282 us; the launch traced here: 280 us
  Pallas kernels  166 us (59%)
  matrix products  63.2 us (22%)
  local copies, waits for them, and re-layouts  25 us (9%)
  other arithmetic  12.3 us (4%)
  waiting for transfers between devices  10.5 us (4%)
  starting transfers between devices  3.11 us (1%)
    pallas_call x6, Pallas kernels, reduce_relay(): pl.pallas_call(kernel, out_shape=(jax.ShapeDtypeStruct((rows, width), cur...  88.4 us
    pallas_call x6, Pallas kernels, gather_rows(): pl.pallas_call(kernel, out_shape=jax.ShapeDtypeStruct((2 * chips, rows, w...  77.1 us
    dot_general x6, matrix products, expert_mix(): jnp.einsum('efmh,ehd->fmd', gated, down_w, preferred_element_type=jnp.flo...  40.1 us
    dot_general x6, matrix products, expert_mix(): jnp.einsum('fmd,edh->efmh', rows, gate_w, preferred_element_type=jnp.floa...  23.1 us
    ppermute x6, waiting for transfers between devices, sibling(): return lax.ppermute(array, axis, [(i, i ^ 1) for i in range(devices)])  10.5 us
    reshape x6, local copies, waits for them, and re-layouts, on_device(): gather_rows(normed.reshape(lanes, 128), chips, 0)  10.5 us
    convert_element_type x6, other arithmetic, rms_norm(): return (values * scale * gain_row[None, :]).astype(jnp.bfloat16)  8.56 us
  transfers between devices with their start and end apart: 6, of which 6 were waited for; matrix products, arithmetic and copies ran while one was open for 0% of the time, Pallas kernels for 0%

profile of v5, /device:TPU:24, one launch (start us, length us, event | category | flops | bytes accessed | tf_op | source)
XLA Modules:
  0.0 280.3 jit_solution(14489721450064680980)
XLA Ops:
  0.0 0.7 select_reduce_fusion
  1.6 0.9 multiply_reduce_fusion.5
  2.7 1.4 fusion.222.src_ref
  4.1 15.1 %shard_map.73 = bf16[32,96,128]{2,1,0:T(8,128)(2,1)} custom-call(bf16[96,128]{1,0:T(8,128)(2,1)} %fusion.222.src_ref), custom_call_target="tpu_custom_call" | custom-call | tf_op jit(solution)/shard_map/pallas_call | solution.py:115
  19.1 1.7 reshape.195
  20.9 3.9 %fusion.54 = f32[4,32,4,256]{3,1,0,2:T(8,128)S(1)} fusion(bf16[1,4,3072,256]{3,2,1,0:T(8,128)(2,1)} %param.9, bf16[32,4,3072,1]{2,1,0,3:T(4,128)(2,1)S(1)} %bitcast.292), kind=kOutput, calls=%fused_computation.42 | convolution fusion | flops 805306368 | bytes 7602176 | tf_op jit(solution)/shard_map/fmd,edh->efmh/dot_general | solution.py:238
  24.8 6.7 %fusion.36 = f32[32,4,3072]{2,0,1:T(8,128)S(1)} fusion(bf16[1,4,256,3072]{3,2,1,0:T(8,128)(2,1)} %param.11, bf16[1,4,3072,256]{3,2,1,0:T(8,128)(2,1)} %param.10, bf16[32,4,3072,1]{2,1,0,3:T(4,128)(2,1)S(1)} %bitcast.293, f32[4,32,4,256]{3,1,0,2:T(8,128)S(1)} %fusion.54, f32[4,32,4]{1,0,2:T(4,128)S(1)} %copy.120), kind=kOutput, calls=%fused_computation.36 | convolution fusion | flops 1611530240 | bytes 15468544 | tf_op jit(solution)/shard_map/efmh,ehd->fmd/dot_general | solution.py:241
  31.6 0.5 collective-permute-start
  32.0 1.9 collective-permute-done
  34.3 0.9 reshape.198.sent_ref
  35.2 15.4 %shard_map.74 = (bf16[96,128]{1,0:T(8,128)(2,1)}, bf16[96,128]{1,0:T(8,128)(2,1)}) custom-call(bf16[16,96,128]{2,1,0:T(8,128)(2,1)} %reshape.198.sent_ref, bf16[96,128]{1,0:T(8,128)(2,1)} %copy-done.2), custom_call_target="tpu_custom_call" | custom-call | tf_op jit(solution)/shard_map/pallas_call | solution.py:192
  50.6 0.8 reshape.199
  51.7 1.4 fusion.223
  53.1 12.5 %shard_map.75 = bf16[32,96,128]{2,1,0:T(8,128)(2,1)} custom-call(bf16[96,128]{1,0:T(8,128)(2,1)} %get-tuple-element.43.src_ref), custom_call_target="tpu_custom_call" | custom-call | tf_op jit(solution)/shard_map/pallas_call | solution.py:115
  65.6 1.7 reshape.200
  67.4 3.9 %fusion.57 = f32[4,32,4,256]{3,1,0,2:T(8,128)S(1)} fusion(bf16[1,4,3072,256]{3,2,1,0:T(8,128)(2,1)} %param.9, bf16[32,4,3072,1]{2,1,0,3:T(4,128)(2,1)S(1)} %bitcast.294), kind=kOutput, calls=%fused_computation.43 | convolution fusion | flops 805306368 | bytes 7602176 | tf_op jit(solution)/shard_map/fmd,edh->efmh/dot_general | solution.py:238
  71.3 6.7 %fusion.39 = f32[32,4,3072]{2,0,1:T(8,128)S(1)} fusion(bf16[1,4,256,3072]{3,2,1,0:T(8,128)(2,1)} %param.11, bf16[1,4,3072,256]{3,2,1,0:T(8,128)(2,1)} %param.10, bf16[32,4,3072,1]{2,1,0,3:T(4,128)(2,1)S(1)} %bitcast.295, f32[4,32,4,256]{3,1,0,2:T(8,128)S(1)} %fusion.57, f32[4,32,4]{1,0,2:T(4,128)S(1)} %copy.124), kind=kOutput, calls=%fused_computation.37 | convolution fusion | flops 1611530240 | bytes 15468544 | tf_op jit(solution)/shard_map/efmh,ehd->fmd/dot_general | solution.py:241
  78.0 0.6 collective-permute-start.1
  78.6 1.9 collective-permute-done.1
  80.9 0.9 reshape.201.sent_ref
  81.8 15.1 %shard_map.76 = (bf16[96,128]{1,0:T(8,128)(2,1)}, bf16[96,128]{1,0:T(8,128)(2,1)}) custom-call(bf16[16,96,128]{2,1,0:T(8,128)(2,1)} %reshape.201.sent_ref, bf16[96,128]{1,0:T(8,128)(2,1)} %get-tuple-element.44.current_ref), custom_call_target="tpu_custom_call" | custom-call | tf_op jit(solution)/shard_map/pallas_call | solution.py:192
  96.9 0.8 reshape.202
  98.0 1.4 fusion.224
  99.4 12.3 %shard_map.77 = bf16[32,96,128]{2,1,0:T(8,128)(2,1)} custom-call(bf16[96,128]{1,0:T(8,128)(2,1)} %get-tuple-element.39.src_ref), custom_call_target="tpu_custom_call" | custom-call | tf_op jit(solution)/shard_map/pallas_call | solution.py:115
  111.7 1.7 reshape.203
  113.5 3.9 %fusion.60 = f32[4,32,4,256]{3,1,0,2:T(8,128)S(1)} fusion(bf16[1,4,3072,256]{3,2,1,0:T(8,128)(2,1)} %param.9, bf16[32,4,3072,1]{2,1,0,3:T(4,128)(2,1)S(1)} %bitcast.296), kind=kOutput, calls=%fused_computation.44 | convolution fusion | flops 805306368 | bytes 7602176 | tf_op jit(solution)/shard_map/fmd,edh->efmh/dot_general | solution.py:238
  117.3 6.7 %fusion.42 = f32[32,4,3072]{2,0,1:T(8,128)S(1)} fusion(bf16[1,4,256,3072]{3,2,1,0:T(8,128)(2,1)} %param.11, bf16[1,4,3072,256]{3,2,1,0:T(8,128)(2,1)} %param.10, bf16[32,4,3072,1]{2,1,0,3:T(4,128)(2,1)S(1)} %bitcast.297, f32[4,32,4,256]{3,1,0,2:T(8,128)S(1)} %fusion.60, f32[4,32,4]{1,0,2:T(4,128)S(1)} %copy.128), kind=kOutput, calls=%fused_computation.38 | convolution fusion | flops 1611530240 | bytes 15468544 | tf_op jit(solution)/shard_map/efmh,ehd->fmd/dot_general | solution.py:241
  124.0 0.5 collective-permute-start.2
  124.5 1.9 collective-permute-done.2
  126.8 0.9 reshape.204.sent_ref
  127.7 14.9 %shard_map.78 = (bf16[96,128]{1,0:T(8,128)(2,1)}, bf16[96,128]{1,0:T(8,128)(2,1)}) custom-call(bf16[16,96,128]{2,1,0:T(8,128)(2,1)} %reshape.204.sent_ref, bf16[96,128]{1,0:T(8,128)(2,1)} %get-tuple-element.40.current_ref), custom_call_target="tpu_custom_call" | custom-call | tf_op jit(solution)/shard_map/pallas_call | solution.py:192
  142.6 0.8 reshape.205
  143.7 1.4 fusion.225
  145.1 12.3 %shard_map.79 = bf16[32,96,128]{2,1,0:T(8,128)(2,1)} custom-call(bf16[96,128]{1,0:T(8,128)(2,1)} %get-tuple-element.35.src_ref), custom_call_target="tpu_custom_call" | custom-call | tf_op jit(solution)/shard_map/pallas_call | solution.py:115
  157.5 1.7 reshape.206
  159.2 3.9 %fusion.63 = f32[4,32,4,256]{3,1,0,2:T(8,128)S(1)} fusion(bf16[1,4,3072,256]{3,2,1,0:T(8,128)(2,1)} %param.9, bf16[32,4,3072,1]{2,1,0,3:T(4,128)(2,1)S(1)} %bitcast.298), kind=kOutput, calls=%fused_computation.45 | convolution fusion | flops 805306368 | bytes 7602176 | tf_op jit(solution)/shard_map/fmd,edh->efmh/dot_general | solution.py:238
  163.1 6.7 %fusion.45 = f32[32,4,3072]{2,0,1:T(8,128)S(1)} fusion(bf16[1,4,256,3072]{3,2,1,0:T(8,128)(2,1)} %param.11, bf16[1,4,3072,256]{3,2,1,0:T(8,128)(2,1)} %param.10, bf16[32,4,3072,1]{2,1,0,3:T(4,128)(2,1)S(1)} %bitcast.299, f32[4,32,4,256]{3,1,0,2:T(8,128)S(1)} %fusion.63, f32[4,32,4]{1,0,2:T(4,128)S(1)} %copy.132), kind=kOutput, calls=%fused_computation.39 | convolution fusion | flops 1611530240 | bytes 15468544 | tf_op jit(solution)/shard_map/efmh,ehd->fmd/dot_general | solution.py:241
  169.8 0.7 collective-permute-start.3
  170.6 1.8 collective-permute-done.3
  172.8 0.9 reshape.207.sent_ref
  173.7 14.6 %shard_map.80 = (bf16[96,128]{1,0:T(8,128)(2,1)}, bf16[96,128]{1,0:T(8,128)(2,1)}) custom-call(bf16[16,96,128]{2,1,0:T(8,128)(2,1)} %reshape.207.sent_ref, bf16[96,128]{1,0:T(8,128)(2,1)} %get-tuple-element.36.current_ref), custom_call_target="tpu_custom_call" | custom-call | tf_op jit(solution)/shard_map/pallas_call | solution.py:192
  188.3 0.8 reshape.208
  189.4 1.4 fusion.226
  190.9 12.5 %shard_map.81 = bf16[32,96,128]{2,1,0:T(8,128)(2,1)} custom-call(bf16[96,128]{1,0:T(8,128)(2,1)} %get-tuple-element.31.src_ref), custom_call_target="tpu_custom_call" | custom-call | tf_op jit(solution)/shard_map/pallas_call | solution.py:115
  203.4 1.7 reshape.209
  205.1 3.9 %fusion.66 = f32[4,32,4,256]{3,1,0,2:T(8,128)S(1)} fusion(bf16[1,4,3072,256]{3,2,1,0:T(8,128)(2,1)} %param.9, bf16[32,4,3072,1]{2,1,0,3:T(4,128)(2,1)S(1)} %bitcast.300), kind=kOutput, calls=%fused_computation.46 | convolution fusion | flops 805306368 | bytes 7602176 | tf_op jit(solution)/shard_map/fmd,edh->efmh/dot_general | solution.py:238
  209.0 6.7 %fusion.48 = f32[32,4,3072]{2,0,1:T(8,128)S(1)} fusion(bf16[1,4,256,3072]{3,2,1,0:T(8,128)(2,1)} %param.11, bf16[1,4,3072,256]{3,2,1,0:T(8,128)(2,1)} %param.10, bf16[32,4,3072,1]{2,1,0,3:T(4,128)(2,1)S(1)} %bitcast.301, f32[4,32,4,256]{3,1,0,2:T(8,128)S(1)} %fusion.66, f32[4,32,4]{1,0,2:T(4,128)S(1)} %copy.136), kind=kOutput, calls=%fused_computation.40 | convolution fusion | flops 1611530240 | bytes 15468544 | tf_op jit(solution)/shard_map/efmh,ehd->fmd/dot_general | solution.py:241
  215.8 0.5 collective-permute-start.4
  216.4 1.8 collective-permute-done.4
  218.6 0.9 reshape.210.sent_ref
  219.5 14.2 %shard_map.82 = (bf16[96,128]{1,0:T(8,128)(2,1)}, bf16[96,128]{1,0:T(8,128)(2,1)}) custom-call(bf16[16,96,128]{2,1,0:T(8,128)(2,1)} %reshape.210.sent_ref, bf16[96,128]{1,0:T(8,128)(2,1)} %get-tuple-element.32.current_ref), custom_call_target="tpu_custom_call" | custom-call | tf_op jit(solution)/shard_map/pallas_call | solution.py:192
  233.7 0.8 reshape.211
  234.8 1.4 fusion.227
  236.2 12.4 %shard_map.83 = bf16[32,96,128]{2,1,0:T(8,128)(2,1)} custom-call(bf16[96,128]{1,0:T(8,128)(2,1)} %get-tuple-element.27.src_ref), custom_call_target="tpu_custom_call" | custom-call | tf_op jit(solution)/shard_map/pallas_call | solution.py:115
  248.6 1.7 reshape.212
  250.4 3.9 %fusion.69 = f32[4,32,4,256]{3,1,0,2:T(8,128)S(1)} fusion(bf16[1,4,3072,256]{3,2,1,0:T(8,128)(2,1)} %param.9, bf16[32,4,3072,1]{2,1,0,3:T(4,128)(2,1)S(1)} %bitcast.302), kind=kOutput, calls=%fused_computation.47 | convolution fusion | flops 805306368 | bytes 7602176 | tf_op jit(solution)/shard_map/fmd,edh->efmh/dot_general | solution.py:238
  254.3 6.7 %fusion.51 = f32[32,4,3072]{2,0,1:T(8,128)S(1)} fusion(bf16[1,4,256,3072]{3,2,1,0:T(8,128)(2,1)} %param.11, bf16[1,4,3072,256]{3,2,1,0:T(8,128)(2,1)} %param.10, bf16[32,4,3072,1]{2,1,0,3:T(4,128)(2,1)S(1)} %bitcast.303, f32[4,32,4,256]{3,1,0,2:T(8,128)S(1)} %fusion.69, f32[4,32,4]{1,0,2:T(4,128)S(1)} %copy.140), kind=kOutput, calls=%fused_computation.41 | convolution fusion | flops 1611530240 | bytes 15468544 | tf_op jit(solution)/shard_map/efmh,ehd->fmd/dot_general | solution.py:241
  261.0 0.5 collective-permute-start.5
  261.6 0.6 copy.219
  262.2 1.2 collective-permute-done.5
  263.8 0.9 reshape.213.sent_ref
  264.7 14.2 %shard_map.84 = (bf16[96,128]{1,0:T(8,128)(2,1)}, bf16[96,128]{1,0:T(8,128)(2,1)}) custom-call(bf16[16,96,128]{2,1,0:T(8,128)(2,1)} %reshape.213.sent_ref, bf16[96,128]{1,0:T(8,128)(2,1)} %get-tuple-element.28.current_ref), custom_call_target="tpu_custom_call" | custom-call | tf_op jit(solution)/shard_map/pallas_call | solution.py:192
  278.9 0.8 broadcast_in_dim.44
  279.7 0.6 bitcast_dynamic-update-slice_fusion
  (86 shorter events, 5.6 us)
Async XLA Ops:
  2.5 22.3 %copy-start.2 = (bf16[96,128]{1,0:T(8,128)(2,1)}, bf16[96,128]{1,0:T(8,128)(2,1)S(1)}, u32[]{:S(2)}) copy-start(bf16[96,128]{1,0:T(8,128)(2,1)S(1)} %squeeze.52.current_ref) | copy-start | bytes 73732
  24.8 26.6 %copy-start.1 = (bf16[3,4,3072]{2,1,0:T(4,128)(2,1)S(1)}, bf16[3,4,3072]{2,1,0:T(4,128)(2,1)}, u32[]{:S(2)}) copy-start(bf16[3,4,3072]{2,1,0:T(4,128)(2,1)} %param.7) | copy-start | bytes 221188
  24.8 26.9 %copy-start = (f32[1,3072]{1,0:T(1,128)S(1)}, f32[1,3072]{1,0:T(1,128)}, u32[]{:S(2)}) copy-start(f32[1,3072]{1,0:T(1,128)} %param.8) | copy-start | bytes 36868
  31.6 2.4 collective-permute-start
  78.0 2.5 collective-permute-start.1
  124.0 2.4 collective-permute-start.2
  163.1 7.4 %copy-start.3 = (bf16[96,128]{1,0:T(8,128)(2,1)S(1)}, bf16[96,128]{1,0:T(8,128)(2,1)}, u32[]{:S(2)}) copy-start(bf16[96,128]{1,0:T(8,128)(2,1)} %get-tuple-element.16) | copy-start | bytes 73732
  163.1 7.5 %copy-start.5 = (bf16[96,128]{1,0:T(8,128)(2,1)S(1)}, bf16[96,128]{1,0:T(8,128)(2,1)}, u32[]{:S(2)}) copy-start(bf16[96,128]{1,0:T(8,128)(2,1)} %get-tuple-element.18) | copy-start | bytes 73732
  169.8 2.6 collective-permute-start.3
  209.0 7.3 %copy-start.4 = (bf16[96,128]{1,0:T(8,128)(2,1)S(1)}, bf16[96,128]{1,0:T(8,128)(2,1)}, u32[]{:S(2)}) copy-start(bf16[96,128]{1,0:T(8,128)(2,1)} %get-tuple-element.20) | copy-start | bytes 73732
  209.0 7.3 %copy-start.6 = (bf16[96,128]{1,0:T(8,128)(2,1)S(1)}, bf16[96,128]{1,0:T(8,128)(2,1)}, u32[]{:S(2)}) copy-start(bf16[96,128]{1,0:T(8,128)(2,1)} %get-tuple-element.22) | copy-start | bytes 73732
  215.8 2.4 collective-permute-start.4
  254.2 7.3 %copy-start.7 = (bf16[96,128]{1,0:T(8,128)(2,1)S(1)}, bf16[96,128]{1,0:T(8,128)(2,1)}, u32[]{:S(2)}) copy-start(bf16[96,128]{1,0:T(8,128)(2,1)} %get-tuple-element.24) | copy-start | bytes 73732
  261.0 2.4 collective-permute-start.5

commit v6 on v4

--- a/solution.py
+++ b/solution.py
@@ -199,7 +199,8 @@
         near = exchange(normed.reshape(lanes, 128), chips, True, 0)
         rows = jnp.concatenate([near, sibling(near, "fsdp")], axis=0).reshape(shards, local, width)
         partial_value = expert_mix(rows, coef_now, gate_w, up_w, down_w)
-        chip_sum = partial_value[:chips] + sibling(partial_value[chips:], "fsdp")
+        far_sum = sibling(partial_value[chips:].astype(jnp.bfloat16), "fsdp")
+        chip_sum = partial_value[:chips] + far_sum.astype(jnp.float32)
         sent = chip_sum.astype(jnp.bfloat16).reshape(chips, lanes, 128)
         result, carried = reduce_relay(sent, current.reshape(lanes, 128), chips, sections, 1)
         result = result.reshape(local, width)

time: 278 us -> 275 us (0.989)
  waiting for transfers between devices: 21.7 us -> 17.6 us
    ppermute x12, waiting for transfers between devices: 21.7 us -> 17.6 us  [sibling(): return lax.ppermute(array, axis, [(i, i ^ 1) for i in range(devices)])]
where the time goes in v6:
time: 275 us; the launch traced here: 273 us
  Pallas kernels  154 us (56%)
  matrix products  63.2 us (23%)
  other arithmetic  18.6 us (7%)
  waiting for transfers between devices  17.6 us (6%)
  local copies, waits for them, and re-layouts  16.3 us (6%)
    pallas_call x6, Pallas kernels, reduce_relay(): pl.pallas_call(kernel, out_shape=(jax.ShapeDtypeStruct((rows, width), cur...  89.1 us
    pallas_call x6, Pallas kernels, exchange(): pl.pallas_call(kernel, out_shape=jax.ShapeDtypeStruct((chips, rows, width...  65.2 us
    dot_general x6, matrix products, expert_mix(): jnp.einsum('efmh,ehd->fmd', gated, down_w, preferred_element_type=jnp.flo...  40.1 us
    dot_general x6, matrix products, expert_mix(): jnp.einsum('fmd,edh->efmh', rows, gate_w, preferred_element_type=jnp.floa...  23.1 us
    ppermute x12, waiting for transfers between devices, sibling(): return lax.ppermute(array, axis, [(i, i ^ 1) for i in range(devices)])  17.6 us
    convert_element_type x6, other arithmetic, rms_norm(): return (values * scale * gain_row[None, :]).astype(jnp.bfloat16)  8.56 us
    concatenate x6, other arithmetic, on_device(): jnp.concatenate([near, sibling(near, 'fsdp')], axis=0)  6.39 us
  transfers between devices with their start and end apart: 12, of which 12 were waited for; matrix products, arithmetic and copies ran while one was open for 1% of the time, Pallas kernels for 0%

profile of v6, /device:TPU:24, one launch (start us, length us, event | category | flops | bytes accessed | tf_op | source)
XLA Modules:
  0.0 272.9 jit_solution(10587191871335943182)
XLA Ops:
  0.0 0.9 multiply_reduce_fusion.5
  1.1 1.4 fusion.222.src_ref
  2.5 13.3 %shard_map.73 = bf16[16,96,128]{2,1,0:T(8,128)(2,1)} custom-call(bf16[96,128]{1,0:T(8,128)(2,1)} %fusion.222.src_ref), custom_call_target="tpu_custom_call" | custom-call | tf_op jit(solution)/shard_map/pallas_call | solution.py:42
  15.9 0.7 select_reduce_fusion
  17.8 1.1 pad_maximum_fusion
  19.1 3.9 %fusion.54 = f32[4,32,4,256]{3,1,0,2:T(8,128)S(1)} fusion(bf16[1,4,3072,256]{3,2,1,0:T(8,128)(2,1)} %param.9, bf16[32,4,3072,1]{2,1,0,3:T(4,128)(2,1)S(1)} %bitcast.292), kind=kOutput, calls=%fused_computation.42 | convolution fusion | flops 805306368 | bytes 7602176 | tf_op jit(solution)/shard_map/fmd,edh->efmh/dot_general | solution.py:163
  23.0 6.7 %fusion.36 = f32[32,4,3072]{2,0,1:T(8,128)S(1)} fusion(bf16[1,4,256,3072]{3,2,1,0:T(8,128)(2,1)} %param.11, bf16[1,4,3072,256]{3,2,1,0:T(8,128)(2,1)} %param.10, bf16[32,4,3072,1]{2,1,0,3:T(4,128)(2,1)S(1)} %bitcast.293, f32[4,32,4,256]{3,1,0,2:T(8,128)S(1)} %fusion.54, f32[4,32,4]{1,0,2:T(4,128)S(1)} %copy.120), kind=kOutput, calls=%fused_computation.36 | convolution fusion | flops 1611530240 | bytes 15468544 | tf_op jit(solution)/shard_map/efmh,ehd->fmd/dot_general | solution.py:166
  30.0 1.6 collective-permute-done.1
  31.9 0.9 reshape.198.sent_ref
  32.8 15.6 %shard_map.74 = (bf16[96,128]{1,0:T(8,128)(2,1)}, bf16[96,128]{1,0:T(8,128)(2,1)}) custom-call(bf16[16,96,128]{2,1,0:T(8,128)(2,1)} %reshape.198.sent_ref, bf16[96,128]{1,0:T(8,128)(2,1)} %copy-done.2), custom_call_target="tpu_custom_call" | custom-call | tf_op jit(solution)/shard_map/pallas_call | solution.py:117
  48.4 0.8 reshape.199
  49.5 1.4 fusion.223
  50.9 10.6 %shard_map.75 = bf16[16,96,128]{2,1,0:T(8,128)(2,1)} custom-call(bf16[96,128]{1,0:T(8,128)(2,1)} %get-tuple-element.43.src_ref), custom_call_target="tpu_custom_call" | custom-call | tf_op jit(solution)/shard_map/pallas_call | solution.py:42
  61.6 1.9 collective-permute-done.2
  63.5 1.1 pad_maximum_fusion.1
  64.8 3.9 %fusion.57 = f32[4,32,4,256]{3,1,0,2:T(8,128)S(1)} fusion(bf16[1,4,3072,256]{3,2,1,0:T(8,128)(2,1)} %param.9, bf16[32,4,3072,1]{2,1,0,3:T(4,128)(2,1)S(1)} %bitcast.294), kind=kOutput, calls=%fused_computation.43 | convolution fusion | flops 805306368 | bytes 7602176 | tf_op jit(solution)/shard_map/fmd,edh->efmh/dot_general | solution.py:163
  68.6 6.7 %fusion.39 = f32[32,4,3072]{2,0,1:T(8,128)S(1)} fusion(bf16[1,4,256,3072]{3,2,1,0:T(8,128)(2,1)} %param.11, bf16[1,4,3072,256]{3,2,1,0:T(8,128)(2,1)} %param.10, bf16[32,4,3072,1]{2,1,0,3:T(4,128)(2,1)S(1)} %bitcast.295, f32[4,32,4,256]{3,1,0,2:T(8,128)S(1)} %fusion.57, f32[4,32,4]{1,0,2:T(4,128)S(1)} %copy.124), kind=kOutput, calls=%fused_computation.37 | convolution fusion | flops 1611530240 | bytes 15468544 | tf_op jit(solution)/shard_map/efmh,ehd->fmd/dot_general | solution.py:166
  75.6 1.6 collective-permute-done.3
  77.6 0.9 reshape.201.sent_ref
  78.5 15.1 %shard_map.76 = (bf16[96,128]{1,0:T(8,128)(2,1)}, bf16[96,128]{1,0:T(8,128)(2,1)}) custom-call(bf16[16,96,128]{2,1,0:T(8,128)(2,1)} %reshape.201.sent_ref, bf16[96,128]{1,0:T(8,128)(2,1)} %get-tuple-element.44.current_ref), custom_call_target="tpu_custom_call" | custom-call | tf_op jit(solution)/shard_map/pallas_call | solution.py:117
  93.6 0.8 reshape.202
  94.7 1.4 fusion.224
  96.1 10.3 %shard_map.77 = bf16[16,96,128]{2,1,0:T(8,128)(2,1)} custom-call(bf16[96,128]{1,0:T(8,128)(2,1)} %get-tuple-element.39.src_ref), custom_call_target="tpu_custom_call" | custom-call | tf_op jit(solution)/shard_map/pallas_call | solution.py:42
  106.5 1.9 collective-permute-done.4
  108.4 1.1 pad_maximum_fusion.2
  109.6 3.9 %fusion.60 = f32[4,32,4,256]{3,1,0,2:T(8,128)S(1)} fusion(bf16[1,4,3072,256]{3,2,1,0:T(8,128)(2,1)} %param.9, bf16[32,4,3072,1]{2,1,0,3:T(4,128)(2,1)S(1)} %bitcast.296), kind=kOutput, calls=%fused_computation.44 | convolution fusion | flops 805306368 | bytes 7602176 | tf_op jit(solution)/shard_map/fmd,edh->efmh/dot_general | solution.py:163
  113.5 6.7 %fusion.42 = f32[32,4,3072]{2,0,1:T(8,128)S(1)} fusion(bf16[1,4,256,3072]{3,2,1,0:T(8,128)(2,1)} %param.11, bf16[1,4,3072,256]{3,2,1,0:T(8,128)(2,1)} %param.10, bf16[32,4,3072,1]{2,1,0,3:T(4,128)(2,1)S(1)} %bitcast.297, f32[4,32,4,256]{3,1,0,2:T(8,128)S(1)} %fusion.60, f32[4,32,4]{1,0,2:T(4,128)S(1)} %copy.128), kind=kOutput, calls=%fused_computation.38 | convolution fusion | flops 1611530240 | bytes 15468544 | tf_op jit(solution)/shard_map/efmh,ehd->fmd/dot_general | solution.py:166
  120.5 1.6 collective-permute-done.5
  122.4 0.9 reshape.204.sent_ref
  123.3 15.1 %shard_map.78 = (bf16[96,128]{1,0:T(8,128)(2,1)}, bf16[96,128]{1,0:T(8,128)(2,1)}) custom-call(bf16[16,96,128]{2,1,0:T(8,128)(2,1)} %reshape.204.sent_ref, bf16[96,128]{1,0:T(8,128)(2,1)} %get-tuple-element.40.current_ref), custom_call_target="tpu_custom_call" | custom-call | tf_op jit(solution)/shard_map/pallas_call | solution.py:117
  138.4 0.8 reshape.205
  139.5 1.4 fusion.225
  140.9 10.4 %shard_map.79 = bf16[16,96,128]{2,1,0:T(8,128)(2,1)} custom-call(bf16[96,128]{1,0:T(8,128)(2,1)} %get-tuple-element.35.src_ref), custom_call_target="tpu_custom_call" | custom-call | tf_op jit(solution)/shard_map/pallas_call | solution.py:42
  151.5 1.8 collective-permute-done.6
  153.3 1.1 pad_maximum_fusion.3
  154.6 3.9 %fusion.63 = f32[4,32,4,256]{3,1,0,2:T(8,128)S(1)} fusion(bf16[1,4,3072,256]{3,2,1,0:T(8,128)(2,1)} %param.9, bf16[32,4,3072,1]{2,1,0,3:T(4,128)(2,1)S(1)} %bitcast.298), kind=kOutput, calls=%fused_computation.45 | convolution fusion | flops 805306368 | bytes 7602176 | tf_op jit(solution)/shard_map/fmd,edh->efmh/dot_general | solution.py:163
  158.5 6.7 %fusion.45 = f32[32,4,3072]{2,0,1:T(8,128)S(1)} fusion(bf16[1,4,256,3072]{3,2,1,0:T(8,128)(2,1)} %param.11, bf16[1,4,3072,256]{3,2,1,0:T(8,128)(2,1)} %param.10, bf16[32,4,3072,1]{2,1,0,3:T(4,128)(2,1)S(1)} %bitcast.299, f32[4,32,4,256]{3,1,0,2:T(8,128)S(1)} %fusion.63, f32[4,32,4]{1,0,2:T(4,128)S(1)} %copy.132), kind=kOutput, calls=%fused_computation.39 | convolution fusion | flops 1611530240 | bytes 15468544 | tf_op jit(solution)/shard_map/efmh,ehd->fmd/dot_general | solution.py:166
  165.6 1.5 collective-permute-done.7
  167.4 0.9 reshape.207.sent_ref
  168.3 14.5 %shard_map.80 = (bf16[96,128]{1,0:T(8,128)(2,1)}, bf16[96,128]{1,0:T(8,128)(2,1)}) custom-call(bf16[16,96,128]{2,1,0:T(8,128)(2,1)} %reshape.207.sent_ref, bf16[96,128]{1,0:T(8,128)(2,1)} %get-tuple-element.36.current_ref), custom_call_target="tpu_custom_call" | custom-call | tf_op jit(solution)/shard_map/pallas_call | solution.py:117
  182.8 0.8 reshape.208
  183.9 1.4 fusion.226
  185.4 10.3 %shard_map.81 = bf16[16,96,128]{2,1,0:T(8,128)(2,1)} custom-call(bf16[96,128]{1,0:T(8,128)(2,1)} %get-tuple-element.31.src_ref), custom_call_target="tpu_custom_call" | custom-call | tf_op jit(solution)/shard_map/pallas_call | solution.py:42
  196.0 1.9 collective-permute-done.8
  197.9 1.1 pad_maximum_fusion.4
  199.1 3.9 %fusion.66 = f32[4,32,4,256]{3,1,0,2:T(8,128)S(1)} fusion(bf16[1,4,3072,256]{3,2,1,0:T(8,128)(2,1)} %param.9, bf16[32,4,3072,1]{2,1,0,3:T(4,128)(2,1)S(1)} %bitcast.300), kind=kOutput, calls=%fused_computation.46 | convolution fusion | flops 805306368 | bytes 7602176 | tf_op jit(solution)/shard_map/fmd,edh->efmh/dot_general | solution.py:163
  203.0 6.7 %fusion.48 = f32[32,4,3072]{2,0,1:T(8,128)S(1)} fusion(bf16[1,4,256,3072]{3,2,1,0:T(8,128)(2,1)} %param.11, bf16[1,4,3072,256]{3,2,1,0:T(8,128)(2,1)} %param.10, bf16[32,4,3072,1]{2,1,0,3:T(4,128)(2,1)S(1)} %bitcast.301, f32[4,32,4,256]{3,1,0,2:T(8,128)S(1)} %fusion.66, f32[4,32,4]{1,0,2:T(4,128)S(1)} %copy.136), kind=kOutput, calls=%fused_computation.40 | convolution fusion | flops 1611530240 | bytes 15468544 | tf_op jit(solution)/shard_map/efmh,ehd->fmd/dot_general | solution.py:166
  210.0 1.5 collective-permute-done.9
  211.9 0.9 reshape.210.sent_ref
  212.8 14.4 %shard_map.82 = (bf16[96,128]{1,0:T(8,128)(2,1)}, bf16[96,128]{1,0:T(8,128)(2,1)}) custom-call(bf16[16,96,128]{2,1,0:T(8,128)(2,1)} %reshape.210.sent_ref, bf16[96,128]{1,0:T(8,128)(2,1)} %get-tuple-element.32.current_ref), custom_call_target="tpu_custom_call" | custom-call | tf_op jit(solution)/shard_map/pallas_call | solution.py:117
  227.2 0.8 reshape.211
  228.3 1.4 fusion.227
  229.8 10.3 %shard_map.83 = bf16[16,96,128]{2,1,0:T(8,128)(2,1)} custom-call(bf16[96,128]{1,0:T(8,128)(2,1)} %get-tuple-element.27.src_ref), custom_call_target="tpu_custom_call" | custom-call | tf_op jit(solution)/shard_map/pallas_call | solution.py:42
  240.2 0.8 broadcast_in_dim.42
  240.9 1.1 collective-permute-done.10
  242.1 1.1 pad_maximum_fusion.5
  243.3 3.9 %fusion.69 = f32[4,32,4,256]{3,1,0,2:T(8,128)S(1)} fusion(bf16[1,4,3072,256]{3,2,1,0:T(8,128)(2,1)} %param.9, bf16[32,4,3072,1]{2,1,0,3:T(4,128)(2,1)S(1)} %bitcast.302), kind=kOutput, calls=%fused_computation.47 | convolution fusion | flops 805306368 | bytes 7602176 | tf_op jit(solution)/shard_map/fmd,edh->efmh/dot_general | solution.py:163
  247.2 6.7 %fusion.51 = f32[32,4,3072]{2,0,1:T(8,128)S(1)} fusion(bf16[1,4,256,3072]{3,2,1,0:T(8,128)(2,1)} %param.11, bf16[1,4,3072,256]{3,2,1,0:T(8,128)(2,1)} %param.10, bf16[32,4,3072,1]{2,1,0,3:T(4,128)(2,1)S(1)} %bitcast.303, f32[4,32,4,256]{3,1,0,2:T(8,128)S(1)} %fusion.69, f32[4,32,4]{1,0,2:T(4,128)S(1)} %copy.140), kind=kOutput, calls=%fused_computation.41 | convolution fusion | flops 1611530240 | bytes 15468544 | tf_op jit(solution)/shard_map/efmh,ehd->fmd/dot_general | solution.py:166
  254.2 0.6 copy.219
  254.8 0.9 collective-permute-done.11
  256.1 0.9 reshape.213.sent_ref
  257.0 14.4 %shard_map.84 = (bf16[96,128]{1,0:T(8,128)(2,1)}, bf16[96,128]{1,0:T(8,128)(2,1)}) custom-call(bf16[16,96,128]{2,1,0:T(8,128)(2,1)} %reshape.213.sent_ref, bf16[96,128]{1,0:T(8,128)(2,1)} %get-tuple-element.28.current_ref), custom_call_target="tpu_custom_call" | custom-call | tf_op jit(solution)/shard_map/pallas_call | solution.py:117
  271.5 0.8 broadcast_in_dim.44
  272.2 0.6 bitcast_dynamic-update-slice_fusion
  (102 shorter events, 8.8 us)
Async XLA Ops:
  0.9 22.1 %copy-start.2 = (bf16[96,128]{1,0:T(8,128)(2,1)}, bf16[96,128]{1,0:T(8,128)(2,1)S(1)}, u32[]{:S(2)}) copy-start(bf16[96,128]{1,0:T(8,128)(2,1)S(1)} %squeeze.52.current_ref) | copy-start | bytes 73732
  15.8 2.0 collective-permute-start
  23.0 26.2 %copy-start.1 = (bf16[3,4,3072]{2,1,0:T(4,128)(2,1)S(1)}, bf16[3,4,3072]{2,1,0:T(4,128)(2,1)}, u32[]{:S(2)}) copy-start(bf16[3,4,3072]{2,1,0:T(4,128)(2,1)} %param.7) | copy-start | bytes 221188
  23.0 26.5 %copy-start = (f32[1,3072]{1,0:T(1,128)S(1)}, f32[1,3072]{1,0:T(1,128)}, u32[]{:S(2)}) copy-start(f32[1,3072]{1,0:T(1,128)} %param.8) | copy-start | bytes 36868
  29.7 1.8 collective-permute-start.1
  61.5 2.0 collective-permute-start.2
  75.4 1.8 collective-permute-start.3
  106.4 2.0 collective-permute-start.4
  120.2 1.8 collective-permute-start.5
  151.3 2.0 collective-permute-start.6
  158.5 7.0 %copy-start.3 = (bf16[96,128]{1,0:T(8,128)(2,1)S(1)}, bf16[96,128]{1,0:T(8,128)(2,1)}, u32[]{:S(2)}) copy-start(bf16[96,128]{1,0:T(8,128)(2,1)} %get-tuple-element.16) | copy-start | bytes 73732
  158.5 7.1 %copy-start.4 = (bf16[96,128]{1,0:T(8,128)(2,1)S(1)}, bf16[96,128]{1,0:T(8,128)(2,1)}, u32[]{:S(2)}) copy-start(bf16[96,128]{1,0:T(8,128)(2,1)} %get-tuple-element.18) | copy-start | bytes 73732
  158.5 37.5 %copy-start.5 = (bf16[96,128]{1,0:T(8,128)(2,1)S(1)}, bf16[96,128]{1,0:T(8,128)(2,1)}, u32[]{:S(2)}) copy-start(bf16[96,128]{1,0:T(8,128)(2,1)} %get-tuple-element.20) | copy-start | bytes 73732
  165.2 1.8 collective-permute-start.7
  195.6 2.2 collective-permute-start.8
  203.0 7.0 %copy-start.6 = (bf16[96,128]{1,0:T(8,128)(2,1)S(1)}, bf16[96,128]{1,0:T(8,128)(2,1)}, u32[]{:S(2)}) copy-start(bf16[96,128]{1,0:T(8,128)(2,1)} %get-tuple-element.22) | copy-start | bytes 73732
  209.7 1.8 collective-permute-start.9
  240.1 2.0 collective-permute-start.10
  253.9 1.8 collective-permute-start.11

commit v7 on v6

--- a/solution.py
+++ b/solution.py
@@ -160,10 +160,14 @@
 
 
 def expert_mix(rows, coef, gate_w, up_w, down_w):
-    gate = jnp.einsum("fmd,edh->efmh", rows, gate_w, preferred_element_type=jnp.float32)
-    upward = jnp.einsum("fmd,edh->efmh", rows, up_w, preferred_element_type=jnp.float32)
-    gated = (jax.nn.silu(gate) * upward * coef[..., None]).astype(jnp.bfloat16)
-    return jnp.einsum("efmh,ehd->fmd", gated, down_w, preferred_element_type=jnp.float32)
+    gate = jnp.einsum("fmd,edh->fmeh", rows, gate_w, preferred_element_type=jnp.float32)
+    upward = jnp.einsum("fmd,edh->fmeh", rows, up_w, preferred_element_type=jnp.float32)
+    share = jnp.transpose(coef, (1, 2, 0))[..., None]
+    gated = (jax.nn.silu(gate) * upward * share).astype(jnp.bfloat16)
+    shards, local, experts, hidden = gated.shape
+    gated = gated.reshape(shards, local, experts * hidden)
+    down = down_w.reshape(experts * hidden, down_w.shape[2])
+    return jnp.einsum("fmk,kd->fmd", gated, down, preferred_element_type=jnp.float32)
 
 
 def on_device(inputs, gain, w_gate, w_up, w_down, routes, shares):

time: 275 us -> 267 us (0.971)
  matrix products: 63.2 us -> 54.5 us
    dot_general x12 -> x18, matrix products: 63.2 us -> 54.5 us  [the longest x6 24.5 us: expert_mix(): jnp.einsum('fmd,edh->fmeh', rows, up_w, preferred_element_type=jnp.float32)]
where the time goes in v7:
time: 267 us; the launch traced here: 265 us
  Pallas kernels  154 us (58%)
  matrix products  54.5 us (20%)
  other arithmetic  18.7 us (7%)
  waiting for transfers between devices  17.6 us (7%)
  local copies, waits for them, and re-layouts  16.5 us (6%)
    pallas_call x6, Pallas kernels, reduce_relay(): pl.pallas_call(kernel, out_shape=(jax.ShapeDtypeStruct((rows, width), cur...  89.1 us
    pallas_call x6, Pallas kernels, exchange(): pl.pallas_call(kernel, out_shape=jax.ShapeDtypeStruct((chips, rows, width...  65.2 us
    dot_general x6, matrix products, expert_mix(): jnp.einsum('fmd,edh->fmeh', rows, up_w, preferred_element_type=jnp.float32)  24.5 us
    dot_general x6, matrix products, expert_mix(): jnp.einsum('fmd,edh->fmeh', rows, gate_w, preferred_element_type=jnp.floa...  24 us
    ppermute x12, waiting for transfers between devices, sibling(): return lax.ppermute(array, axis, [(i, i ^ 1) for i in range(devices)])  17.6 us
    convert_element_type x6, other arithmetic, rms_norm(): return (values * scale * gain_row[None, :]).astype(jnp.bfloat16)  8.57 us
    concatenate x6, other arithmetic, on_device(): jnp.concatenate([near, sibling(near, 'fsdp')], axis=0)  6.39 us
    dot_general x6, matrix products, expert_mix(): jnp.einsum('fmk,kd->fmd', gated, down, preferred_element_type=jnp.float32)  5.97 us
  transfers between devices with their start and end apart: 12, of which 12 were waited for; matrix products, arithmetic and copies ran while one was open for 1% of the time, Pallas kernels for 0%

profile of v7, /device:TPU:24, one launch (start us, length us, event | category | flops | bytes accessed | tf_op | source)
XLA Modules:
  0.0 264.9 jit_solution(12881646501172602416)
XLA Ops:
  0.0 0.9 multiply_reduce_fusion.5
  1.1 1.4 fusion.114.src_ref
  2.5 13.3 %shard_map.73 = bf16[16,96,128]{2,1,0:T(8,128)(2,1)} custom-call(bf16[96,128]{1,0:T(8,128)(2,1)} %fusion.114.src_ref), custom_call_target="tpu_custom_call" | custom-call | tf_op jit(solution)/shard_map/pallas_call | solution.py:42
  17.8 1.1 pad_maximum_fusion
  19.1 4.0 %fusion.22 = f32[32,4,4,256]{3,0,2,1:T(8,128)S(1)} fusion(bf16[1,4,3072,256]{3,2,1,0:T(8,128)(2,1)} %param.9, bf16[32,4,3072,1]{2,1,0,3:T(4,128)(2,1)S(1)} %bitcast.222), kind=kOutput, calls=%fused_computation.22 | convolution fusion | flops 805306368 | bytes 7602176 | tf_op jit(solution)/shard_map/fmd,edh->fmeh/dot_general | solution.py:163
  23.1 4.1 %fusion.78 = bf16[4,4,4,8,256]{4,3,2,1,0:T(8,128)(2,1)S(1)} fusion(bf16[1,4,3072,256]{3,2,1,0:T(8,128)(2,1)} %param.10, bf16[32,4,3072,1]{2,1,0,3:T(4,128)(2,1)S(1)} %bitcast.223, f32[32,4,4,256]{3,0,2,1:T(8,128)S(1)} %fusion.22, f32[32,4,4]{0,2,1:T(4,128)S(1)} %copy.156), kind=kOutput, calls=%fused_computation.42 | convolution fusion | flops 806223872 | bytes 7866368 | tf_op jit(solution)/shard_map/fmd,edh->fmeh/dot_general | solution.py:164
  27.3 1.0 fusion.132
  28.6 1.6 collective-permute-done.1
  30.6 0.9 reshape.211.sent_ref
  31.5 15.6 %shard_map.74 = (bf16[96,128]{1,0:T(8,128)(2,1)}, bf16[96,128]{1,0:T(8,128)(2,1)}) custom-call(bf16[16,96,128]{2,1,0:T(8,128)(2,1)} %reshape.211.sent_ref, bf16[96,128]{1,0:T(8,128)(2,1)} %copy-done.2), custom_call_target="tpu_custom_call" | custom-call | tf_op jit(solution)/shard_map/pallas_call | solution.py:117
  47.1 0.8 reshape.212
  48.2 1.4 fusion.115
  49.6 10.6 %shard_map.75 = bf16[16,96,128]{2,1,0:T(8,128)(2,1)} custom-call(bf16[96,128]{1,0:T(8,128)(2,1)} %get-tuple-element.43.src_ref), custom_call_target="tpu_custom_call" | custom-call | tf_op jit(solution)/shard_map/pallas_call | solution.py:42
  60.3 1.9 collective-permute-done.2
  62.2 1.1 pad_maximum_fusion.1
  63.5 4.0 %fusion.20 = f32[32,4,4,256]{3,0,2,1:T(8,128)S(1)} fusion(bf16[1,4,3072,256]{3,2,1,0:T(8,128)(2,1)} %param.9, bf16[32,4,3072,1]{2,1,0,3:T(4,128)(2,1)S(1)} %bitcast.224), kind=kOutput, calls=%fused_computation.20 | convolution fusion | flops 805306368 | bytes 7602176 | tf_op jit(solution)/shard_map/fmd,edh->fmeh/dot_general | solution.py:163
  67.5 4.1 %fusion.81 = bf16[4,4,4,8,256]{4,3,2,1,0:T(8,128)(2,1)S(1)} fusion(bf16[1,4,3072,256]{3,2,1,0:T(8,128)(2,1)} %param.10, bf16[32,4,3072,1]{2,1,0,3:T(4,128)(2,1)S(1)} %bitcast.225, f32[32,4,4,256]{3,0,2,1:T(8,128)S(1)} %fusion.20, f32[32,4,4]{0,2,1:T(4,128)S(1)} %copy.161), kind=kOutput, calls=%fused_computation.43 | convolution fusion | flops 806223872 | bytes 7866368 | tf_op jit(solution)/shard_map/fmd,edh->fmeh/dot_general | solution.py:164
  71.6 1.0 fusion.133
  72.9 1.6 collective-permute-done.3
  74.9 0.9 reshape.215.sent_ref
  75.8 15.1 %shard_map.76 = (bf16[96,128]{1,0:T(8,128)(2,1)}, bf16[96,128]{1,0:T(8,128)(2,1)}) custom-call(bf16[16,96,128]{2,1,0:T(8,128)(2,1)} %reshape.215.sent_ref, bf16[96,128]{1,0:T(8,128)(2,1)} %get-tuple-element.44.current_ref), custom_call_target="tpu_custom_call" | custom-call | tf_op jit(solution)/shard_map/pallas_call | solution.py:117
  90.9 0.8 reshape.216
  92.0 1.4 fusion.116
  93.5 10.3 %shard_map.77 = bf16[16,96,128]{2,1,0:T(8,128)(2,1)} custom-call(bf16[96,128]{1,0:T(8,128)(2,1)} %get-tuple-element.39.src_ref), custom_call_target="tpu_custom_call" | custom-call | tf_op jit(solution)/shard_map/pallas_call | solution.py:42
  103.8 1.9 collective-permute-done.4
  105.7 1.1 pad_maximum_fusion.2
  107.0 4.0 %fusion.18 = f32[32,4,4,256]{3,0,2,1:T(8,128)S(1)} fusion(bf16[1,4,3072,256]{3,2,1,0:T(8,128)(2,1)} %param.9, bf16[32,4,3072,1]{2,1,0,3:T(4,128)(2,1)S(1)} %bitcast.226), kind=kOutput, calls=%fused_computation.18 | convolution fusion | flops 805306368 | bytes 7602176 | tf_op jit(solution)/shard_map/fmd,edh->fmeh/dot_general | solution.py:163
  111.0 4.1 %fusion.84 = bf16[4,4,4,8,256]{4,3,2,1,0:T(8,128)(2,1)S(1)} fusion(bf16[1,4,3072,256]{3,2,1,0:T(8,128)(2,1)} %param.10, bf16[32,4,3072,1]{2,1,0,3:T(4,128)(2,1)S(1)} %bitcast.227, f32[32,4,4,256]{3,0,2,1:T(8,128)S(1)} %fusion.18, f32[32,4,4]{0,2,1:T(4,128)S(1)} %copy.166), kind=kOutput, calls=%fused_computation.44 | convolution fusion | flops 806223872 | bytes 7866368 | tf_op jit(solution)/shard_map/fmd,edh->fmeh/dot_general | solution.py:164
  115.2 1.0 fusion.134
  116.5 1.6 collective-permute-done.5
  118.4 0.9 reshape.219.sent_ref
  119.3 15.0 %shard_map.78 = (bf16[96,128]{1,0:T(8,128)(2,1)}, bf16[96,128]{1,0:T(8,128)(2,1)}) custom-call(bf16[16,96,128]{2,1,0:T(8,128)(2,1)} %reshape.219.sent_ref, bf16[96,128]{1,0:T(8,128)(2,1)} %get-tuple-element.40.current_ref), custom_call_target="tpu_custom_call" | custom-call | tf_op jit(solution)/shard_map/pallas_call | solution.py:117
  134.4 0.8 reshape.220
  135.5 1.4 fusion.117
  136.9 10.4 %shard_map.79 = bf16[16,96,128]{2,1,0:T(8,128)(2,1)} custom-call(bf16[96,128]{1,0:T(8,128)(2,1)} %get-tuple-element.35.src_ref), custom_call_target="tpu_custom_call" | custom-call | tf_op jit(solution)/shard_map/pallas_call | solution.py:42
  147.5 1.8 collective-permute-done.6
  149.3 1.1 pad_maximum_fusion.3
  150.6 4.0 %fusion.16 = f32[32,4,4,256]{3,0,2,1:T(8,128)S(1)} fusion(bf16[1,4,3072,256]{3,2,1,0:T(8,128)(2,1)} %param.9, bf16[32,4,3072,1]{2,1,0,3:T(4,128)(2,1)S(1)} %bitcast.228), kind=kOutput, calls=%fused_computation.16 | convolution fusion | flops 805306368 | bytes 7602176 | tf_op jit(solution)/shard_map/fmd,edh->fmeh/dot_general | solution.py:163
  154.6 4.1 %fusion.87 = bf16[4,4,4,8,256]{4,3,2,1,0:T(8,128)(2,1)S(1)} fusion(bf16[1,4,3072,256]{3,2,1,0:T(8,128)(2,1)} %param.10, bf16[32,4,3072,1]{2,1,0,3:T(4,128)(2,1)S(1)} %bitcast.229, f32[32,4,4,256]{3,0,2,1:T(8,128)S(1)} %fusion.16, f32[32,4,4]{0,2,1:T(4,128)S(1)} %copy.171), kind=kOutput, calls=%fused_computation.45 | convolution fusion | flops 806223872 | bytes 7866368 | tf_op jit(solution)/shard_map/fmd,edh->fmeh/dot_general | solution.py:164
  158.8 1.0 fusion.135
  160.2 1.5 collective-permute-done.7
  162.1 0.9 reshape.223.sent_ref
  163.0 14.6 %shard_map.80 = (bf16[96,128]{1,0:T(8,128)(2,1)}, bf16[96,128]{1,0:T(8,128)(2,1)}) custom-call(bf16[16,96,128]{2,1,0:T(8,128)(2,1)} %reshape.223.sent_ref, bf16[96,128]{1,0:T(8,128)(2,1)} %get-tuple-element.36.current_ref), custom_call_target="tpu_custom_call" | custom-call | tf_op jit(solution)/shard_map/pallas_call | solution.py:117
  177.5 0.8 reshape.224
  178.6 1.4 fusion.118
  180.1 10.3 %shard_map.81 = bf16[16,96,128]{2,1,0:T(8,128)(2,1)} custom-call(bf16[96,128]{1,0:T(8,128)(2,1)} %get-tuple-element.31.src_ref), custom_call_target="tpu_custom_call" | custom-call | tf_op jit(solution)/shard_map/pallas_call | solution.py:42
  190.8 1.9 collective-permute-done.8
  192.6 1.1 pad_maximum_fusion.4
  193.9 4.0 %fusion.14 = f32[32,4,4,256]{3,0,2,1:T(8,128)S(1)} fusion(bf16[1,4,3072,256]{3,2,1,0:T(8,128)(2,1)} %param.9, bf16[32,4,3072,1]{2,1,0,3:T(4,128)(2,1)S(1)} %bitcast.230), kind=kOutput, calls=%fused_computation.14 | convolution fusion | flops 805306368 | bytes 7602176 | tf_op jit(solution)/shard_map/fmd,edh->fmeh/dot_general | solution.py:163
  197.9 4.1 %fusion.90 = bf16[4,4,4,8,256]{4,3,2,1,0:T(8,128)(2,1)S(1)} fusion(bf16[1,4,3072,256]{3,2,1,0:T(8,128)(2,1)} %param.10, bf16[32,4,3072,1]{2,1,0,3:T(4,128)(2,1)S(1)} %bitcast.231, f32[32,4,4,256]{3,0,2,1:T(8,128)S(1)} %fusion.14, f32[32,4,4]{0,2,1:T(4,128)S(1)} %copy.176), kind=kOutput, calls=%fused_computation.46 | convolution fusion | flops 806223872 | bytes 7866368 | tf_op jit(solution)/shard_map/fmd,edh->fmeh/dot_general | solution.py:164
  202.1 1.0 fusion.136
  203.4 1.5 collective-permute-done.9
  205.3 0.9 reshape.227.sent_ref
  206.2 14.3 %shard_map.82 = (bf16[96,128]{1,0:T(8,128)(2,1)}, bf16[96,128]{1,0:T(8,128)(2,1)}) custom-call(bf16[16,96,128]{2,1,0:T(8,128)(2,1)} %reshape.227.sent_ref, bf16[96,128]{1,0:T(8,128)(2,1)} %get-tuple-element.32.current_ref), custom_call_target="tpu_custom_call" | custom-call | tf_op jit(solution)/shard_map/pallas_call | solution.py:117
  221.7 1.4 fusion.119
  223.1 10.3 %shard_map.83 = bf16[16,96,128]{2,1,0:T(8,128)(2,1)} custom-call(bf16[96,128]{1,0:T(8,128)(2,1)} %get-tuple-element.27.src_ref), custom_call_target="tpu_custom_call" | custom-call | tf_op jit(solution)/shard_map/pallas_call | solution.py:42
  234.3 1.1 collective-permute-done.10
  235.4 1.1 pad_maximum_fusion.5
  236.7 4.0 %fusion.12 = f32[32,4,4,256]{3,0,2,1:T(8,128)S(1)} fusion(bf16[1,4,3072,256]{3,2,1,0:T(8,128)(2,1)} %param.9, bf16[32,4,3072,1]{2,1,0,3:T(4,128)(2,1)S(1)} %bitcast.232), kind=kOutput, calls=%fused_computation.12 | convolution fusion | flops 805306368 | bytes 7602176 | tf_op jit(solution)/shard_map/fmd,edh->fmeh/dot_general | solution.py:163
  240.7 4.1 %fusion.93 = bf16[4,4,4,8,256]{4,3,2,1,0:T(8,128)(2,1)S(1)} fusion(bf16[1,4,3072,256]{3,2,1,0:T(8,128)(2,1)} %param.10, bf16[32,4,3072,1]{2,1,0,3:T(4,128)(2,1)S(1)} %bitcast.233, f32[32,4,4,256]{3,0,2,1:T(8,128)S(1)} %fusion.12, f32[32,4,4]{0,2,1:T(4,128)S(1)} %copy.181), kind=kOutput, calls=%fused_computation.47 | convolution fusion | flops 806223872 | bytes 7866368 | tf_op jit(solution)/shard_map/fmd,edh->fmeh/dot_general | solution.py:164
  244.9 1.0 fusion.137
  246.8 0.9 collective-permute-done.11
  248.1 0.9 reshape.231.sent_ref
  249.0 14.5 %shard_map.84 = (bf16[96,128]{1,0:T(8,128)(2,1)}, bf16[96,128]{1,0:T(8,128)(2,1)}) custom-call(bf16[16,96,128]{2,1,0:T(8,128)(2,1)} %reshape.231.sent_ref, bf16[96,128]{1,0:T(8,128)(2,1)} %get-tuple-element.28.current_ref), custom_call_target="tpu_custom_call" | custom-call | tf_op jit(solution)/shard_map/pallas_call | solution.py:117
  (144 shorter events, 13.4 us)
Async XLA Ops:
  0.9 22.2 %copy-start.2 = (bf16[96,128]{1,0:T(8,128)(2,1)}, bf16[96,128]{1,0:T(8,128)(2,1)S(1)}, u32[]{:S(2)}) copy-start(bf16[96,128]{1,0:T(8,128)(2,1)S(1)} %squeeze.61.current_ref) | copy-start | bytes 73732
  15.8 2.0 collective-permute-start
  19.1 8.2 %slice-start = ((s8[6291456]{0:T(1024)(128)(4,1)}), s8[4194304]{0:T(1024)(128)(4,1)S(1)}, s32[]{:S(2)}) async-start(s8[6291456]{0:T(1024)(128)(4,1)} %bitcast.197), calls=%async_computation | async-start | bytes 8388608
  23.1 4.2 %slice-start.1 = ((s8[6291456]{0:T(1024)(128)(4,1)}), s8[2097152]{0:T(1024)(128)(4,1)S(1)}, s32[]{:S(2)}) async-start(s8[6291456]{0:T(1024)(128)(4,1)} %bitcast.197), calls=%async_computation.1 | async-start | bytes 4194304
  27.3 20.5 %copy-start.1 = (bf16[3,4,3072]{2,1,0:T(4,128)(2,1)S(1)}, bf16[3,4,3072]{2,1,0:T(4,128)(2,1)}, u32[]{:S(2)}) copy-start(bf16[3,4,3072]{2,1,0:T(4,128)(2,1)} %param.7) | copy-start | bytes 221188
  27.3 20.9 %copy-start = (f32[1,3072]{1,0:T(1,128)S(1)}, f32[1,3072]{1,0:T(1,128)}, u32[]{:S(2)}) copy-start(f32[1,3072]{1,0:T(1,128)} %param.8) | copy-start | bytes 36868
  28.4 1.8 collective-permute-start.1
  60.2 2.0 collective-permute-start.2
  63.4 8.2 %slice-start.2 = ((s8[6291456]{0:T(1024)(128)(4,1)}), s8[4194304]{0:T(1024)(128)(4,1)S(1)}, s32[]{:S(2)}) async-start(s8[6291456]{0:T(1024)(128)(4,1)} %bitcast.200), calls=%async_computation.2 | async-start | bytes 8388608
  67.5 4.2 %slice-start.3 = ((s8[6291456]{0:T(1024)(128)(4,1)}), s8[2097152]{0:T(1024)(128)(4,1)S(1)}, s32[]{:S(2)}) async-start(s8[6291456]{0:T(1024)(128)(4,1)} %bitcast.200), calls=%async_computation.3 | async-start | bytes 4194304
  72.7 1.8 collective-permute-start.3
  103.7 2.0 collective-permute-start.4
  107.0 8.2 %slice-start.4 = ((s8[6291456]{0:T(1024)(128)(4,1)}), s8[4194304]{0:T(1024)(128)(4,1)S(1)}, s32[]{:S(2)}) async-start(s8[6291456]{0:T(1024)(128)(4,1)} %bitcast.203), calls=%async_computation.4 | async-start | bytes 8388608
  111.0 4.2 %slice-start.5 = ((s8[6291456]{0:T(1024)(128)(4,1)}), s8[2097152]{0:T(1024)(128)(4,1)S(1)}, s32[]{:S(2)}) async-start(s8[6291456]{0:T(1024)(128)(4,1)} %bitcast.203), calls=%async_computation.5 | async-start | bytes 4194304
  116.2 1.8 collective-permute-start.5
  147.3 2.0 collective-permute-start.6
  150.6 8.2 %slice-start.6 = ((s8[6291456]{0:T(1024)(128)(4,1)}), s8[4194304]{0:T(1024)(128)(4,1)S(1)}, s32[]{:S(2)}) async-start(s8[6291456]{0:T(1024)(128)(4,1)} %bitcast.206), calls=%async_computation.6 | async-start | bytes 8388608
  154.6 4.2 %slice-start.7 = ((s8[6291456]{0:T(1024)(128)(4,1)}), s8[2097152]{0:T(1024)(128)(4,1)S(1)}, s32[]{:S(2)}) async-start(s8[6291456]{0:T(1024)(128)(4,1)} %bitcast.206), calls=%async_computation.7 | async-start | bytes 4194304
  158.7 1.4 copy-start.3
  158.7 1.4 copy-start.4
  158.8 31.9 %copy-start.5 = (bf16[96,128]{1,0:T(8,128)(2,1)S(1)}, bf16[96,128]{1,0:T(8,128)(2,1)}, u32[]{:S(2)}) copy-start(bf16[96,128]{1,0:T(8,128)(2,1)} %get-tuple-element.20) | copy-start | bytes 73732
  159.9 1.8 collective-permute-start.7
  190.4 2.2 collective-permute-start.8
  193.9 8.2 %slice-start.8 = ((s8[6291456]{0:T(1024)(128)(4,1)}), s8[4194304]{0:T(1024)(128)(4,1)S(1)}, s32[]{:S(2)}) async-start(s8[6291456]{0:T(1024)(128)(4,1)} %bitcast.209), calls=%async_computation.8 | async-start | bytes 8388608
  197.9 4.2 %slice-start.9 = ((s8[6291456]{0:T(1024)(128)(4,1)}), s8[2097152]{0:T(1024)(128)(4,1)S(1)}, s32[]{:S(2)}) async-start(s8[6291456]{0:T(1024)(128)(4,1)} %bitcast.209), calls=%async_computation.9 | async-start | bytes 4194304
  202.0 1.4 copy-start.6
  203.1 1.8 collective-permute-start.9
  233.4 2.0 collective-permute-start.10
  236.7 8.2 %slice-start.10 = ((s8[6291456]{0:T(1024)(128)(4,1)}), s8[4194304]{0:T(1024)(128)(4,1)S(1)}, s32[]{:S(2)}) async-start(s8[6291456]{0:T(1024)(128)(4,1)} %bitcast.212), calls=%async_computation.10 | async-start | bytes 8388608
  240.7 4.1 %slice-start.11 = ((s8[6291456]{0:T(1024)(128)(4,1)}), s8[2097152]{0:T(1024)(128)(4,1)S(1)}, s32[]{:S(2)}) async-start(s8[6291456]{0:T(1024)(128)(4,1)} %bitcast.212), calls=%async_computation.11 | async-start | bytes 4194304
  245.9 1.8 collective-permute-start.11

commit v8 on v7

--- a/solution.py
+++ b/solution.py
@@ -189,29 +189,28 @@
         ],
         axis=2,
     )
-    output = jnp.zeros_like(inputs)
+    lanes = local * width // 128
+    flat_inputs = inputs.reshape(micro, lanes, 128)
+    output = jnp.zeros_like(flat_inputs)
     carried = None
     for tick in range(micro + sections - 1):
         position = tick - section_index
         valid = jnp.logical_and(position >= 0, position < micro)
         clipped = jnp.clip(position, 0, micro - 1)
-        entry = lax.dynamic_index_in_dim(inputs, clipped, 0, keepdims=False)
+        entry = lax.dynamic_index_in_dim(flat_inputs, clipped, 0, keepdims=False)
         coef_now = lax.dynamic_index_in_dim(coef, clipped, 0, keepdims=False)
         current = entry if carried is None else jnp.where(section_index == 0, entry, carried)
-        normed = rms_norm(current, gain_row)
-        lanes = local * width // 128
+        normed = rms_norm(current.reshape(local, width), gain_row)
         near = exchange(normed.reshape(lanes, 128), chips, True, 0)
         rows = jnp.concatenate([near, sibling(near, "fsdp")], axis=0).reshape(shards, local, width)
         partial_value = expert_mix(rows, coef_now, gate_w, up_w, down_w)
         far_sum = sibling(partial_value[chips:].astype(jnp.bfloat16), "fsdp")
         chip_sum = partial_value[:chips] + far_sum.astype(jnp.float32)
         sent = chip_sum.astype(jnp.bfloat16).reshape(chips, lanes, 128)
-        result, carried = reduce_relay(sent, current.reshape(lanes, 128), chips, sections, 1)
-        result = result.reshape(local, width)
-        carried = carried.reshape(local, width)
+        result, carried = reduce_relay(sent, current, chips, sections, 1)
         updated = lax.dynamic_update_index_in_dim(output, result, clipped, 0)
         output = jnp.where(valid, updated, output)
-    return output[None]
+    return output.reshape(1, micro, local, width)
 
 
 def solution(mesh):

time: 267 us -> 264 us (0.989)
  local copies, waits for them, and re-layouts: 16.5 us -> 12.5 us
    convert_element_type x6, other arithmetic: 8.57 us -> 4.92 us  [rms_norm(): return (values * scale * gain_row[None, :]).astype(jnp.bfloat16)]
    reduce_sum x6 -> x12, other arithmetic: 1.61 us -> 5.13 us  [rms_norm(): scale = lax.rsqrt(jnp.mean(values * values, axis=-1, keepdims=True) + 1e-05)]
where the time goes in v8:
time: 264 us; the launch traced here: 262 us
  Pallas kernels  154 us (58%)
  matrix products  54.5 us (21%)
  waiting for transfers between devices  19.2 us (7%)
  other arithmetic  18.7 us (7%)
  local copies, waits for them, and re-layouts  12.5 us (5%)
    pallas_call x6, Pallas kernels, reduce_relay(): pl.pallas_call(kernel, out_shape=(jax.ShapeDtypeStruct((rows, width), cur...  89.2 us
    pallas_call x6, Pallas kernels, exchange(): pl.pallas_call(kernel, out_shape=jax.ShapeDtypeStruct((chips, rows, width...  65.1 us
    dot_general x6, matrix products, expert_mix(): jnp.einsum('fmd,edh->fmeh', rows, up_w, preferred_element_type=jnp.float32)  24.5 us
    dot_general x6, matrix products, expert_mix(): jnp.einsum('fmd,edh->fmeh', rows, gate_w, preferred_element_type=jnp.floa...  24 us
    ppermute x12, waiting for transfers between devices, sibling(): return lax.ppermute(array, axis, [(i, i ^ 1) for i in range(devices)])  19.2 us
    concatenate x6, other arithmetic, on_device(): jnp.concatenate([near, sibling(near, 'fsdp')], axis=0)  6.39 us
    dot_general x6, matrix products, expert_mix(): jnp.einsum('fmk,kd->fmd', gated, down, preferred_element_type=jnp.float32)  5.96 us
    reshape x6, local copies, waits for them, and re-layouts, on_device(): sent = chip_sum.astype(jnp.bfloat16).reshape(chips, lanes, 128)  5.4 us
  transfers between devices with their start and end apart: 12, of which 12 were waited for; matrix products, arithmetic and copies ran while one was open for 1% of the time, Pallas kernels for 0%

profile of v8, /device:TPU:24, one launch (start us, length us, event | category | flops | bytes accessed | tf_op | source)
XLA Modules:
  0.0 262.4 jit_solution(2861045288411434679)
XLA Ops:
  0.0 0.9 reshape.169
  1.4 1.4 fusion.119
  2.8 13.3 %shard_map.73 = bf16[16,96,128]{2,1,0:T(8,128)(2,1)} custom-call(bf16[96,128]{1,0:T(8,128)(2,1)} %get-tuple-element.37.src_ref), custom_call_target="tpu_custom_call" | custom-call | tf_op jit(solution)/shard_map/pallas_call | solution.py:42
  16.3 0.7 select_reduce_fusion
  18.2 1.1 pad_maximum_fusion
  19.5 4.0 %fusion.22 = f32[32,4,4,256]{3,0,2,1:T(8,128)S(1)} fusion(bf16[1,4,3072,256]{3,2,1,0:T(8,128)(2,1)} %param.9, bf16[32,4,3072,1]{2,1,0,3:T(4,128)(2,1)S(1)} %bitcast.238), kind=kOutput, calls=%fused_computation.22 | convolution fusion | flops 805306368 | bytes 7602176 | tf_op jit(solution)/shard_map/fmd,edh->fmeh/dot_general | solution.py:163
  23.5 4.1 %fusion.78 = bf16[4,4,4,8,256]{4,3,2,1,0:T(8,128)(2,1)S(1)} fusion(bf16[1,4,3072,256]{3,2,1,0:T(8,128)(2,1)} %param.10, bf16[32,4,3072,1]{2,1,0,3:T(4,128)(2,1)S(1)} %bitcast.239, f32[32,4,4,256]{3,0,2,1:T(8,128)S(1)} %fusion.22, f32[32,4,4]{0,2,1:T(4,128)S(1)} %copy.156), kind=kOutput, calls=%fused_computation.42 | convolution fusion | flops 806223872 | bytes 7866368 | tf_op jit(solution)/shard_map/fmd,edh->fmeh/dot_general | solution.py:164
  27.6 1.0 fusion.142
  28.9 1.6 collective-permute-done.1
  30.9 0.9 reshape.175.sent_ref
  31.8 15.6 %shard_map.74 = (bf16[96,128]{1,0:T(8,128)(2,1)}, bf16[96,128]{1,0:T(8,128)(2,1)}) custom-call(bf16[16,96,128]{2,1,0:T(8,128)(2,1)} %reshape.175.sent_ref, bf16[96,128]{1,0:T(8,128)(2,1)} %get-tuple-element.38.current_ref), custom_call_target="tpu_custom_call" | custom-call | tf_op jit(solution)/shard_map/pallas_call | solution.py:117
  47.4 0.9 fusion.114
  49.4 10.6 %shard_map.75 = bf16[16,96,128]{2,1,0:T(8,128)(2,1)} custom-call(bf16[96,128]{1,0:T(8,128)(2,1)} %fusion.120.src_ref), custom_call_target="tpu_custom_call" | custom-call | tf_op jit(solution)/shard_map/pallas_call | solution.py:42
  60.0 1.9 collective-permute-done.2
  61.9 1.1 pad_maximum_fusion.1
  63.2 4.0 %fusion.20 = f32[32,4,4,256]{3,0,2,1:T(8,128)S(1)} fusion(bf16[1,4,3072,256]{3,2,1,0:T(8,128)(2,1)} %param.9, bf16[32,4,3072,1]{2,1,0,3:T(4,128)(2,1)S(1)} %bitcast.240), kind=kOutput, calls=%fused_computation.20 | convolution fusion | flops 805306368 | bytes 7602176 | tf_op jit(solution)/shard_map/fmd,edh->fmeh/dot_general | solution.py:163
  67.2 4.1 %fusion.81 = bf16[4,4,4,8,256]{4,3,2,1,0:T(8,128)(2,1)S(1)} fusion(bf16[1,4,3072,256]{3,2,1,0:T(8,128)(2,1)} %param.10, bf16[32,4,3072,1]{2,1,0,3:T(4,128)(2,1)S(1)} %bitcast.241, f32[32,4,4,256]{3,0,2,1:T(8,128)S(1)} %fusion.20, f32[32,4,4]{0,2,1:T(4,128)S(1)} %copy.161), kind=kOutput, calls=%fused_computation.43 | convolution fusion | flops 806223872 | bytes 7866368 | tf_op jit(solution)/shard_map/fmd,edh->fmeh/dot_general | solution.py:164
  71.4 1.0 fusion.143
  72.7 1.6 collective-permute-done.3
  74.6 0.9 reshape.178.sent_ref
  75.5 15.1 %shard_map.76 = (bf16[96,128]{1,0:T(8,128)(2,1)}, bf16[96,128]{1,0:T(8,128)(2,1)}) custom-call(bf16[16,96,128]{2,1,0:T(8,128)(2,1)} %reshape.178.sent_ref, bf16[96,128]{1,0:T(8,128)(2,1)} %copy-done.3), custom_call_target="tpu_custom_call" | custom-call | tf_op jit(solution)/shard_map/pallas_call | solution.py:117
  90.7 0.9 fusion.115
  92.6 10.3 %shard_map.77 = bf16[16,96,128]{2,1,0:T(8,128)(2,1)} custom-call(bf16[96,128]{1,0:T(8,128)(2,1)} %fusion.121.src_ref), custom_call_target="tpu_custom_call" | custom-call | tf_op jit(solution)/shard_map/pallas_call | solution.py:42
  103.0 1.9 collective-permute-done.4
  104.9 1.1 pad_maximum_fusion.2
  106.2 4.0 %fusion.18 = f32[32,4,4,256]{3,0,2,1:T(8,128)S(1)} fusion(bf16[1,4,3072,256]{3,2,1,0:T(8,128)(2,1)} %param.9, bf16[32,4,3072,1]{2,1,0,3:T(4,128)(2,1)S(1)} %bitcast.242), kind=kOutput, calls=%fused_computation.18 | convolution fusion | flops 805306368 | bytes 7602176 | tf_op jit(solution)/shard_map/fmd,edh->fmeh/dot_general | solution.py:163
  110.2 4.1 %fusion.84 = bf16[4,4,4,8,256]{4,3,2,1,0:T(8,128)(2,1)S(1)} fusion(bf16[1,4,3072,256]{3,2,1,0:T(8,128)(2,1)} %param.10, bf16[32,4,3072,1]{2,1,0,3:T(4,128)(2,1)S(1)} %bitcast.243, f32[32,4,4,256]{3,0,2,1:T(8,128)S(1)} %fusion.18, f32[32,4,4]{0,2,1:T(4,128)S(1)} %copy.166), kind=kOutput, calls=%fused_computation.44 | convolution fusion | flops 806223872 | bytes 7866368 | tf_op jit(solution)/shard_map/fmd,edh->fmeh/dot_general | solution.py:164
  114.4 1.0 fusion.144
  115.7 1.6 collective-permute-done.5
  117.6 0.9 reshape.181.sent_ref
  118.5 15.1 %shard_map.78 = (bf16[96,128]{1,0:T(8,128)(2,1)}, bf16[96,128]{1,0:T(8,128)(2,1)}) custom-call(bf16[16,96,128]{2,1,0:T(8,128)(2,1)} %reshape.181.sent_ref, bf16[96,128]{1,0:T(8,128)(2,1)} %copy-done.4), custom_call_target="tpu_custom_call" | custom-call | tf_op jit(solution)/shard_map/pallas_call | solution.py:117
  133.6 0.9 fusion.116
  134.9 0.7 fusion.122.src_ref
  135.6 10.4 %shard_map.79 = bf16[16,96,128]{2,1,0:T(8,128)(2,1)} custom-call(bf16[96,128]{1,0:T(8,128)(2,1)} %fusion.122.src_ref), custom_call_target="tpu_custom_call" | custom-call | tf_op jit(solution)/shard_map/pallas_call | solution.py:42
  146.1 1.9 collective-permute-done.6
  148.0 1.1 pad_maximum_fusion.3
  149.2 4.0 %fusion.16 = f32[32,4,4,256]{3,0,2,1:T(8,128)S(1)} fusion(bf16[1,4,3072,256]{3,2,1,0:T(8,128)(2,1)} %param.9, bf16[32,4,3072,1]{2,1,0,3:T(4,128)(2,1)S(1)} %bitcast.244), kind=kOutput, calls=%fused_computation.16 | convolution fusion | flops 805306368 | bytes 7602176 | tf_op jit(solution)/shard_map/fmd,edh->fmeh/dot_general | solution.py:163
  153.3 4.1 %fusion.87 = bf16[4,4,4,8,256]{4,3,2,1,0:T(8,128)(2,1)S(1)} fusion(bf16[1,4,3072,256]{3,2,1,0:T(8,128)(2,1)} %param.10, bf16[32,4,3072,1]{2,1,0,3:T(4,128)(2,1)S(1)} %bitcast.245, f32[32,4,4,256]{3,0,2,1:T(8,128)S(1)} %fusion.16, f32[32,4,4]{0,2,1:T(4,128)S(1)} %copy.171), kind=kOutput, calls=%fused_computation.45 | convolution fusion | flops 806223872 | bytes 7866368 | tf_op jit(solution)/shard_map/fmd,edh->fmeh/dot_general | solution.py:164
  157.4 1.0 fusion.145
  158.7 1.6 collective-permute-done.7
  160.7 0.9 reshape.184.sent_ref
  161.6 14.6 %shard_map.80 = (bf16[96,128]{1,0:T(8,128)(2,1)}, bf16[96,128]{1,0:T(8,128)(2,1)}) custom-call(bf16[16,96,128]{2,1,0:T(8,128)(2,1)} %reshape.184.sent_ref, bf16[96,128]{1,0:T(8,128)(2,1)} %copy-done.5), custom_call_target="tpu_custom_call" | custom-call | tf_op jit(solution)/shard_map/pallas_call | solution.py:117
  176.2 0.9 fusion.117
  177.4 0.7 fusion.123.src_ref
  178.1 10.3 %shard_map.81 = bf16[16,96,128]{2,1,0:T(8,128)(2,1)} custom-call(bf16[96,128]{1,0:T(8,128)(2,1)} %fusion.123.src_ref), custom_call_target="tpu_custom_call" | custom-call | tf_op jit(solution)/shard_map/pallas_call | solution.py:42
  188.7 1.9 collective-permute-done.8
  190.6 1.1 pad_maximum_fusion.4
  191.9 4.0 %fusion.14 = f32[32,4,4,256]{3,0,2,1:T(8,128)S(1)} fusion(bf16[1,4,3072,256]{3,2,1,0:T(8,128)(2,1)} %param.9, bf16[32,4,3072,1]{2,1,0,3:T(4,128)(2,1)S(1)} %bitcast.246), kind=kOutput, calls=%fused_computation.14 | convolution fusion | flops 805306368 | bytes 7602176 | tf_op jit(solution)/shard_map/fmd,edh->fmeh/dot_general | solution.py:163
  195.9 4.1 %fusion.90 = bf16[4,4,4,8,256]{4,3,2,1,0:T(8,128)(2,1)S(1)} fusion(bf16[1,4,3072,256]{3,2,1,0:T(8,128)(2,1)} %param.10, bf16[32,4,3072,1]{2,1,0,3:T(4,128)(2,1)S(1)} %bitcast.247, f32[32,4,4,256]{3,0,2,1:T(8,128)S(1)} %fusion.14, f32[32,4,4]{0,2,1:T(4,128)S(1)} %copy.176), kind=kOutput, calls=%fused_computation.46 | convolution fusion | flops 806223872 | bytes 7866368 | tf_op jit(solution)/shard_map/fmd,edh->fmeh/dot_general | solution.py:164
  200.1 1.0 fusion.146
  201.4 1.5 collective-permute-done.9
  203.4 0.9 reshape.187.sent_ref
  204.3 14.4 %shard_map.82 = (bf16[96,128]{1,0:T(8,128)(2,1)}, bf16[96,128]{1,0:T(8,128)(2,1)}) custom-call(bf16[16,96,128]{2,1,0:T(8,128)(2,1)} %reshape.187.sent_ref, bf16[96,128]{1,0:T(8,128)(2,1)} %copy-done.1), custom_call_target="tpu_custom_call" | custom-call | tf_op jit(solution)/shard_map/pallas_call | solution.py:117
  218.7 0.9 fusion.118
  220.6 10.3 %shard_map.83 = bf16[16,96,128]{2,1,0:T(8,128)(2,1)} custom-call(bf16[96,128]{1,0:T(8,128)(2,1)} %fusion.124.src_ref), custom_call_target="tpu_custom_call" | custom-call | tf_op jit(solution)/shard_map/pallas_call | solution.py:42
  231.1 1.8 collective-permute-done.10
  232.9 1.1 pad_maximum_fusion.5
  234.2 4.0 %fusion.12 = f32[32,4,4,256]{3,0,2,1:T(8,128)S(1)} fusion(bf16[1,4,3072,256]{3,2,1,0:T(8,128)(2,1)} %param.9, bf16[32,4,3072,1]{2,1,0,3:T(4,128)(2,1)S(1)} %bitcast.248), kind=kOutput, calls=%fused_computation.12 | convolution fusion | flops 805306368 | bytes 7602176 | tf_op jit(solution)/shard_map/fmd,edh->fmeh/dot_general | solution.py:163
  238.2 4.1 %fusion.93 = bf16[4,4,4,8,256]{4,3,2,1,0:T(8,128)(2,1)S(1)} fusion(bf16[1,4,3072,256]{3,2,1,0:T(8,128)(2,1)} %param.10, bf16[32,4,3072,1]{2,1,0,3:T(4,128)(2,1)S(1)} %bitcast.249, f32[32,4,4,256]{3,0,2,1:T(8,128)S(1)} %fusion.12, f32[32,4,4]{0,2,1:T(4,128)S(1)} %copy.181), kind=kOutput, calls=%fused_computation.47 | convolution fusion | flops 806223872 | bytes 7866368 | tf_op jit(solution)/shard_map/fmd,edh->fmeh/dot_general | solution.py:164
  242.4 1.0 fusion.147
  243.7 1.5 collective-permute-done.11
  245.7 0.9 reshape.190.sent_ref
  246.6 14.4 %shard_map.84 = (bf16[96,128]{1,0:T(8,128)(2,1)}, bf16[96,128]{1,0:T(8,128)(2,1)}) custom-call(bf16[16,96,128]{2,1,0:T(8,128)(2,1)} %reshape.190.sent_ref, bf16[96,128]{1,0:T(8,128)(2,1)} %copy-done.2), custom_call_target="tpu_custom_call" | custom-call | tf_op jit(solution)/shard_map/pallas_call | solution.py:117
  261.0 0.8 fusion.125
  (147 shorter events, 12.4 us)
Async XLA Ops:
  16.2 2.0 collective-permute-start
  19.4 8.2 %slice-start = ((s8[6291456]{0:T(1024)(128)(4,1)}), s8[4194304]{0:T(1024)(128)(4,1)S(1)}, s32[]{:S(2)}) async-start(s8[6291456]{0:T(1024)(128)(4,1)} %bitcast.214), calls=%async_computation | async-start | bytes 8388608
  23.5 4.2 %slice-start.1 = ((s8[6291456]{0:T(1024)(128)(4,1)}), s8[2097152]{0:T(1024)(128)(4,1)S(1)}, s32[]{:S(2)}) async-start(s8[6291456]{0:T(1024)(128)(4,1)} %bitcast.214), calls=%async_computation.1 | async-start | bytes 4194304
  27.6 21.0 %copy-start = (f32[1,3072]{1,0:T(1,128)S(1)}, f32[1,3072]{1,0:T(1,128)}, u32[]{:S(2)}) copy-start(f32[1,3072]{1,0:T(1,128)} %param.8) | copy-start | bytes 36868
  28.7 1.8 collective-permute-start.1
  48.3 18.9 %copy-start.3 = (bf16[96,128]{1,0:T(8,128)(2,1)}, bf16[96,128]{1,0:T(8,128)(2,1)S(1)}, u32[]{:S(2)}) copy-start(bf16[96,128]{1,0:T(8,128)(2,1)S(1)} %get-tuple-element.36.current_ref) | copy-start | bytes 73732
  59.9 2.0 collective-permute-start.2
  63.2 8.2 %slice-start.2 = ((s8[6291456]{0:T(1024)(128)(4,1)}), s8[4194304]{0:T(1024)(128)(4,1)S(1)}, s32[]{:S(2)}) async-start(s8[6291456]{0:T(1024)(128)(4,1)} %bitcast.217), calls=%async_computation.2 | async-start | bytes 8388608
  67.2 4.2 %slice-start.3 = ((s8[6291456]{0:T(1024)(128)(4,1)}), s8[2097152]{0:T(1024)(128)(4,1)S(1)}, s32[]{:S(2)}) async-start(s8[6291456]{0:T(1024)(128)(4,1)} %bitcast.217), calls=%async_computation.3 | async-start | bytes 4194304
  72.4 1.8 collective-permute-start.3
  91.5 18.7 %copy-start.4 = (bf16[96,128]{1,0:T(8,128)(2,1)}, bf16[96,128]{1,0:T(8,128)(2,1)S(1)}, u32[]{:S(2)}) copy-start(bf16[96,128]{1,0:T(8,128)(2,1)S(1)} %get-tuple-element.34.current_ref) | copy-start | bytes 73732
  102.9 2.0 collective-permute-start.4
  106.2 8.2 %slice-start.4 = ((s8[6291456]{0:T(1024)(128)(4,1)}), s8[4194304]{0:T(1024)(128)(4,1)S(1)}, s32[]{:S(2)}) async-start(s8[6291456]{0:T(1024)(128)(4,1)} %bitcast.220), calls=%async_computation.4 | async-start | bytes 8388608
  110.2 4.2 %slice-start.5 = ((s8[6291456]{0:T(1024)(128)(4,1)}), s8[2097152]{0:T(1024)(128)(4,1)S(1)}, s32[]{:S(2)}) async-start(s8[6291456]{0:T(1024)(128)(4,1)} %bitcast.220), calls=%async_computation.5 | async-start | bytes 4194304
  115.4 1.8 collective-permute-start.5
  134.5 18.8 %copy-start.5 = (bf16[96,128]{1,0:T(8,128)(2,1)}, bf16[96,128]{1,0:T(8,128)(2,1)S(1)}, u32[]{:S(2)}) copy-start(bf16[96,128]{1,0:T(8,128)(2,1)S(1)} %get-tuple-element.32.current_ref) | copy-start | bytes 73732
  146.0 2.0 collective-permute-start.6
  149.2 8.2 %slice-start.6 = ((s8[6291456]{0:T(1024)(128)(4,1)}), s8[4194304]{0:T(1024)(128)(4,1)S(1)}, s32[]{:S(2)}) async-start(s8[6291456]{0:T(1024)(128)(4,1)} %bitcast.223), calls=%async_computation.6 | async-start | bytes 8388608
  153.3 4.2 %slice-start.7 = ((s8[6291456]{0:T(1024)(128)(4,1)}), s8[2097152]{0:T(1024)(128)(4,1)S(1)}, s32[]{:S(2)}) async-start(s8[6291456]{0:T(1024)(128)(4,1)} %bitcast.223), calls=%async_computation.7 | async-start | bytes 4194304
  158.5 1.8 collective-permute-start.7
  177.0 18.9 %copy-start.1 = (bf16[96,128]{1,0:T(8,128)(2,1)}, bf16[96,128]{1,0:T(8,128)(2,1)S(1)}, u32[]{:S(2)}) copy-start(bf16[96,128]{1,0:T(8,128)(2,1)S(1)} %get-tuple-element.30.current_ref) | copy-start | bytes 73732
  188.4 2.2 collective-permute-start.8
  191.9 8.2 %slice-start.8 = ((s8[6291456]{0:T(1024)(128)(4,1)}), s8[4194304]{0:T(1024)(128)(4,1)S(1)}, s32[]{:S(2)}) async-start(s8[6291456]{0:T(1024)(128)(4,1)} %bitcast.226), calls=%async_computation.8 | async-start | bytes 8388608
  195.9 4.2 %slice-start.9 = ((s8[6291456]{0:T(1024)(128)(4,1)}), s8[2097152]{0:T(1024)(128)(4,1)S(1)}, s32[]{:S(2)}) async-start(s8[6291456]{0:T(1024)(128)(4,1)} %bitcast.226), calls=%async_computation.9 | async-start | bytes 4194304
  200.0 1.4 copy-start.6
  200.1 30.9 %copy-start.7 = (bf16[96,128]{1,0:T(8,128)(2,1)S(1)}, bf16[96,128]{1,0:T(8,128)(2,1)}, u32[]{:S(2)}) copy-start(bf16[96,128]{1,0:T(8,128)(2,1)} %get-tuple-element.18) | copy-start | bytes 73732
  200.1 31.0 %copy-start.8 = (bf16[96,128]{1,0:T(8,128)(2,1)S(1)}, bf16[96,128]{1,0:T(8,128)(2,1)}, u32[]{:S(2)}) copy-start(bf16[96,128]{1,0:T(8,128)(2,1)} %get-tuple-element.20) | copy-start | bytes 73732
  201.1 1.8 collective-permute-start.9
  219.5 18.7 %copy-start.2 = (bf16[96,128]{1,0:T(8,128)(2,1)}, bf16[96,128]{1,0:T(8,128)(2,1)S(1)}, u32[]{:S(2)}) copy-start(bf16[96,128]{1,0:T(8,128)(2,1)S(1)} %get-tuple-element.28.current_ref) | copy-start | bytes 73732
  230.9 2.0 collective-permute-start.10
  234.2 8.2 %slice-start.10 = ((s8[6291456]{0:T(1024)(128)(4,1)}), s8[4194304]{0:T(1024)(128)(4,1)S(1)}, s32[]{:S(2)}) async-start(s8[6291456]{0:T(1024)(128)(4,1)} %bitcast.229), calls=%async_computation.10 | async-start | bytes 8388608
  238.2 4.2 %slice-start.11 = ((s8[6291456]{0:T(1024)(128)(4,1)}), s8[2097152]{0:T(1024)(128)(4,1)S(1)}, s32[]{:S(2)}) async-start(s8[6291456]{0:T(1024)(128)(4,1)} %bitcast.229), calls=%async_computation.11 | async-start | bytes 4194304
  242.3 1.4 copy-start.9
  242.3 1.4 copy-start.10
  243.5 1.8 collective-permute-start.11

commit v9 on v8

--- a/solution.py
+++ b/solution.py
@@ -151,6 +151,16 @@
     return (values * scale * gain_row[None, :]).astype(jnp.bfloat16)
 
 
+def rms_norm_lanes(rows, gain_lanes, tokens):
+    values = rows.astype(jnp.float32)
+    per_row = jnp.sum(values * values, axis=1)
+    per_token = jnp.sum(per_row.reshape(tokens, -1), axis=1)
+    width = rows.size // tokens
+    scale = lax.rsqrt(per_token / width + 1e-05)
+    scale_rows = jnp.repeat(scale, rows.shape[0] // tokens)
+    return (values * scale_rows[:, None] * gain_lanes).astype(jnp.bfloat16)
+
+
 def combine_weights(route_layer, share_layer, experts, shards):
     micro, tokens, top = route_layer.shape
     per = tokens // shards
@@ -190,6 +200,7 @@
         axis=2,
     )
     lanes = local * width // 128
+    gain_lanes = jnp.tile(gain_row.reshape(lanes // local, 128), (local, 1))
     flat_inputs = inputs.reshape(micro, lanes, 128)
     output = jnp.zeros_like(flat_inputs)
     carried = None
@@ -200,8 +211,8 @@
         entry = lax.dynamic_index_in_dim(flat_inputs, clipped, 0, keepdims=False)
         coef_now = lax.dynamic_index_in_dim(coef, clipped, 0, keepdims=False)
         current = entry if carried is None else jnp.where(section_index == 0, entry, carried)
-        normed = rms_norm(current.reshape(local, width), gain_row)
-        near = exchange(normed.reshape(lanes, 128), chips, True, 0)
+        normed = rms_norm_lanes(current, gain_lanes, local)
+        near = exchange(normed, chips, True, 0)
         rows = jnp.concatenate([near, sibling(near, "fsdp")], axis=0).reshape(shards, local, width)
         partial_value = expert_mix(rows, coef_now, gate_w, up_w, down_w)
         far_sum = sibling(partial_value[chips:].astype(jnp.bfloat16), "fsdp")

time: 264 us -> 264 us (level)
  no operation moved by 1% of the time
where the time goes in v9:
time: 264 us; the launch traced here: 262 us
  Pallas kernels  154 us (58%)
  matrix products  54.6 us (21%)
  waiting for transfers between devices  19.2 us (7%)
  other arithmetic  18.7 us (7%)
  local copies, waits for them, and re-layouts  12.5 us (5%)
    pallas_call x6, Pallas kernels, reduce_relay(): pl.pallas_call(kernel, out_shape=(jax.ShapeDtypeStruct((rows, width), cur...  89 us
    pallas_call x6, Pallas kernels, exchange(): pl.pallas_call(kernel, out_shape=jax.ShapeDtypeStruct((chips, rows, width...  65.2 us
    dot_general x6, matrix products, expert_mix(): jnp.einsum('fmd,edh->fmeh', rows, up_w, preferred_element_type=jnp.float32)  24.5 us
    dot_general x6, matrix products, expert_mix(): jnp.einsum('fmd,edh->fmeh', rows, gate_w, preferred_element_type=jnp.floa...  24 us
    ppermute x12, waiting for transfers between devices, sibling(): return lax.ppermute(array, axis, [(i, i ^ 1) for i in range(devices)])  19.2 us
    concatenate x6, other arithmetic, on_device(): jnp.concatenate([near, sibling(near, 'fsdp')], axis=0)  6.39 us
    dot_general x6, matrix products, expert_mix(): jnp.einsum('fmk,kd->fmd', gated, down, preferred_element_type=jnp.float32)  5.97 us
    reshape x6, local copies, waits for them, and re-layouts, on_device(): sent = chip_sum.astype(jnp.bfloat16).reshape(chips, lanes, 128)  5.37 us
  transfers between devices with their start and end apart: 12, of which 12 were waited for; matrix products, arithmetic and copies ran while one was open for 1% of the time, Pallas kernels for 0%

profile of v9, /device:TPU:24, one launch (start us, length us, event | category | flops | bytes accessed | tf_op | source)
XLA Modules:
  0.0 262.3 jit_solution(17187211001045441162)
XLA Ops:
  0.0 0.9 reshape.103
  1.4 1.4 fusion.120.src_ref
  2.8 13.3 %shard_map.73 = bf16[16,96,128]{2,1,0:T(8,128)(2,1)} custom-call(bf16[96,128]{1,0:T(8,128)(2,1)} %fusion.120.src_ref), custom_call_target="tpu_custom_call" | custom-call | tf_op jit(solution)/shard_map/pallas_call | solution.py:42
  16.3 0.7 select_reduce_fusion
  18.2 1.1 pad_maximum_fusion
  19.5 4.0 %fusion.22 = f32[32,4,4,256]{3,0,2,1:T(8,128)S(1)} fusion(bf16[1,4,3072,256]{3,2,1,0:T(8,128)(2,1)} %param.9, bf16[32,4,3072,1]{2,1,0,3:T(4,128)(2,1)S(1)} %bitcast.238), kind=kOutput, calls=%fused_computation.22 | convolution fusion | flops 805306368 | bytes 7602176 | tf_op jit(solution)/shard_map/fmd,edh->fmeh/dot_general | solution.py:173
  23.5 4.1 %fusion.78 = bf16[4,4,4,8,256]{4,3,2,1,0:T(8,128)(2,1)S(1)} fusion(bf16[1,4,3072,256]{3,2,1,0:T(8,128)(2,1)} %param.10, bf16[32,4,3072,1]{2,1,0,3:T(4,128)(2,1)S(1)} %bitcast.239, f32[32,4,4,256]{3,0,2,1:T(8,128)S(1)} %fusion.22, f32[32,4,4]{0,2,1:T(4,128)S(1)} %copy.156), kind=kOutput, calls=%fused_computation.42 | convolution fusion | flops 806223872 | bytes 7866368 | tf_op jit(solution)/shard_map/fmd,edh->fmeh/dot_general | solution.py:174
  27.6 1.0 fusion.143
  28.9 1.6 collective-permute-done.1
  30.9 0.9 reshape.109.sent_ref
  31.8 15.6 %shard_map.74 = (bf16[96,128]{1,0:T(8,128)(2,1)}, bf16[96,128]{1,0:T(8,128)(2,1)}) custom-call(bf16[16,96,128]{2,1,0:T(8,128)(2,1)} %reshape.109.sent_ref, bf16[96,128]{1,0:T(8,128)(2,1)} %copy-done.1), custom_call_target="tpu_custom_call" | custom-call | tf_op jit(solution)/shard_map/pallas_call | solution.py:117
  47.4 0.9 fusion.115
  49.3 10.6 %shard_map.75 = bf16[16,96,128]{2,1,0:T(8,128)(2,1)} custom-call(bf16[96,128]{1,0:T(8,128)(2,1)} %fusion.121.src_ref), custom_call_target="tpu_custom_call" | custom-call | tf_op jit(solution)/shard_map/pallas_call | solution.py:42
  60.0 1.9 collective-permute-done.2
  61.9 1.1 pad_maximum_fusion.1
  63.2 4.0 %fusion.20 = f32[32,4,4,256]{3,0,2,1:T(8,128)S(1)} fusion(bf16[1,4,3072,256]{3,2,1,0:T(8,128)(2,1)} %param.9, bf16[32,4,3072,1]{2,1,0,3:T(4,128)(2,1)S(1)} %bitcast.240), kind=kOutput, calls=%fused_computation.20 | convolution fusion | flops 805306368 | bytes 7602176 | tf_op jit(solution)/shard_map/fmd,edh->fmeh/dot_general | solution.py:173
  67.2 4.1 %fusion.81 = bf16[4,4,4,8,256]{4,3,2,1,0:T(8,128)(2,1)S(1)} fusion(bf16[1,4,3072,256]{3,2,1,0:T(8,128)(2,1)} %param.10, bf16[32,4,3072,1]{2,1,0,3:T(4,128)(2,1)S(1)} %bitcast.241, f32[32,4,4,256]{3,0,2,1:T(8,128)S(1)} %fusion.20, f32[32,4,4]{0,2,1:T(4,128)S(1)} %copy.161), kind=kOutput, calls=%fused_computation.43 | convolution fusion | flops 806223872 | bytes 7866368 | tf_op jit(solution)/shard_map/fmd,edh->fmeh/dot_general | solution.py:174
  71.4 1.0 fusion.144
  72.6 1.6 collective-permute-done.3
  74.6 0.9 reshape.113.sent_ref
  75.5 15.1 %shard_map.76 = (bf16[96,128]{1,0:T(8,128)(2,1)}, bf16[96,128]{1,0:T(8,128)(2,1)}) custom-call(bf16[16,96,128]{2,1,0:T(8,128)(2,1)} %reshape.113.sent_ref, bf16[96,128]{1,0:T(8,128)(2,1)} %copy-done.4), custom_call_target="tpu_custom_call" | custom-call | tf_op jit(solution)/shard_map/pallas_call | solution.py:117
  90.7 0.9 fusion.116
  91.9 0.7 fusion.122.src_ref
  92.6 10.3 %shard_map.77 = bf16[16,96,128]{2,1,0:T(8,128)(2,1)} custom-call(bf16[96,128]{1,0:T(8,128)(2,1)} %fusion.122.src_ref), custom_call_target="tpu_custom_call" | custom-call | tf_op jit(solution)/shard_map/pallas_call | solution.py:42
  103.0 1.9 collective-permute-done.4
  104.9 1.1 pad_maximum_fusion.2
  106.2 4.0 %fusion.18 = f32[32,4,4,256]{3,0,2,1:T(8,128)S(1)} fusion(bf16[1,4,3072,256]{3,2,1,0:T(8,128)(2,1)} %param.9, bf16[32,4,3072,1]{2,1,0,3:T(4,128)(2,1)S(1)} %bitcast.242), kind=kOutput, calls=%fused_computation.18 | convolution fusion | flops 805306368 | bytes 7602176 | tf_op jit(solution)/shard_map/fmd,edh->fmeh/dot_general | solution.py:173
  110.2 4.1 %fusion.84 = bf16[4,4,4,8,256]{4,3,2,1,0:T(8,128)(2,1)S(1)} fusion(bf16[1,4,3072,256]{3,2,1,0:T(8,128)(2,1)} %param.10, bf16[32,4,3072,1]{2,1,0,3:T(4,128)(2,1)S(1)} %bitcast.243, f32[32,4,4,256]{3,0,2,1:T(8,128)S(1)} %fusion.18, f32[32,4,4]{0,2,1:T(4,128)S(1)} %copy.166), kind=kOutput, calls=%fused_computation.44 | convolution fusion | flops 806223872 | bytes 7866368 | tf_op jit(solution)/shard_map/fmd,edh->fmeh/dot_general | solution.py:174
  114.4 1.0 fusion.145
  115.6 1.6 collective-permute-done.5
  117.6 0.9 reshape.117.sent_ref
  118.5 15.0 %shard_map.78 = (bf16[96,128]{1,0:T(8,128)(2,1)}, bf16[96,128]{1,0:T(8,128)(2,1)}) custom-call(bf16[16,96,128]{2,1,0:T(8,128)(2,1)} %reshape.117.sent_ref, bf16[96,128]{1,0:T(8,128)(2,1)} %copy-done.5), custom_call_target="tpu_custom_call" | custom-call | tf_op jit(solution)/shard_map/pallas_call | solution.py:117
  133.6 0.9 fusion.117
  134.8 0.7 fusion.123.src_ref
  135.5 10.4 %shard_map.79 = bf16[16,96,128]{2,1,0:T(8,128)(2,1)} custom-call(bf16[96,128]{1,0:T(8,128)(2,1)} %fusion.123.src_ref), custom_call_target="tpu_custom_call" | custom-call | tf_op jit(solution)/shard_map/pallas_call | solution.py:42
  146.0 1.9 collective-permute-done.6
  147.9 1.1 pad_maximum_fusion.3
  149.2 4.0 %fusion.16 = f32[32,4,4,256]{3,0,2,1:T(8,128)S(1)} fusion(bf16[1,4,3072,256]{3,2,1,0:T(8,128)(2,1)} %param.9, bf16[32,4,3072,1]{2,1,0,3:T(4,128)(2,1)S(1)} %bitcast.244), kind=kOutput, calls=%fused_computation.16 | convolution fusion | flops 805306368 | bytes 7602176 | tf_op jit(solution)/shard_map/fmd,edh->fmeh/dot_general | solution.py:173
  153.2 4.1 %fusion.87 = bf16[4,4,4,8,256]{4,3,2,1,0:T(8,128)(2,1)S(1)} fusion(bf16[1,4,3072,256]{3,2,1,0:T(8,128)(2,1)} %param.10, bf16[32,4,3072,1]{2,1,0,3:T(4,128)(2,1)S(1)} %bitcast.245, f32[32,4,4,256]{3,0,2,1:T(8,128)S(1)} %fusion.16, f32[32,4,4]{0,2,1:T(4,128)S(1)} %copy.171), kind=kOutput, calls=%fused_computation.45 | convolution fusion | flops 806223872 | bytes 7866368 | tf_op jit(solution)/shard_map/fmd,edh->fmeh/dot_general | solution.py:174
  157.4 1.0 fusion.146
  158.7 1.6 collective-permute-done.7
  160.7 0.9 reshape.121.sent_ref
  161.6 14.5 %shard_map.80 = (bf16[96,128]{1,0:T(8,128)(2,1)}, bf16[96,128]{1,0:T(8,128)(2,1)}) custom-call(bf16[16,96,128]{2,1,0:T(8,128)(2,1)} %reshape.121.sent_ref, bf16[96,128]{1,0:T(8,128)(2,1)} %copy-done.6), custom_call_target="tpu_custom_call" | custom-call | tf_op jit(solution)/shard_map/pallas_call | solution.py:117
  176.1 0.9 fusion.118
  178.0 10.3 %shard_map.81 = bf16[16,96,128]{2,1,0:T(8,128)(2,1)} custom-call(bf16[96,128]{1,0:T(8,128)(2,1)} %fusion.124.src_ref), custom_call_target="tpu_custom_call" | custom-call | tf_op jit(solution)/shard_map/pallas_call | solution.py:42
  188.6 1.9 collective-permute-done.8
  190.5 1.1 pad_maximum_fusion.4
  191.8 4.0 %fusion.14 = f32[32,4,4,256]{3,0,2,1:T(8,128)S(1)} fusion(bf16[1,4,3072,256]{3,2,1,0:T(8,128)(2,1)} %param.9, bf16[32,4,3072,1]{2,1,0,3:T(4,128)(2,1)S(1)} %bitcast.246), kind=kOutput, calls=%fused_computation.14 | convolution fusion | flops 805306368 | bytes 7602176 | tf_op jit(solution)/shard_map/fmd,edh->fmeh/dot_general | solution.py:173
  195.8 4.1 %fusion.90 = bf16[4,4,4,8,256]{4,3,2,1,0:T(8,128)(2,1)S(1)} fusion(bf16[1,4,3072,256]{3,2,1,0:T(8,128)(2,1)} %param.10, bf16[32,4,3072,1]{2,1,0,3:T(4,128)(2,1)S(1)} %bitcast.247, f32[32,4,4,256]{3,0,2,1:T(8,128)S(1)} %fusion.14, f32[32,4,4]{0,2,1:T(4,128)S(1)} %copy.176), kind=kOutput, calls=%fused_computation.46 | convolution fusion | flops 806223872 | bytes 7866368 | tf_op jit(solution)/shard_map/fmd,edh->fmeh/dot_general | solution.py:174
  200.0 1.0 fusion.147
  201.3 1.5 collective-permute-done.9
  203.3 0.9 reshape.125.sent_ref
  204.2 14.4 %shard_map.82 = (bf16[96,128]{1,0:T(8,128)(2,1)}, bf16[96,128]{1,0:T(8,128)(2,1)}) custom-call(bf16[16,96,128]{2,1,0:T(8,128)(2,1)} %reshape.125.sent_ref, bf16[96,128]{1,0:T(8,128)(2,1)} %copy-done.2), custom_call_target="tpu_custom_call" | custom-call | tf_op jit(solution)/shard_map/pallas_call | solution.py:117
  218.6 0.9 fusion.119
  220.5 10.3 %shard_map.83 = bf16[16,96,128]{2,1,0:T(8,128)(2,1)} custom-call(bf16[96,128]{1,0:T(8,128)(2,1)} %fusion.125.src_ref), custom_call_target="tpu_custom_call" | custom-call | tf_op jit(solution)/shard_map/pallas_call | solution.py:42
  231.0 1.8 collective-permute-done.10
  232.8 1.1 pad_maximum_fusion.5
  234.1 4.0 %fusion.12 = f32[32,4,4,256]{3,0,2,1:T(8,128)S(1)} fusion(bf16[1,4,3072,256]{3,2,1,0:T(8,128)(2,1)} %param.9, bf16[32,4,3072,1]{2,1,0,3:T(4,128)(2,1)S(1)} %bitcast.248), kind=kOutput, calls=%fused_computation.12 | convolution fusion | flops 805306368 | bytes 7602176 | tf_op jit(solution)/shard_map/fmd,edh->fmeh/dot_general | solution.py:173
  238.2 4.1 %fusion.93 = bf16[4,4,4,8,256]{4,3,2,1,0:T(8,128)(2,1)S(1)} fusion(bf16[1,4,3072,256]{3,2,1,0:T(8,128)(2,1)} %param.10, bf16[32,4,3072,1]{2,1,0,3:T(4,128)(2,1)S(1)} %bitcast.249, f32[32,4,4,256]{3,0,2,1:T(8,128)S(1)} %fusion.12, f32[32,4,4]{0,2,1:T(4,128)S(1)} %copy.181), kind=kOutput, calls=%fused_computation.47 | convolution fusion | flops 806223872 | bytes 7866368 | tf_op jit(solution)/shard_map/fmd,edh->fmeh/dot_general | solution.py:174
  242.3 1.0 fusion.148
  243.7 1.5 collective-permute-done.11
  245.6 0.9 reshape.129.sent_ref
  246.5 14.4 %shard_map.84 = (bf16[96,128]{1,0:T(8,128)(2,1)}, bf16[96,128]{1,0:T(8,128)(2,1)}) custom-call(bf16[16,96,128]{2,1,0:T(8,128)(2,1)} %reshape.129.sent_ref, bf16[96,128]{1,0:T(8,128)(2,1)} %copy-done.3), custom_call_target="tpu_custom_call" | custom-call | tf_op jit(solution)/shard_map/pallas_call | solution.py:117
  260.9 0.8 fusion.126
  (149 shorter events, 12.3 us)
Async XLA Ops:
  1.0 22.4 %copy-start.1 = (bf16[96,128]{1,0:T(8,128)(2,1)}, bf16[96,128]{1,0:T(8,128)(2,1)S(1)}, u32[]{:S(2)}) copy-start(bf16[96,128]{1,0:T(8,128)(2,1)S(1)} %get-tuple-element.38.current_ref) | copy-start | bytes 73732
  16.2 2.0 collective-permute-start
  19.4 8.2 %slice-start = ((s8[6291456]{0:T(1024)(128)(4,1)}), s8[4194304]{0:T(1024)(128)(4,1)S(1)}, s32[]{:S(2)}) async-start(s8[6291456]{0:T(1024)(128)(4,1)} %bitcast.214), calls=%async_computation | async-start | bytes 8388608
  23.5 4.1 %slice-start.1 = ((s8[6291456]{0:T(1024)(128)(4,1)}), s8[2097152]{0:T(1024)(128)(4,1)S(1)}, s32[]{:S(2)}) async-start(s8[6291456]{0:T(1024)(128)(4,1)} %bitcast.214), calls=%async_computation.1 | async-start | bytes 4194304
  27.6 21.0 %copy-start = (f32[1,3072]{1,0:T(1,128)S(1)}, f32[1,3072]{1,0:T(1,128)}, u32[]{:S(2)}) copy-start(f32[1,3072]{1,0:T(1,128)} %param.8) | copy-start | bytes 36868
  28.7 1.8 collective-permute-start.1
  48.2 19.0 %copy-start.4 = (bf16[96,128]{1,0:T(8,128)(2,1)}, bf16[96,128]{1,0:T(8,128)(2,1)S(1)}, u32[]{:S(2)}) copy-start(bf16[96,128]{1,0:T(8,128)(2,1)S(1)} %get-tuple-element.36.current_ref) | copy-start | bytes 73732
  59.9 2.0 collective-permute-start.2
  63.2 8.2 %slice-start.2 = ((s8[6291456]{0:T(1024)(128)(4,1)}), s8[4194304]{0:T(1024)(128)(4,1)S(1)}, s32[]{:S(2)}) async-start(s8[6291456]{0:T(1024)(128)(4,1)} %bitcast.217), calls=%async_computation.2 | async-start | bytes 8388608
  67.2 4.2 %slice-start.3 = ((s8[6291456]{0:T(1024)(128)(4,1)}), s8[2097152]{0:T(1024)(128)(4,1)S(1)}, s32[]{:S(2)}) async-start(s8[6291456]{0:T(1024)(128)(4,1)} %bitcast.217), calls=%async_computation.3 | async-start | bytes 4194304
  72.4 1.8 collective-permute-start.3
  91.5 18.7 %copy-start.5 = (bf16[96,128]{1,0:T(8,128)(2,1)}, bf16[96,128]{1,0:T(8,128)(2,1)S(1)}, u32[]{:S(2)}) copy-start(bf16[96,128]{1,0:T(8,128)(2,1)S(1)} %get-tuple-element.34.current_ref) | copy-start | bytes 73732
  102.9 2.0 collective-permute-start.4
  106.2 8.2 %slice-start.4 = ((s8[6291456]{0:T(1024)(128)(4,1)}), s8[4194304]{0:T(1024)(128)(4,1)S(1)}, s32[]{:S(2)}) async-start(s8[6291456]{0:T(1024)(128)(4,1)} %bitcast.220), calls=%async_computation.4 | async-start | bytes 8388608
  110.2 4.2 %slice-start.5 = ((s8[6291456]{0:T(1024)(128)(4,1)}), s8[2097152]{0:T(1024)(128)(4,1)S(1)}, s32[]{:S(2)}) async-start(s8[6291456]{0:T(1024)(128)(4,1)} %bitcast.220), calls=%async_computation.5 | async-start | bytes 4194304
  115.4 1.8 collective-permute-start.5
  134.4 18.8 %copy-start.6 = (bf16[96,128]{1,0:T(8,128)(2,1)}, bf16[96,128]{1,0:T(8,128)(2,1)S(1)}, u32[]{:S(2)}) copy-start(bf16[96,128]{1,0:T(8,128)(2,1)S(1)} %get-tuple-element.32.current_ref) | copy-start | bytes 73732
  145.9 2.0 collective-permute-start.6
  149.2 8.2 %slice-start.6 = ((s8[6291456]{0:T(1024)(128)(4,1)}), s8[4194304]{0:T(1024)(128)(4,1)S(1)}, s32[]{:S(2)}) async-start(s8[6291456]{0:T(1024)(128)(4,1)} %bitcast.223), calls=%async_computation.6 | async-start | bytes 8388608
  153.2 4.2 %slice-start.7 = ((s8[6291456]{0:T(1024)(128)(4,1)}), s8[2097152]{0:T(1024)(128)(4,1)S(1)}, s32[]{:S(2)}) async-start(s8[6291456]{0:T(1024)(128)(4,1)} %bitcast.223), calls=%async_computation.7 | async-start | bytes 4194304
  158.5 1.8 collective-permute-start.7
  176.9 18.9 %copy-start.2 = (bf16[96,128]{1,0:T(8,128)(2,1)}, bf16[96,128]{1,0:T(8,128)(2,1)S(1)}, u32[]{:S(2)}) copy-start(bf16[96,128]{1,0:T(8,128)(2,1)S(1)} %get-tuple-element.30.current_ref) | copy-start | bytes 73732
  188.3 2.2 collective-permute-start.8
  191.8 8.2 %slice-start.8 = ((s8[6291456]{0:T(1024)(128)(4,1)}), s8[4194304]{0:T(1024)(128)(4,1)S(1)}, s32[]{:S(2)}) async-start(s8[6291456]{0:T(1024)(128)(4,1)} %bitcast.226), calls=%async_computation.8 | async-start | bytes 8388608
  195.8 4.2 %slice-start.9 = ((s8[6291456]{0:T(1024)(128)(4,1)}), s8[2097152]{0:T(1024)(128)(4,1)S(1)}, s32[]{:S(2)}) async-start(s8[6291456]{0:T(1024)(128)(4,1)} %bitcast.226), calls=%async_computation.9 | async-start | bytes 4194304
  199.9 1.4 copy-start.7
  200.0 30.9 %copy-start.8 = (bf16[96,128]{1,0:T(8,128)(2,1)S(1)}, bf16[96,128]{1,0:T(8,128)(2,1)}, u32[]{:S(2)}) copy-start(bf16[96,128]{1,0:T(8,128)(2,1)} %get-tuple-element.18) | copy-start | bytes 73732
  200.0 31.0 %copy-start.9 = (bf16[96,128]{1,0:T(8,128)(2,1)S(1)}, bf16[96,128]{1,0:T(8,128)(2,1)}, u32[]{:S(2)}) copy-start(bf16[96,128]{1,0:T(8,128)(2,1)} %get-tuple-element.20) | copy-start | bytes 73732
  201.1 1.8 collective-permute-start.9
  219.4 18.7 %copy-start.3 = (bf16[96,128]{1,0:T(8,128)(2,1)}, bf16[96,128]{1,0:T(8,128)(2,1)S(1)}, u32[]{:S(2)}) copy-start(bf16[96,128]{1,0:T(8,128)(2,1)S(1)} %get-tuple-element.28.current_ref) | copy-start | bytes 73732
  230.8 2.0 collective-permute-start.10
  234.1 8.2 %slice-start.10 = ((s8[6291456]{0:T(1024)(128)(4,1)}), s8[4194304]{0:T(1024)(128)(4,1)S(1)}, s32[]{:S(2)}) async-start(s8[6291456]{0:T(1024)(128)(4,1)} %bitcast.229), calls=%async_computation.10 | async-start | bytes 8388608
  238.1 4.2 %slice-start.11 = ((s8[6291456]{0:T(1024)(128)(4,1)}), s8[2097152]{0:T(1024)(128)(4,1)S(1)}, s32[]{:S(2)}) async-start(s8[6291456]{0:T(1024)(128)(4,1)} %bitcast.229), calls=%async_computation.11 | async-start | bytes 4194304
  242.2 1.3 copy-start.10
  242.3 1.4 copy-start.11
  243.4 1.8 collective-permute-start.11

commit v10 on v8

--- a/solution.py
+++ b/solution.py
@@ -89,11 +89,12 @@
             copy.start()
             copies.append(copy)
         local.wait()
+        mixed = pieces[chip].astype(jnp.float32)
+        for j, copy in enumerate(copies, start=1):
+            copy.wait_recv()
+            mixed = mixed + pieces[lax.rem(chip - j + chips, chips)].astype(jnp.float32)
         for copy in copies:
-            copy.wait()
-        mixed = pieces[0].astype(jnp.float32)
-        for k in range(1, chips):
-            mixed = mixed + pieces[k].astype(jnp.float32)
+            copy.wait_send()
         result_ref[...] = (current_ref[...].astype(jnp.float32) + mixed).astype(result_ref.dtype)
         relay = pltpu.make_async_remote_copy(
             src_ref=result_ref,

time: 264 us -> 264 us (level)
  no operation moved by 1% of the time
where the time goes in v10:
time: 264 us; the launch traced here: 262 us
  Pallas kernels  154 us (58%)
  matrix products  54.6 us (21%)
  waiting for transfers between devices  19.2 us (7%)
  other arithmetic  18.7 us (7%)
  local copies, waits for them, and re-layouts  12.5 us (5%)
    pallas_call x6, Pallas kernels, reduce_relay(): pl.pallas_call(kernel, out_shape=(jax.ShapeDtypeStruct((rows, width), cur...  89.3 us
    pallas_call x6, Pallas kernels, exchange(): pl.pallas_call(kernel, out_shape=jax.ShapeDtypeStruct((chips, rows, width...  65 us
    dot_general x6, matrix products, expert_mix(): jnp.einsum('fmd,edh->fmeh', rows, up_w, preferred_element_type=jnp.float32)  24.6 us
    dot_general x6, matrix products, expert_mix(): jnp.einsum('fmd,edh->fmeh', rows, gate_w, preferred_element_type=jnp.floa...  24 us
    ppermute x12, waiting for transfers between devices, sibling(): return lax.ppermute(array, axis, [(i, i ^ 1) for i in range(devices)])  19.2 us
    concatenate x6, other arithmetic, on_device(): jnp.concatenate([near, sibling(near, 'fsdp')], axis=0)  6.39 us
    dot_general x6, matrix products, expert_mix(): jnp.einsum('fmk,kd->fmd', gated, down, preferred_element_type=jnp.float32)  5.96 us
    reshape x6, local copies, waits for them, and re-layouts, on_device(): sent = chip_sum.astype(jnp.bfloat16).reshape(chips, lanes, 128)  5.4 us
  transfers between devices with their start and end apart: 12, of which 12 were waited for; matrix products, arithmetic and copies ran while one was open for 1% of the time, Pallas kernels for 0%

profile of v10, /device:TPU:24, one launch (start us, length us, event | category | flops | bytes accessed | tf_op | source)
XLA Modules:
  0.0 262.5 jit_solution(12138546373851626053)
XLA Ops:
  0.0 0.9 reshape.169
  1.4 1.4 fusion.119
  2.8 13.3 %shard_map.73 = bf16[16,96,128]{2,1,0:T(8,128)(2,1)} custom-call(bf16[96,128]{1,0:T(8,128)(2,1)} %get-tuple-element.37.src_ref), custom_call_target="tpu_custom_call" | custom-call | tf_op jit(solution)/shard_map/pallas_call | solution.py:42
  16.3 0.7 select_reduce_fusion
  18.2 1.1 pad_maximum_fusion
  19.5 4.0 %fusion.22 = f32[32,4,4,256]{3,0,2,1:T(8,128)S(1)} fusion(bf16[1,4,3072,256]{3,2,1,0:T(8,128)(2,1)} %param.9, bf16[32,4,3072,1]{2,1,0,3:T(4,128)(2,1)S(1)} %bitcast.238), kind=kOutput, calls=%fused_computation.22 | convolution fusion | flops 805306368 | bytes 7602176 | tf_op jit(solution)/shard_map/fmd,edh->fmeh/dot_general | solution.py:164
  23.5 4.1 %fusion.78 = bf16[4,4,4,8,256]{4,3,2,1,0:T(8,128)(2,1)S(1)} fusion(bf16[1,4,3072,256]{3,2,1,0:T(8,128)(2,1)} %param.10, bf16[32,4,3072,1]{2,1,0,3:T(4,128)(2,1)S(1)} %bitcast.239, f32[32,4,4,256]{3,0,2,1:T(8,128)S(1)} %fusion.22, f32[32,4,4]{0,2,1:T(4,128)S(1)} %copy.156), kind=kOutput, calls=%fused_computation.42 | convolution fusion | flops 806223872 | bytes 7866368 | tf_op jit(solution)/shard_map/fmd,edh->fmeh/dot_general | solution.py:165
  27.6 1.0 fusion.142
  28.9 1.6 collective-permute-done.1
  30.9 0.9 reshape.175.sent_ref
  31.8 15.6 %shard_map.74 = (bf16[96,128]{1,0:T(8,128)(2,1)}, bf16[96,128]{1,0:T(8,128)(2,1)}) custom-call(bf16[16,96,128]{2,1,0:T(8,128)(2,1)} %reshape.175.sent_ref, bf16[96,128]{1,0:T(8,128)(2,1)} %get-tuple-element.38.current_ref), custom_call_target="tpu_custom_call" | custom-call | tf_op jit(solution)/shard_map/pallas_call | solution.py:118
  47.4 0.9 fusion.114
  49.4 10.5 %shard_map.75 = bf16[16,96,128]{2,1,0:T(8,128)(2,1)} custom-call(bf16[96,128]{1,0:T(8,128)(2,1)} %fusion.120.src_ref), custom_call_target="tpu_custom_call" | custom-call | tf_op jit(solution)/shard_map/pallas_call | solution.py:42
  60.0 1.9 collective-permute-done.2
  61.9 1.1 pad_maximum_fusion.1
  63.2 4.0 %fusion.20 = f32[32,4,4,256]{3,0,2,1:T(8,128)S(1)} fusion(bf16[1,4,3072,256]{3,2,1,0:T(8,128)(2,1)} %param.9, bf16[32,4,3072,1]{2,1,0,3:T(4,128)(2,1)S(1)} %bitcast.240), kind=kOutput, calls=%fused_computation.20 | convolution fusion | flops 805306368 | bytes 7602176 | tf_op jit(solution)/shard_map/fmd,edh->fmeh/dot_general | solution.py:164
  67.2 4.1 %fusion.81 = bf16[4,4,4,8,256]{4,3,2,1,0:T(8,128)(2,1)S(1)} fusion(bf16[1,4,3072,256]{3,2,1,0:T(8,128)(2,1)} %param.10, bf16[32,4,3072,1]{2,1,0,3:T(4,128)(2,1)S(1)} %bitcast.241, f32[32,4,4,256]{3,0,2,1:T(8,128)S(1)} %fusion.20, f32[32,4,4]{0,2,1:T(4,128)S(1)} %copy.161), kind=kOutput, calls=%fused_computation.43 | convolution fusion | flops 806223872 | bytes 7866368 | tf_op jit(solution)/shard_map/fmd,edh->fmeh/dot_general | solution.py:165
  71.4 1.0 fusion.143
  72.6 1.6 collective-permute-done.3
  74.6 0.9 reshape.178.sent_ref
  75.5 15.2 %shard_map.76 = (bf16[96,128]{1,0:T(8,128)(2,1)}, bf16[96,128]{1,0:T(8,128)(2,1)}) custom-call(bf16[16,96,128]{2,1,0:T(8,128)(2,1)} %reshape.178.sent_ref, bf16[96,128]{1,0:T(8,128)(2,1)} %copy-done.3), custom_call_target="tpu_custom_call" | custom-call | tf_op jit(solution)/shard_map/pallas_call | solution.py:118
  90.7 0.9 fusion.115
  92.0 0.7 fusion.121.src_ref
  92.7 10.2 %shard_map.77 = bf16[16,96,128]{2,1,0:T(8,128)(2,1)} custom-call(bf16[96,128]{1,0:T(8,128)(2,1)} %fusion.121.src_ref), custom_call_target="tpu_custom_call" | custom-call | tf_op jit(solution)/shard_map/pallas_call | solution.py:42
  103.0 1.9 collective-permute-done.4
  104.9 1.1 pad_maximum_fusion.2
  106.2 4.0 %fusion.18 = f32[32,4,4,256]{3,0,2,1:T(8,128)S(1)} fusion(bf16[1,4,3072,256]{3,2,1,0:T(8,128)(2,1)} %param.9, bf16[32,4,3072,1]{2,1,0,3:T(4,128)(2,1)S(1)} %bitcast.242), kind=kOutput, calls=%fused_computation.18 | convolution fusion | flops 805306368 | bytes 7602176 | tf_op jit(solution)/shard_map/fmd,edh->fmeh/dot_general | solution.py:164
  110.2 4.1 %fusion.84 = bf16[4,4,4,8,256]{4,3,2,1,0:T(8,128)(2,1)S(1)} fusion(bf16[1,4,3072,256]{3,2,1,0:T(8,128)(2,1)} %param.10, bf16[32,4,3072,1]{2,1,0,3:T(4,128)(2,1)S(1)} %bitcast.243, f32[32,4,4,256]{3,0,2,1:T(8,128)S(1)} %fusion.18, f32[32,4,4]{0,2,1:T(4,128)S(1)} %copy.166), kind=kOutput, calls=%fused_computation.44 | convolution fusion | flops 806223872 | bytes 7866368 | tf_op jit(solution)/shard_map/fmd,edh->fmeh/dot_general | solution.py:165
  114.3 1.0 fusion.144
  115.6 1.6 collective-permute-done.5
  117.6 0.9 reshape.181.sent_ref
  118.5 15.1 %shard_map.78 = (bf16[96,128]{1,0:T(8,128)(2,1)}, bf16[96,128]{1,0:T(8,128)(2,1)}) custom-call(bf16[16,96,128]{2,1,0:T(8,128)(2,1)} %reshape.181.sent_ref, bf16[96,128]{1,0:T(8,128)(2,1)} %copy-done.4), custom_call_target="tpu_custom_call" | custom-call | tf_op jit(solution)/shard_map/pallas_call | solution.py:118
  133.6 0.9 fusion.116
  134.8 0.7 fusion.122.src_ref
  135.5 10.4 %shard_map.79 = bf16[16,96,128]{2,1,0:T(8,128)(2,1)} custom-call(bf16[96,128]{1,0:T(8,128)(2,1)} %fusion.122.src_ref), custom_call_target="tpu_custom_call" | custom-call | tf_op jit(solution)/shard_map/pallas_call | solution.py:42
  146.0 1.9 collective-permute-done.6
  148.0 1.1 pad_maximum_fusion.3
  149.2 4.0 %fusion.16 = f32[32,4,4,256]{3,0,2,1:T(8,128)S(1)} fusion(bf16[1,4,3072,256]{3,2,1,0:T(8,128)(2,1)} %param.9, bf16[32,4,3072,1]{2,1,0,3:T(4,128)(2,1)S(1)} %bitcast.244), kind=kOutput, calls=%fused_computation.16 | convolution fusion | flops 805306368 | bytes 7602176 | tf_op jit(solution)/shard_map/fmd,edh->fmeh/dot_general | solution.py:164
  153.3 4.1 %fusion.87 = bf16[4,4,4,8,256]{4,3,2,1,0:T(8,128)(2,1)S(1)} fusion(bf16[1,4,3072,256]{3,2,1,0:T(8,128)(2,1)} %param.10, bf16[32,4,3072,1]{2,1,0,3:T(4,128)(2,1)S(1)} %bitcast.245, f32[32,4,4,256]{3,0,2,1:T(8,128)S(1)} %fusion.16, f32[32,4,4]{0,2,1:T(4,128)S(1)} %copy.171), kind=kOutput, calls=%fused_computation.45 | convolution fusion | flops 806223872 | bytes 7866368 | tf_op jit(solution)/shard_map/fmd,edh->fmeh/dot_general | solution.py:165
  157.4 1.0 fusion.145
  158.7 1.6 collective-permute-done.7
  160.7 0.9 reshape.184.sent_ref
  161.6 14.6 %shard_map.80 = (bf16[96,128]{1,0:T(8,128)(2,1)}, bf16[96,128]{1,0:T(8,128)(2,1)}) custom-call(bf16[16,96,128]{2,1,0:T(8,128)(2,1)} %reshape.184.sent_ref, bf16[96,128]{1,0:T(8,128)(2,1)} %copy-done.5), custom_call_target="tpu_custom_call" | custom-call | tf_op jit(solution)/shard_map/pallas_call | solution.py:118
  176.2 0.9 fusion.117
  178.1 10.3 %shard_map.81 = bf16[16,96,128]{2,1,0:T(8,128)(2,1)} custom-call(bf16[96,128]{1,0:T(8,128)(2,1)} %fusion.123.src_ref), custom_call_target="tpu_custom_call" | custom-call | tf_op jit(solution)/shard_map/pallas_call | solution.py:42
  188.7 1.9 collective-permute-done.8
  190.6 1.1 pad_maximum_fusion.4
  191.9 4.0 %fusion.14 = f32[32,4,4,256]{3,0,2,1:T(8,128)S(1)} fusion(bf16[1,4,3072,256]{3,2,1,0:T(8,128)(2,1)} %param.9, bf16[32,4,3072,1]{2,1,0,3:T(4,128)(2,1)S(1)} %bitcast.246), kind=kOutput, calls=%fused_computation.14 | convolution fusion | flops 805306368 | bytes 7602176 | tf_op jit(solution)/shard_map/fmd,edh->fmeh/dot_general | solution.py:164
  196.0 4.1 %fusion.90 = bf16[4,4,4,8,256]{4,3,2,1,0:T(8,128)(2,1)S(1)} fusion(bf16[1,4,3072,256]{3,2,1,0:T(8,128)(2,1)} %param.10, bf16[32,4,3072,1]{2,1,0,3:T(4,128)(2,1)S(1)} %bitcast.247, f32[32,4,4,256]{3,0,2,1:T(8,128)S(1)} %fusion.14, f32[32,4,4]{0,2,1:T(4,128)S(1)} %copy.176), kind=kOutput, calls=%fused_computation.46 | convolution fusion | flops 806223872 | bytes 7866368 | tf_op jit(solution)/shard_map/fmd,edh->fmeh/dot_general | solution.py:165
  200.1 1.0 fusion.146
  201.5 1.5 collective-permute-done.9
  203.4 0.9 reshape.187.sent_ref
  204.3 14.3 %shard_map.82 = (bf16[96,128]{1,0:T(8,128)(2,1)}, bf16[96,128]{1,0:T(8,128)(2,1)}) custom-call(bf16[16,96,128]{2,1,0:T(8,128)(2,1)} %reshape.187.sent_ref, bf16[96,128]{1,0:T(8,128)(2,1)} %copy-done.1), custom_call_target="tpu_custom_call" | custom-call | tf_op jit(solution)/shard_map/pallas_call | solution.py:118
  218.6 0.9 fusion.118
  220.6 10.3 %shard_map.83 = bf16[16,96,128]{2,1,0:T(8,128)(2,1)} custom-call(bf16[96,128]{1,0:T(8,128)(2,1)} %fusion.124.src_ref), custom_call_target="tpu_custom_call" | custom-call | tf_op jit(solution)/shard_map/pallas_call | solution.py:42
  231.0 1.8 collective-permute-done.10
  232.9 1.1 pad_maximum_fusion.5
  234.2 4.0 %fusion.12 = f32[32,4,4,256]{3,0,2,1:T(8,128)S(1)} fusion(bf16[1,4,3072,256]{3,2,1,0:T(8,128)(2,1)} %param.9, bf16[32,4,3072,1]{2,1,0,3:T(4,128)(2,1)S(1)} %bitcast.248), kind=kOutput, calls=%fused_computation.12 | convolution fusion | flops 805306368 | bytes 7602176 | tf_op jit(solution)/shard_map/fmd,edh->fmeh/dot_general | solution.py:164
  238.2 4.1 %fusion.93 = bf16[4,4,4,8,256]{4,3,2,1,0:T(8,128)(2,1)S(1)} fusion(bf16[1,4,3072,256]{3,2,1,0:T(8,128)(2,1)} %param.10, bf16[32,4,3072,1]{2,1,0,3:T(4,128)(2,1)S(1)} %bitcast.249, f32[32,4,4,256]{3,0,2,1:T(8,128)S(1)} %fusion.12, f32[32,4,4]{0,2,1:T(4,128)S(1)} %copy.181), kind=kOutput, calls=%fused_computation.47 | convolution fusion | flops 806223872 | bytes 7866368 | tf_op jit(solution)/shard_map/fmd,edh->fmeh/dot_general | solution.py:165
  242.4 1.0 fusion.147
  243.7 1.5 collective-permute-done.11
  245.6 0.9 reshape.190.sent_ref
  246.5 14.5 %shard_map.84 = (bf16[96,128]{1,0:T(8,128)(2,1)}, bf16[96,128]{1,0:T(8,128)(2,1)}) custom-call(bf16[16,96,128]{2,1,0:T(8,128)(2,1)} %reshape.190.sent_ref, bf16[96,128]{1,0:T(8,128)(2,1)} %copy-done.2), custom_call_target="tpu_custom_call" | custom-call | tf_op jit(solution)/shard_map/pallas_call | solution.py:118
  261.0 0.8 fusion.125
  (147 shorter events, 12.3 us)
Async XLA Ops:
  16.2 2.0 collective-permute-start
  19.4 8.2 %slice-start = ((s8[6291456]{0:T(1024)(128)(4,1)}), s8[4194304]{0:T(1024)(128)(4,1)S(1)}, s32[]{:S(2)}) async-start(s8[6291456]{0:T(1024)(128)(4,1)} %bitcast.214), calls=%async_computation | async-start | bytes 8388608
  23.5 4.2 %slice-start.1 = ((s8[6291456]{0:T(1024)(128)(4,1)}), s8[2097152]{0:T(1024)(128)(4,1)S(1)}, s32[]{:S(2)}) async-start(s8[6291456]{0:T(1024)(128)(4,1)} %bitcast.214), calls=%async_computation.1 | async-start | bytes 4194304
  27.6 21.0 %copy-start = (f32[1,3072]{1,0:T(1,128)S(1)}, f32[1,3072]{1,0:T(1,128)}, u32[]{:S(2)}) copy-start(f32[1,3072]{1,0:T(1,128)} %param.8) | copy-start | bytes 36868
  28.7 1.8 collective-permute-start.1
  48.3 18.9 %copy-start.3 = (bf16[96,128]{1,0:T(8,128)(2,1)}, bf16[96,128]{1,0:T(8,128)(2,1)S(1)}, u32[]{:S(2)}) copy-start(bf16[96,128]{1,0:T(8,128)(2,1)S(1)} %get-tuple-element.36.current_ref) | copy-start | bytes 73732
  59.9 2.0 collective-permute-start.2
  63.2 8.2 %slice-start.2 = ((s8[6291456]{0:T(1024)(128)(4,1)}), s8[4194304]{0:T(1024)(128)(4,1)S(1)}, s32[]{:S(2)}) async-start(s8[6291456]{0:T(1024)(128)(4,1)} %bitcast.217), calls=%async_computation.2 | async-start | bytes 8388608
  67.2 4.2 %slice-start.3 = ((s8[6291456]{0:T(1024)(128)(4,1)}), s8[2097152]{0:T(1024)(128)(4,1)S(1)}, s32[]{:S(2)}) async-start(s8[6291456]{0:T(1024)(128)(4,1)} %bitcast.217), calls=%async_computation.3 | async-start | bytes 4194304
  72.4 1.8 collective-permute-start.3
  91.6 18.6 %copy-start.4 = (bf16[96,128]{1,0:T(8,128)(2,1)}, bf16[96,128]{1,0:T(8,128)(2,1)S(1)}, u32[]{:S(2)}) copy-start(bf16[96,128]{1,0:T(8,128)(2,1)S(1)} %get-tuple-element.34.current_ref) | copy-start | bytes 73732
  102.9 2.0 collective-permute-start.4
  106.1 8.2 %slice-start.4 = ((s8[6291456]{0:T(1024)(128)(4,1)}), s8[4194304]{0:T(1024)(128)(4,1)S(1)}, s32[]{:S(2)}) async-start(s8[6291456]{0:T(1024)(128)(4,1)} %bitcast.220), calls=%async_computation.4 | async-start | bytes 8388608
  110.2 4.2 %slice-start.5 = ((s8[6291456]{0:T(1024)(128)(4,1)}), s8[2097152]{0:T(1024)(128)(4,1)S(1)}, s32[]{:S(2)}) async-start(s8[6291456]{0:T(1024)(128)(4,1)} %bitcast.220), calls=%async_computation.5 | async-start | bytes 4194304
  115.4 1.8 collective-permute-start.5
  134.5 18.8 %copy-start.5 = (bf16[96,128]{1,0:T(8,128)(2,1)}, bf16[96,128]{1,0:T(8,128)(2,1)S(1)}, u32[]{:S(2)}) copy-start(bf16[96,128]{1,0:T(8,128)(2,1)S(1)} %get-tuple-element.32.current_ref) | copy-start | bytes 73732
  145.9 2.0 collective-permute-start.6
  149.2 8.2 %slice-start.6 = ((s8[6291456]{0:T(1024)(128)(4,1)}), s8[4194304]{0:T(1024)(128)(4,1)S(1)}, s32[]{:S(2)}) async-start(s8[6291456]{0:T(1024)(128)(4,1)} %bitcast.223), calls=%async_computation.6 | async-start | bytes 8388608
  153.2 4.2 %slice-start.7 = ((s8[6291456]{0:T(1024)(128)(4,1)}), s8[2097152]{0:T(1024)(128)(4,1)S(1)}, s32[]{:S(2)}) async-start(s8[6291456]{0:T(1024)(128)(4,1)} %bitcast.223), calls=%async_computation.7 | async-start | bytes 4194304
  158.5 1.8 collective-permute-start.7
  177.0 18.9 %copy-start.1 = (bf16[96,128]{1,0:T(8,128)(2,1)}, bf16[96,128]{1,0:T(8,128)(2,1)S(1)}, u32[]{:S(2)}) copy-start(bf16[96,128]{1,0:T(8,128)(2,1)S(1)} %get-tuple-element.30.current_ref) | copy-start | bytes 73732
  188.4 2.2 collective-permute-start.8
  191.9 8.2 %slice-start.8 = ((s8[6291456]{0:T(1024)(128)(4,1)}), s8[4194304]{0:T(1024)(128)(4,1)S(1)}, s32[]{:S(2)}) async-start(s8[6291456]{0:T(1024)(128)(4,1)} %bitcast.226), calls=%async_computation.8 | async-start | bytes 8388608
  195.9 4.2 %slice-start.9 = ((s8[6291456]{0:T(1024)(128)(4,1)}), s8[2097152]{0:T(1024)(128)(4,1)S(1)}, s32[]{:S(2)}) async-start(s8[6291456]{0:T(1024)(128)(4,1)} %bitcast.226), calls=%async_computation.9 | async-start | bytes 4194304
  200.0 1.4 copy-start.6
  200.1 30.9 %copy-start.7 = (bf16[96,128]{1,0:T(8,128)(2,1)S(1)}, bf16[96,128]{1,0:T(8,128)(2,1)}, u32[]{:S(2)}) copy-start(bf16[96,128]{1,0:T(8,128)(2,1)} %get-tuple-element.18) | copy-start | bytes 73732
  200.1 30.9 %copy-start.8 = (bf16[96,128]{1,0:T(8,128)(2,1)S(1)}, bf16[96,128]{1,0:T(8,128)(2,1)}, u32[]{:S(2)}) copy-start(bf16[96,128]{1,0:T(8,128)(2,1)} %get-tuple-element.20) | copy-start | bytes 73732
  201.2 1.8 collective-permute-start.9
  219.5 18.7 %copy-start.2 = (bf16[96,128]{1,0:T(8,128)(2,1)}, bf16[96,128]{1,0:T(8,128)(2,1)S(1)}, u32[]{:S(2)}) copy-start(bf16[96,128]{1,0:T(8,128)(2,1)S(1)} %get-tuple-element.28.current_ref) | copy-start | bytes 73732
  230.9 2.0 collective-permute-start.10
  234.1 8.2 %slice-start.10 = ((s8[6291456]{0:T(1024)(128)(4,1)}), s8[4194304]{0:T(1024)(128)(4,1)S(1)}, s32[]{:S(2)}) async-start(s8[6291456]{0:T(1024)(128)(4,1)} %bitcast.229), calls=%async_computation.10 | async-start | bytes 8388608
  238.2 4.2 %slice-start.11 = ((s8[6291456]{0:T(1024)(128)(4,1)}), s8[2097152]{0:T(1024)(128)(4,1)S(1)}, s32[]{:S(2)}) async-start(s8[6291456]{0:T(1024)(128)(4,1)} %bitcast.229), calls=%async_computation.11 | async-start | bytes 4194304
  242.3 1.3 copy-start.9
  242.3 1.4 copy-start.10
  243.4 1.8 collective-permute-start.11

commit v11 on v8

--- a/solution.py
+++ b/solution.py
@@ -8,6 +8,21 @@
 MESH = pl.DeviceIdType.MESH
 
 
+def farthest_first(chips):
+    side = int(round(chips ** 0.5))
+    hops = lambda d: min(d, side - d)
+    offsets = [(dx, dz) for dx in range(side) for dz in range(side) if (dx, dz) != (0, 0)]
+    offsets.sort(key=lambda o: -(hops(o[0]) + hops(o[1])))
+    return side, [(0, 0)] + offsets
+
+
+def torus_peer(chip, j, chips):
+    side, offsets = farthest_first(chips)
+    dx, dz = offsets[j]
+    x, z = chip // side, chip % side
+    return lax.rem(x + dx, side) * side + lax.rem(z + dz, side)
+
+
 def exchange(src, chips, same, collective_id):
     rows, width = src.shape[-2:]
 
@@ -17,14 +32,14 @@
         chip, core = me // 2, me % 2
         barrier = pltpu.get_barrier_semaphore()
         for j in range(1, chips):
-            peer = lax.rem(chip + j, chips)
+            peer = torus_peer(chip, j, chips)
             pl.semaphore_signal(barrier, 1, device_id=(section, peer * 2 + core), device_id_type=MESH)
         pl.semaphore_wait(barrier, chips - 1)
         local = pltpu.make_async_copy(src_ref if same else src_ref.at[chip], out_ref.at[chip], local_sem)
         local.start()
         copies = []
         for j in range(1, chips):
-            peer = lax.rem(chip + j, chips)
+            peer = torus_peer(chip, j, chips)
             copy = pltpu.make_async_remote_copy(
                 src_ref=src_ref if same else src_ref.at[peer],
                 dst_ref=out_ref.at[chip],
@@ -63,7 +78,7 @@
         chip, core = me // 2, me % 2
         barrier = pltpu.get_barrier_semaphore()
         for j in range(1, chips):
-            peer = lax.rem(chip + j, chips)
+            peer = torus_peer(chip, j, chips)
             pl.semaphore_signal(barrier, 1, device_id=(section, peer * 2 + core), device_id_type=MESH)
 
         @pl.when(section > 0)
@@ -77,7 +92,7 @@
         local.start()
         copies = []
         for j in range(1, chips):
-            peer = lax.rem(chip + j, chips)
+            peer = torus_peer(chip, j, chips)
             copy = pltpu.make_async_remote_copy(
                 src_ref=sent_ref.at[peer],
                 dst_ref=pieces.at[chip],

time: 264 us -> 254 us (0.962)
  Pallas kernels: 154 us -> 144 us
    pallas_call x6, Pallas kernels: 89.2 us -> 83.5 us  [reduce_relay(): pl.pallas_call(kernel, out_shape=(jax.ShapeDtypeStruct((rows, width), cur...]
    pallas_call x6, Pallas kernels: 65.1 us -> 60.6 us  [exchange(): pl.pallas_call(kernel, out_shape=jax.ShapeDtypeStruct((chips, rows, width...]
where the time goes in v11:
time: 254 us; the launch traced here: 252 us
  Pallas kernels  144 us (57%)
  matrix products  54.6 us (21%)
  waiting for transfers between devices  19.2 us (8%)
  other arithmetic  18.7 us (7%)
  local copies, waits for them, and re-layouts  12.5 us (5%)
    pallas_call x6, Pallas kernels, reduce_relay(): pl.pallas_call(kernel, out_shape=(jax.ShapeDtypeStruct((rows, width), cur...  83.5 us
    pallas_call x6, Pallas kernels, exchange(): pl.pallas_call(kernel, out_shape=jax.ShapeDtypeStruct((chips, rows, width...  60.6 us
    dot_general x6, matrix products, expert_mix(): jnp.einsum('fmd,edh->fmeh', rows, up_w, preferred_element_type=jnp.float32)  24.5 us
    dot_general x6, matrix products, expert_mix(): jnp.einsum('fmd,edh->fmeh', rows, gate_w, preferred_element_type=jnp.floa...  24 us
    ppermute x12, waiting for transfers between devices, sibling(): return lax.ppermute(array, axis, [(i, i ^ 1) for i in range(devices)])  19.2 us
    concatenate x6, other arithmetic, on_device(): jnp.concatenate([near, sibling(near, 'fsdp')], axis=0)  6.39 us
    dot_general x6, matrix products, expert_mix(): jnp.einsum('fmk,kd->fmd', gated, down, preferred_element_type=jnp.float32)  5.97 us
    reshape x6, local copies, waits for them, and re-layouts, on_device(): sent = chip_sum.astype(jnp.bfloat16).reshape(chips, lanes, 128)  5.4 us
  transfers between devices with their start and end apart: 12, of which 12 were waited for; matrix products, arithmetic and copies ran while one was open for 1% of the time, Pallas kernels for 0%

profile of v11, /device:TPU:24, one launch (start us, length us, event | category | flops | bytes accessed | tf_op | source)
XLA Modules:
  0.0 252.3 jit_solution(9756672153414073017)
XLA Ops:
  0.0 0.9 reshape.169
  1.4 1.4 fusion.119
  2.8 13.1 %shard_map.73 = bf16[16,96,128]{2,1,0:T(8,128)(2,1)} custom-call(bf16[96,128]{1,0:T(8,128)(2,1)} %get-tuple-element.37.src_ref), custom_call_target="tpu_custom_call" | custom-call | tf_op jit(solution)/shard_map/pallas_call | solution.py:57
  16.1 0.7 select_reduce_fusion
  18.0 1.1 pad_maximum_fusion
  19.2 4.0 %fusion.22 = f32[32,4,4,256]{3,0,2,1:T(8,128)S(1)} fusion(bf16[1,4,3072,256]{3,2,1,0:T(8,128)(2,1)} %param.9, bf16[32,4,3072,1]{2,1,0,3:T(4,128)(2,1)S(1)} %bitcast.238), kind=kOutput, calls=%fused_computation.22 | convolution fusion | flops 805306368 | bytes 7602176 | tf_op jit(solution)/shard_map/fmd,edh->fmeh/dot_general | solution.py:178
  23.3 4.1 %fusion.78 = bf16[4,4,4,8,256]{4,3,2,1,0:T(8,128)(2,1)S(1)} fusion(bf16[1,4,3072,256]{3,2,1,0:T(8,128)(2,1)} %param.10, bf16[32,4,3072,1]{2,1,0,3:T(4,128)(2,1)S(1)} %bitcast.239, f32[32,4,4,256]{3,0,2,1:T(8,128)S(1)} %fusion.22, f32[32,4,4]{0,2,1:T(4,128)S(1)} %copy.156), kind=kOutput, calls=%fused_computation.42 | convolution fusion | flops 806223872 | bytes 7866368 | tf_op jit(solution)/shard_map/fmd,edh->fmeh/dot_general | solution.py:179
  27.4 1.0 fusion.142
  28.7 1.6 collective-permute-done.1
  30.7 0.9 reshape.175.sent_ref
  31.6 14.6 %shard_map.74 = (bf16[96,128]{1,0:T(8,128)(2,1)}, bf16[96,128]{1,0:T(8,128)(2,1)}) custom-call(bf16[16,96,128]{2,1,0:T(8,128)(2,1)} %reshape.175.sent_ref, bf16[96,128]{1,0:T(8,128)(2,1)} %get-tuple-element.38.current_ref), custom_call_target="tpu_custom_call" | custom-call | tf_op jit(solution)/shard_map/pallas_call | solution.py:132
  46.2 0.9 fusion.114
  48.2 9.6 %shard_map.75 = bf16[16,96,128]{2,1,0:T(8,128)(2,1)} custom-call(bf16[96,128]{1,0:T(8,128)(2,1)} %fusion.120.src_ref), custom_call_target="tpu_custom_call" | custom-call | tf_op jit(solution)/shard_map/pallas_call | solution.py:57
  57.8 1.9 collective-permute-done.2
  59.7 1.1 pad_maximum_fusion.1
  61.0 4.0 %fusion.20 = f32[32,4,4,256]{3,0,2,1:T(8,128)S(1)} fusion(bf16[1,4,3072,256]{3,2,1,0:T(8,128)(2,1)} %param.9, bf16[32,4,3072,1]{2,1,0,3:T(4,128)(2,1)S(1)} %bitcast.240), kind=kOutput, calls=%fused_computation.20 | convolution fusion | flops 805306368 | bytes 7602176 | tf_op jit(solution)/shard_map/fmd,edh->fmeh/dot_general | solution.py:178
  65.0 4.1 %fusion.81 = bf16[4,4,4,8,256]{4,3,2,1,0:T(8,128)(2,1)S(1)} fusion(bf16[1,4,3072,256]{3,2,1,0:T(8,128)(2,1)} %param.10, bf16[32,4,3072,1]{2,1,0,3:T(4,128)(2,1)S(1)} %bitcast.241, f32[32,4,4,256]{3,0,2,1:T(8,128)S(1)} %fusion.20, f32[32,4,4]{0,2,1:T(4,128)S(1)} %copy.161), kind=kOutput, calls=%fused_computation.43 | convolution fusion | flops 806223872 | bytes 7866368 | tf_op jit(solution)/shard_map/fmd,edh->fmeh/dot_general | solution.py:179
  69.2 1.0 fusion.143
  70.5 1.6 collective-permute-done.3
  72.5 0.9 reshape.178.sent_ref
  73.4 14.2 %shard_map.76 = (bf16[96,128]{1,0:T(8,128)(2,1)}, bf16[96,128]{1,0:T(8,128)(2,1)}) custom-call(bf16[16,96,128]{2,1,0:T(8,128)(2,1)} %reshape.178.sent_ref, bf16[96,128]{1,0:T(8,128)(2,1)} %copy-done.3), custom_call_target="tpu_custom_call" | custom-call | tf_op jit(solution)/shard_map/pallas_call | solution.py:132
  87.6 0.9 fusion.115
  88.8 0.7 fusion.121.src_ref
  89.5 9.5 %shard_map.77 = bf16[16,96,128]{2,1,0:T(8,128)(2,1)} custom-call(bf16[96,128]{1,0:T(8,128)(2,1)} %fusion.121.src_ref), custom_call_target="tpu_custom_call" | custom-call | tf_op jit(solution)/shard_map/pallas_call | solution.py:57
  99.1 1.9 collective-permute-done.4
  101.0 1.1 pad_maximum_fusion.2
  102.3 4.0 %fusion.18 = f32[32,4,4,256]{3,0,2,1:T(8,128)S(1)} fusion(bf16[1,4,3072,256]{3,2,1,0:T(8,128)(2,1)} %param.9, bf16[32,4,3072,1]{2,1,0,3:T(4,128)(2,1)S(1)} %bitcast.242), kind=kOutput, calls=%fused_computation.18 | convolution fusion | flops 805306368 | bytes 7602176 | tf_op jit(solution)/shard_map/fmd,edh->fmeh/dot_general | solution.py:178
  106.3 4.1 %fusion.84 = bf16[4,4,4,8,256]{4,3,2,1,0:T(8,128)(2,1)S(1)} fusion(bf16[1,4,3072,256]{3,2,1,0:T(8,128)(2,1)} %param.10, bf16[32,4,3072,1]{2,1,0,3:T(4,128)(2,1)S(1)} %bitcast.243, f32[32,4,4,256]{3,0,2,1:T(8,128)S(1)} %fusion.18, f32[32,4,4]{0,2,1:T(4,128)S(1)} %copy.166), kind=kOutput, calls=%fused_computation.44 | convolution fusion | flops 806223872 | bytes 7866368 | tf_op jit(solution)/shard_map/fmd,edh->fmeh/dot_general | solution.py:179
  110.5 1.0 fusion.144
  111.8 1.6 collective-permute-done.5
  113.8 0.9 reshape.181.sent_ref
  114.7 14.2 %shard_map.78 = (bf16[96,128]{1,0:T(8,128)(2,1)}, bf16[96,128]{1,0:T(8,128)(2,1)}) custom-call(bf16[16,96,128]{2,1,0:T(8,128)(2,1)} %reshape.181.sent_ref, bf16[96,128]{1,0:T(8,128)(2,1)} %copy-done.4), custom_call_target="tpu_custom_call" | custom-call | tf_op jit(solution)/shard_map/pallas_call | solution.py:132
  128.9 0.9 fusion.116
  130.1 0.7 fusion.122.src_ref
  130.8 9.5 %shard_map.79 = bf16[16,96,128]{2,1,0:T(8,128)(2,1)} custom-call(bf16[96,128]{1,0:T(8,128)(2,1)} %fusion.122.src_ref), custom_call_target="tpu_custom_call" | custom-call | tf_op jit(solution)/shard_map/pallas_call | solution.py:57
  140.4 1.9 collective-permute-done.6
  142.3 1.1 pad_maximum_fusion.3
  143.6 4.0 %fusion.16 = f32[32,4,4,256]{3,0,2,1:T(8,128)S(1)} fusion(bf16[1,4,3072,256]{3,2,1,0:T(8,128)(2,1)} %param.9, bf16[32,4,3072,1]{2,1,0,3:T(4,128)(2,1)S(1)} %bitcast.244), kind=kOutput, calls=%fused_computation.16 | convolution fusion | flops 805306368 | bytes 7602176 | tf_op jit(solution)/shard_map/fmd,edh->fmeh/dot_general | solution.py:178
  147.6 4.1 %fusion.87 = bf16[4,4,4,8,256]{4,3,2,1,0:T(8,128)(2,1)S(1)} fusion(bf16[1,4,3072,256]{3,2,1,0:T(8,128)(2,1)} %param.10, bf16[32,4,3072,1]{2,1,0,3:T(4,128)(2,1)S(1)} %bitcast.245, f32[32,4,4,256]{3,0,2,1:T(8,128)S(1)} %fusion.16, f32[32,4,4]{0,2,1:T(4,128)S(1)} %copy.171), kind=kOutput, calls=%fused_computation.45 | convolution fusion | flops 806223872 | bytes 7866368 | tf_op jit(solution)/shard_map/fmd,edh->fmeh/dot_general | solution.py:179
  151.8 1.0 fusion.145
  153.1 1.6 collective-permute-done.7
  155.1 0.9 reshape.184.sent_ref
  156.0 13.5 %shard_map.80 = (bf16[96,128]{1,0:T(8,128)(2,1)}, bf16[96,128]{1,0:T(8,128)(2,1)}) custom-call(bf16[16,96,128]{2,1,0:T(8,128)(2,1)} %reshape.184.sent_ref, bf16[96,128]{1,0:T(8,128)(2,1)} %copy-done.5), custom_call_target="tpu_custom_call" | custom-call | tf_op jit(solution)/shard_map/pallas_call | solution.py:132
  169.5 0.9 fusion.117
  171.4 9.5 %shard_map.81 = bf16[16,96,128]{2,1,0:T(8,128)(2,1)} custom-call(bf16[96,128]{1,0:T(8,128)(2,1)} %fusion.123.src_ref), custom_call_target="tpu_custom_call" | custom-call | tf_op jit(solution)/shard_map/pallas_call | solution.py:57
  181.2 1.9 collective-permute-done.8
  183.1 1.1 pad_maximum_fusion.4
  184.4 4.0 %fusion.14 = f32[32,4,4,256]{3,0,2,1:T(8,128)S(1)} fusion(bf16[1,4,3072,256]{3,2,1,0:T(8,128)(2,1)} %param.9, bf16[32,4,3072,1]{2,1,0,3:T(4,128)(2,1)S(1)} %bitcast.246), kind=kOutput, calls=%fused_computation.14 | convolution fusion | flops 805306368 | bytes 7602176 | tf_op jit(solution)/shard_map/fmd,edh->fmeh/dot_general | solution.py:178
  188.4 4.1 %fusion.90 = bf16[4,4,4,8,256]{4,3,2,1,0:T(8,128)(2,1)S(1)} fusion(bf16[1,4,3072,256]{3,2,1,0:T(8,128)(2,1)} %param.10, bf16[32,4,3072,1]{2,1,0,3:T(4,128)(2,1)S(1)} %bitcast.247, f32[32,4,4,256]{3,0,2,1:T(8,128)S(1)} %fusion.14, f32[32,4,4]{0,2,1:T(4,128)S(1)} %copy.176), kind=kOutput, calls=%fused_computation.46 | convolution fusion | flops 806223872 | bytes 7866368 | tf_op jit(solution)/shard_map/fmd,edh->fmeh/dot_general | solution.py:179
  192.6 1.0 fusion.146
  194.0 1.5 collective-permute-done.9
  195.9 0.9 reshape.187.sent_ref
  196.8 13.5 %shard_map.82 = (bf16[96,128]{1,0:T(8,128)(2,1)}, bf16[96,128]{1,0:T(8,128)(2,1)}) custom-call(bf16[16,96,128]{2,1,0:T(8,128)(2,1)} %reshape.187.sent_ref, bf16[96,128]{1,0:T(8,128)(2,1)} %copy-done.1), custom_call_target="tpu_custom_call" | custom-call | tf_op jit(solution)/shard_map/pallas_call | solution.py:132
  210.3 0.9 fusion.118
  212.2 9.5 %shard_map.83 = bf16[16,96,128]{2,1,0:T(8,128)(2,1)} custom-call(bf16[96,128]{1,0:T(8,128)(2,1)} %fusion.124.src_ref), custom_call_target="tpu_custom_call" | custom-call | tf_op jit(solution)/shard_map/pallas_call | solution.py:57
  221.9 1.8 collective-permute-done.10
  223.8 1.1 pad_maximum_fusion.5
  225.0 4.0 %fusion.12 = f32[32,4,4,256]{3,0,2,1:T(8,128)S(1)} fusion(bf16[1,4,3072,256]{3,2,1,0:T(8,128)(2,1)} %param.9, bf16[32,4,3072,1]{2,1,0,3:T(4,128)(2,1)S(1)} %bitcast.248), kind=kOutput, calls=%fused_computation.12 | convolution fusion | flops 805306368 | bytes 7602176 | tf_op jit(solution)/shard_map/fmd,edh->fmeh/dot_general | solution.py:178
  229.1 4.1 %fusion.93 = bf16[4,4,4,8,256]{4,3,2,1,0:T(8,128)(2,1)S(1)} fusion(bf16[1,4,3072,256]{3,2,1,0:T(8,128)(2,1)} %param.10, bf16[32,4,3072,1]{2,1,0,3:T(4,128)(2,1)S(1)} %bitcast.249, f32[32,4,4,256]{3,0,2,1:T(8,128)S(1)} %fusion.12, f32[32,4,4]{0,2,1:T(4,128)S(1)} %copy.181), kind=kOutput, calls=%fused_computation.47 | convolution fusion | flops 806223872 | bytes 7866368 | tf_op jit(solution)/shard_map/fmd,edh->fmeh/dot_general | solution.py:179
  233.2 1.0 fusion.147
  234.6 1.5 collective-permute-done.11
  236.5 0.9 reshape.190.sent_ref
  237.4 13.5 %shard_map.84 = (bf16[96,128]{1,0:T(8,128)(2,1)}, bf16[96,128]{1,0:T(8,128)(2,1)}) custom-call(bf16[16,96,128]{2,1,0:T(8,128)(2,1)} %reshape.190.sent_ref, bf16[96,128]{1,0:T(8,128)(2,1)} %copy-done.2), custom_call_target="tpu_custom_call" | custom-call | tf_op jit(solution)/shard_map/pallas_call | solution.py:132
  250.9 0.8 fusion.125
  (147 shorter events, 12.3 us)
Async XLA Ops:
  16.0 2.0 collective-permute-start
  19.2 8.2 %slice-start = ((s8[6291456]{0:T(1024)(128)(4,1)}), s8[4194304]{0:T(1024)(128)(4,1)S(1)}, s32[]{:S(2)}) async-start(s8[6291456]{0:T(1024)(128)(4,1)} %bitcast.214), calls=%async_computation | async-start | bytes 8388608
  23.3 4.2 %slice-start.1 = ((s8[6291456]{0:T(1024)(128)(4,1)}), s8[2097152]{0:T(1024)(128)(4,1)S(1)}, s32[]{:S(2)}) async-start(s8[6291456]{0:T(1024)(128)(4,1)} %bitcast.214), calls=%async_computation.1 | async-start | bytes 4194304
  27.4 20.0 %copy-start = (f32[1,3072]{1,0:T(1,128)S(1)}, f32[1,3072]{1,0:T(1,128)}, u32[]{:S(2)}) copy-start(f32[1,3072]{1,0:T(1,128)} %param.8) | copy-start | bytes 36868
  28.5 1.8 collective-permute-start.1
  47.1 18.0 %copy-start.3 = (bf16[96,128]{1,0:T(8,128)(2,1)}, bf16[96,128]{1,0:T(8,128)(2,1)S(1)}, u32[]{:S(2)}) copy-start(bf16[96,128]{1,0:T(8,128)(2,1)S(1)} %get-tuple-element.36.current_ref) | copy-start | bytes 73732
  57.7 2.0 collective-permute-start.2
  61.0 8.2 %slice-start.2 = ((s8[6291456]{0:T(1024)(128)(4,1)}), s8[4194304]{0:T(1024)(128)(4,1)S(1)}, s32[]{:S(2)}) async-start(s8[6291456]{0:T(1024)(128)(4,1)} %bitcast.217), calls=%async_computation.2 | async-start | bytes 8388608
  65.0 4.1 %slice-start.3 = ((s8[6291456]{0:T(1024)(128)(4,1)}), s8[2097152]{0:T(1024)(128)(4,1)S(1)}, s32[]{:S(2)}) async-start(s8[6291456]{0:T(1024)(128)(4,1)} %bitcast.217), calls=%async_computation.3 | async-start | bytes 4194304
  70.2 1.8 collective-permute-start.3
  88.4 17.9 %copy-start.4 = (bf16[96,128]{1,0:T(8,128)(2,1)}, bf16[96,128]{1,0:T(8,128)(2,1)S(1)}, u32[]{:S(2)}) copy-start(bf16[96,128]{1,0:T(8,128)(2,1)S(1)} %get-tuple-element.34.current_ref) | copy-start | bytes 73732
  99.0 2.0 collective-permute-start.4
  102.3 8.2 %slice-start.4 = ((s8[6291456]{0:T(1024)(128)(4,1)}), s8[4194304]{0:T(1024)(128)(4,1)S(1)}, s32[]{:S(2)}) async-start(s8[6291456]{0:T(1024)(128)(4,1)} %bitcast.220), calls=%async_computation.4 | async-start | bytes 8388608
  106.3 4.2 %slice-start.5 = ((s8[6291456]{0:T(1024)(128)(4,1)}), s8[2097152]{0:T(1024)(128)(4,1)S(1)}, s32[]{:S(2)}) async-start(s8[6291456]{0:T(1024)(128)(4,1)} %bitcast.220), calls=%async_computation.5 | async-start | bytes 4194304
  111.6 1.8 collective-permute-start.5
  129.7 17.9 %copy-start.5 = (bf16[96,128]{1,0:T(8,128)(2,1)}, bf16[96,128]{1,0:T(8,128)(2,1)S(1)}, u32[]{:S(2)}) copy-start(bf16[96,128]{1,0:T(8,128)(2,1)S(1)} %get-tuple-element.32.current_ref) | copy-start | bytes 73732
  140.3 2.0 collective-permute-start.6
  143.6 8.2 %slice-start.6 = ((s8[6291456]{0:T(1024)(128)(4,1)}), s8[4194304]{0:T(1024)(128)(4,1)S(1)}, s32[]{:S(2)}) async-start(s8[6291456]{0:T(1024)(128)(4,1)} %bitcast.223), calls=%async_computation.6 | async-start | bytes 8388608
  147.6 4.2 %slice-start.7 = ((s8[6291456]{0:T(1024)(128)(4,1)}), s8[2097152]{0:T(1024)(128)(4,1)S(1)}, s32[]{:S(2)}) async-start(s8[6291456]{0:T(1024)(128)(4,1)} %bitcast.223), calls=%async_computation.7 | async-start | bytes 4194304
  152.9 1.8 collective-permute-start.7
  170.3 18.1 %copy-start.1 = (bf16[96,128]{1,0:T(8,128)(2,1)}, bf16[96,128]{1,0:T(8,128)(2,1)S(1)}, u32[]{:S(2)}) copy-start(bf16[96,128]{1,0:T(8,128)(2,1)S(1)} %get-tuple-element.30.current_ref) | copy-start | bytes 73732
  180.9 2.2 collective-permute-start.8
  184.4 8.2 %slice-start.8 = ((s8[6291456]{0:T(1024)(128)(4,1)}), s8[4194304]{0:T(1024)(128)(4,1)S(1)}, s32[]{:S(2)}) async-start(s8[6291456]{0:T(1024)(128)(4,1)} %bitcast.226), calls=%async_computation.8 | async-start | bytes 8388608
  188.4 4.2 %slice-start.9 = ((s8[6291456]{0:T(1024)(128)(4,1)}), s8[2097152]{0:T(1024)(128)(4,1)S(1)}, s32[]{:S(2)}) async-start(s8[6291456]{0:T(1024)(128)(4,1)} %bitcast.226), calls=%async_computation.9 | async-start | bytes 4194304
  192.5 1.4 copy-start.6
  192.6 29.2 %copy-start.7 = (bf16[96,128]{1,0:T(8,128)(2,1)S(1)}, bf16[96,128]{1,0:T(8,128)(2,1)}, u32[]{:S(2)}) copy-start(bf16[96,128]{1,0:T(8,128)(2,1)} %get-tuple-element.18) | copy-start | bytes 73732
  192.6 29.3 %copy-start.8 = (bf16[96,128]{1,0:T(8,128)(2,1)S(1)}, bf16[96,128]{1,0:T(8,128)(2,1)}, u32[]{:S(2)}) copy-start(bf16[96,128]{1,0:T(8,128)(2,1)} %get-tuple-element.20) | copy-start | bytes 73732
  193.7 1.8 collective-permute-start.9
  211.2 17.9 %copy-start.2 = (bf16[96,128]{1,0:T(8,128)(2,1)}, bf16[96,128]{1,0:T(8,128)(2,1)S(1)}, u32[]{:S(2)}) copy-start(bf16[96,128]{1,0:T(8,128)(2,1)S(1)} %get-tuple-element.28.current_ref) | copy-start | bytes 73732
  221.7 2.0 collective-permute-start.10
  225.0 8.2 %slice-start.10 = ((s8[6291456]{0:T(1024)(128)(4,1)}), s8[4194304]{0:T(1024)(128)(4,1)S(1)}, s32[]{:S(2)}) async-start(s8[6291456]{0:T(1024)(128)(4,1)} %bitcast.229), calls=%async_computation.10 | async-start | bytes 8388608
  229.0 4.2 %slice-start.11 = ((s8[6291456]{0:T(1024)(128)(4,1)}), s8[2097152]{0:T(1024)(128)(4,1)S(1)}, s32[]{:S(2)}) async-start(s8[6291456]{0:T(1024)(128)(4,1)} %bitcast.229), calls=%async_computation.11 | async-start | bytes 4194304
  233.2 1.3 copy-start.9
  233.2 1.4 copy-start.10
  234.3 1.8 collective-permute-start.11

commit v12 on v11

--- a/solution.py
+++ b/solution.py
@@ -36,7 +36,6 @@
             pl.semaphore_signal(barrier, 1, device_id=(section, peer * 2 + core), device_id_type=MESH)
         pl.semaphore_wait(barrier, chips - 1)
         local = pltpu.make_async_copy(src_ref if same else src_ref.at[chip], out_ref.at[chip], local_sem)
-        local.start()
         copies = []
         for j in range(1, chips):
             peer = torus_peer(chip, j, chips)
@@ -50,6 +49,7 @@
             )
             copy.start()
             copies.append(copy)
+        local.start()
         local.wait()
         for copy in copies:
             copy.wait()
@@ -89,7 +89,6 @@
         pl.semaphore_wait(barrier, chips - 1 + has_next)
 
         local = pltpu.make_async_copy(sent_ref.at[chip], pieces.at[chip], local_sem)
-        local.start()
         copies = []
         for j in range(1, chips):
             peer = torus_peer(chip, j, chips)
@@ -103,6 +102,7 @@
             )
             copy.start()
             copies.append(copy)
+        local.start()
         local.wait()
         for copy in copies:
             copy.wait()

time: 254 us -> 254 us (level)
  no operation moved by 1% of the time
where the time goes in v12:
time: 254 us; the launch traced here: 252 us
  Pallas kernels  144 us (57%)
  matrix products  54.5 us (21%)
  waiting for transfers between devices  19.2 us (8%)
  other arithmetic  18.7 us (7%)
  local copies, waits for them, and re-layouts  12.5 us (5%)
    pallas_call x6, Pallas kernels, reduce_relay(): pl.pallas_call(kernel, out_shape=(jax.ShapeDtypeStruct((rows, width), cur...  83.5 us
    pallas_call x6, Pallas kernels, exchange(): pl.pallas_call(kernel, out_shape=jax.ShapeDtypeStruct((chips, rows, width...  60.7 us
    dot_general x6, matrix products, expert_mix(): jnp.einsum('fmd,edh->fmeh', rows, up_w, preferred_element_type=jnp.float32)  24.5 us
    dot_general x6, matrix products, expert_mix(): jnp.einsum('fmd,edh->fmeh', rows, gate_w, preferred_element_type=jnp.floa...  24 us
    ppermute x12, waiting for transfers between devices, sibling(): return lax.ppermute(array, axis, [(i, i ^ 1) for i in range(devices)])  19.2 us
    concatenate x6, other arithmetic, on_device(): jnp.concatenate([near, sibling(near, 'fsdp')], axis=0)  6.39 us
    dot_general x6, matrix products, expert_mix(): jnp.einsum('fmk,kd->fmd', gated, down, preferred_element_type=jnp.float32)  5.96 us
    reshape x6, local copies, waits for them, and re-layouts, on_device(): sent = chip_sum.astype(jnp.bfloat16).reshape(chips, lanes, 128)  5.4 us
  transfers between devices with their start and end apart: 12, of which 12 were waited for; matrix products, arithmetic and copies ran while one was open for 1% of the time, Pallas kernels for 0%

profile of v12, /device:TPU:24, one launch (start us, length us, event | category | flops | bytes accessed | tf_op | source)
XLA Modules:
  0.0 252.3 jit_solution(9978853129903753687)
XLA Ops:
  0.0 0.9 reshape.169
  1.4 1.4 fusion.119
  2.8 13.1 %shard_map.73 = bf16[16,96,128]{2,1,0:T(8,128)(2,1)} custom-call(bf16[96,128]{1,0:T(8,128)(2,1)} %get-tuple-element.37.src_ref), custom_call_target="tpu_custom_call" | custom-call | tf_op jit(solution)/shard_map/pallas_call | solution.py:57
  16.1 0.7 select_reduce_fusion
  18.0 1.1 pad_maximum_fusion
  19.2 4.0 %fusion.22 = f32[32,4,4,256]{3,0,2,1:T(8,128)S(1)} fusion(bf16[1,4,3072,256]{3,2,1,0:T(8,128)(2,1)} %param.9, bf16[32,4,3072,1]{2,1,0,3:T(4,128)(2,1)S(1)} %bitcast.238), kind=kOutput, calls=%fused_computation.22 | convolution fusion | flops 805306368 | bytes 7602176 | tf_op jit(solution)/shard_map/fmd,edh->fmeh/dot_general | solution.py:178
  23.3 4.1 %fusion.78 = bf16[4,4,4,8,256]{4,3,2,1,0:T(8,128)(2,1)S(1)} fusion(bf16[1,4,3072,256]{3,2,1,0:T(8,128)(2,1)} %param.10, bf16[32,4,3072,1]{2,1,0,3:T(4,128)(2,1)S(1)} %bitcast.239, f32[32,4,4,256]{3,0,2,1:T(8,128)S(1)} %fusion.22, f32[32,4,4]{0,2,1:T(4,128)S(1)} %copy.156), kind=kOutput, calls=%fused_computation.42 | convolution fusion | flops 806223872 | bytes 7866368 | tf_op jit(solution)/shard_map/fmd,edh->fmeh/dot_general | solution.py:179
  27.4 1.0 fusion.142
  28.7 1.6 collective-permute-done.1
  30.7 0.9 reshape.175.sent_ref
  31.6 14.6 %shard_map.74 = (bf16[96,128]{1,0:T(8,128)(2,1)}, bf16[96,128]{1,0:T(8,128)(2,1)}) custom-call(bf16[16,96,128]{2,1,0:T(8,128)(2,1)} %reshape.175.sent_ref, bf16[96,128]{1,0:T(8,128)(2,1)} %get-tuple-element.38.current_ref), custom_call_target="tpu_custom_call" | custom-call | tf_op jit(solution)/shard_map/pallas_call | solution.py:132
  46.2 0.9 fusion.114
  48.2 9.6 %shard_map.75 = bf16[16,96,128]{2,1,0:T(8,128)(2,1)} custom-call(bf16[96,128]{1,0:T(8,128)(2,1)} %fusion.120.src_ref), custom_call_target="tpu_custom_call" | custom-call | tf_op jit(solution)/shard_map/pallas_call | solution.py:57
  57.8 1.9 collective-permute-done.2
  59.7 1.1 pad_maximum_fusion.1
  61.0 4.0 %fusion.20 = f32[32,4,4,256]{3,0,2,1:T(8,128)S(1)} fusion(bf16[1,4,3072,256]{3,2,1,0:T(8,128)(2,1)} %param.9, bf16[32,4,3072,1]{2,1,0,3:T(4,128)(2,1)S(1)} %bitcast.240), kind=kOutput, calls=%fused_computation.20 | convolution fusion | flops 805306368 | bytes 7602176 | tf_op jit(solution)/shard_map/fmd,edh->fmeh/dot_general | solution.py:178
  65.0 4.1 %fusion.81 = bf16[4,4,4,8,256]{4,3,2,1,0:T(8,128)(2,1)S(1)} fusion(bf16[1,4,3072,256]{3,2,1,0:T(8,128)(2,1)} %param.10, bf16[32,4,3072,1]{2,1,0,3:T(4,128)(2,1)S(1)} %bitcast.241, f32[32,4,4,256]{3,0,2,1:T(8,128)S(1)} %fusion.20, f32[32,4,4]{0,2,1:T(4,128)S(1)} %copy.161), kind=kOutput, calls=%fused_computation.43 | convolution fusion | flops 806223872 | bytes 7866368 | tf_op jit(solution)/shard_map/fmd,edh->fmeh/dot_general | solution.py:179
  69.2 1.0 fusion.143
  70.5 1.6 collective-permute-done.3
  72.5 0.9 reshape.178.sent_ref
  73.4 14.2 %shard_map.76 = (bf16[96,128]{1,0:T(8,128)(2,1)}, bf16[96,128]{1,0:T(8,128)(2,1)}) custom-call(bf16[16,96,128]{2,1,0:T(8,128)(2,1)} %reshape.178.sent_ref, bf16[96,128]{1,0:T(8,128)(2,1)} %copy-done.3), custom_call_target="tpu_custom_call" | custom-call | tf_op jit(solution)/shard_map/pallas_call | solution.py:132
  87.6 0.9 fusion.115
  88.8 0.7 fusion.121.src_ref
  89.5 9.5 %shard_map.77 = bf16[16,96,128]{2,1,0:T(8,128)(2,1)} custom-call(bf16[96,128]{1,0:T(8,128)(2,1)} %fusion.121.src_ref), custom_call_target="tpu_custom_call" | custom-call | tf_op jit(solution)/shard_map/pallas_call | solution.py:57
  99.1 1.9 collective-permute-done.4
  101.0 1.1 pad_maximum_fusion.2
  102.3 4.0 %fusion.18 = f32[32,4,4,256]{3,0,2,1:T(8,128)S(1)} fusion(bf16[1,4,3072,256]{3,2,1,0:T(8,128)(2,1)} %param.9, bf16[32,4,3072,1]{2,1,0,3:T(4,128)(2,1)S(1)} %bitcast.242), kind=kOutput, calls=%fused_computation.18 | convolution fusion | flops 805306368 | bytes 7602176 | tf_op jit(solution)/shard_map/fmd,edh->fmeh/dot_general | solution.py:178
  106.3 4.1 %fusion.84 = bf16[4,4,4,8,256]{4,3,2,1,0:T(8,128)(2,1)S(1)} fusion(bf16[1,4,3072,256]{3,2,1,0:T(8,128)(2,1)} %param.10, bf16[32,4,3072,1]{2,1,0,3:T(4,128)(2,1)S(1)} %bitcast.243, f32[32,4,4,256]{3,0,2,1:T(8,128)S(1)} %fusion.18, f32[32,4,4]{0,2,1:T(4,128)S(1)} %copy.166), kind=kOutput, calls=%fused_computation.44 | convolution fusion | flops 806223872 | bytes 7866368 | tf_op jit(solution)/shard_map/fmd,edh->fmeh/dot_general | solution.py:179
  110.5 1.0 fusion.144
  111.8 1.6 collective-permute-done.5
  113.8 0.9 reshape.181.sent_ref
  114.7 14.2 %shard_map.78 = (bf16[96,128]{1,0:T(8,128)(2,1)}, bf16[96,128]{1,0:T(8,128)(2,1)}) custom-call(bf16[16,96,128]{2,1,0:T(8,128)(2,1)} %reshape.181.sent_ref, bf16[96,128]{1,0:T(8,128)(2,1)} %copy-done.4), custom_call_target="tpu_custom_call" | custom-call | tf_op jit(solution)/shard_map/pallas_call | solution.py:132
  128.9 0.9 fusion.116
  130.1 0.7 fusion.122.src_ref
  130.8 9.5 %shard_map.79 = bf16[16,96,128]{2,1,0:T(8,128)(2,1)} custom-call(bf16[96,128]{1,0:T(8,128)(2,1)} %fusion.122.src_ref), custom_call_target="tpu_custom_call" | custom-call | tf_op jit(solution)/shard_map/pallas_call | solution.py:57
  140.4 1.9 collective-permute-done.6
  142.3 1.1 pad_maximum_fusion.3
  143.6 4.0 %fusion.16 = f32[32,4,4,256]{3,0,2,1:T(8,128)S(1)} fusion(bf16[1,4,3072,256]{3,2,1,0:T(8,128)(2,1)} %param.9, bf16[32,4,3072,1]{2,1,0,3:T(4,128)(2,1)S(1)} %bitcast.244), kind=kOutput, calls=%fused_computation.16 | convolution fusion | flops 805306368 | bytes 7602176 | tf_op jit(solution)/shard_map/fmd,edh->fmeh/dot_general | solution.py:178
  147.6 4.1 %fusion.87 = bf16[4,4,4,8,256]{4,3,2,1,0:T(8,128)(2,1)S(1)} fusion(bf16[1,4,3072,256]{3,2,1,0:T(8,128)(2,1)} %param.10, bf16[32,4,3072,1]{2,1,0,3:T(4,128)(2,1)S(1)} %bitcast.245, f32[32,4,4,256]{3,0,2,1:T(8,128)S(1)} %fusion.16, f32[32,4,4]{0,2,1:T(4,128)S(1)} %copy.171), kind=kOutput, calls=%fused_computation.45 | convolution fusion | flops 806223872 | bytes 7866368 | tf_op jit(solution)/shard_map/fmd,edh->fmeh/dot_general | solution.py:179
  151.8 1.0 fusion.145
  153.1 1.6 collective-permute-done.7
  155.1 0.9 reshape.184.sent_ref
  156.0 13.5 %shard_map.80 = (bf16[96,128]{1,0:T(8,128)(2,1)}, bf16[96,128]{1,0:T(8,128)(2,1)}) custom-call(bf16[16,96,128]{2,1,0:T(8,128)(2,1)} %reshape.184.sent_ref, bf16[96,128]{1,0:T(8,128)(2,1)} %copy-done.5), custom_call_target="tpu_custom_call" | custom-call | tf_op jit(solution)/shard_map/pallas_call | solution.py:132
  169.5 0.9 fusion.117
  171.4 9.5 %shard_map.81 = bf16[16,96,128]{2,1,0:T(8,128)(2,1)} custom-call(bf16[96,128]{1,0:T(8,128)(2,1)} %fusion.123.src_ref), custom_call_target="tpu_custom_call" | custom-call | tf_op jit(solution)/shard_map/pallas_call | solution.py:57
  181.2 1.9 collective-permute-done.8
  183.1 1.1 pad_maximum_fusion.4
  184.4 4.0 %fusion.14 = f32[32,4,4,256]{3,0,2,1:T(8,128)S(1)} fusion(bf16[1,4,3072,256]{3,2,1,0:T(8,128)(2,1)} %param.9, bf16[32,4,3072,1]{2,1,0,3:T(4,128)(2,1)S(1)} %bitcast.246), kind=kOutput, calls=%fused_computation.14 | convolution fusion | flops 805306368 | bytes 7602176 | tf_op jit(solution)/shard_map/fmd,edh->fmeh/dot_general | solution.py:178
  188.4 4.1 %fusion.90 = bf16[4,4,4,8,256]{4,3,2,1,0:T(8,128)(2,1)S(1)} fusion(bf16[1,4,3072,256]{3,2,1,0:T(8,128)(2,1)} %param.10, bf16[32,4,3072,1]{2,1,0,3:T(4,128)(2,1)S(1)} %bitcast.247, f32[32,4,4,256]{3,0,2,1:T(8,128)S(1)} %fusion.14, f32[32,4,4]{0,2,1:T(4,128)S(1)} %copy.176), kind=kOutput, calls=%fused_computation.46 | convolution fusion | flops 806223872 | bytes 7866368 | tf_op jit(solution)/shard_map/fmd,edh->fmeh/dot_general | solution.py:179
  192.6 1.0 fusion.146
  194.0 1.5 collective-permute-done.9
  195.9 0.9 reshape.187.sent_ref
  196.8 13.5 %shard_map.82 = (bf16[96,128]{1,0:T(8,128)(2,1)}, bf16[96,128]{1,0:T(8,128)(2,1)}) custom-call(bf16[16,96,128]{2,1,0:T(8,128)(2,1)} %reshape.187.sent_ref, bf16[96,128]{1,0:T(8,128)(2,1)} %copy-done.1), custom_call_target="tpu_custom_call" | custom-call | tf_op jit(solution)/shard_map/pallas_call | solution.py:132
  210.3 0.9 fusion.118
  212.2 9.5 %shard_map.83 = bf16[16,96,128]{2,1,0:T(8,128)(2,1)} custom-call(bf16[96,128]{1,0:T(8,128)(2,1)} %fusion.124.src_ref), custom_call_target="tpu_custom_call" | custom-call | tf_op jit(solution)/shard_map/pallas_call | solution.py:57
  221.9 1.8 collective-permute-done.10
  223.8 1.1 pad_maximum_fusion.5
  225.0 4.0 %fusion.12 = f32[32,4,4,256]{3,0,2,1:T(8,128)S(1)} fusion(bf16[1,4,3072,256]{3,2,1,0:T(8,128)(2,1)} %param.9, bf16[32,4,3072,1]{2,1,0,3:T(4,128)(2,1)S(1)} %bitcast.248), kind=kOutput, calls=%fused_computation.12 | convolution fusion | flops 805306368 | bytes 7602176 | tf_op jit(solution)/shard_map/fmd,edh->fmeh/dot_general | solution.py:178
  229.1 4.1 %fusion.93 = bf16[4,4,4,8,256]{4,3,2,1,0:T(8,128)(2,1)S(1)} fusion(bf16[1,4,3072,256]{3,2,1,0:T(8,128)(2,1)} %param.10, bf16[32,4,3072,1]{2,1,0,3:T(4,128)(2,1)S(1)} %bitcast.249, f32[32,4,4,256]{3,0,2,1:T(8,128)S(1)} %fusion.12, f32[32,4,4]{0,2,1:T(4,128)S(1)} %copy.181), kind=kOutput, calls=%fused_computation.47 | convolution fusion | flops 806223872 | bytes 7866368 | tf_op jit(solution)/shard_map/fmd,edh->fmeh/dot_general | solution.py:179
  233.2 1.0 fusion.147
  234.6 1.5 collective-permute-done.11
  236.5 0.9 reshape.190.sent_ref
  237.4 13.5 %shard_map.84 = (bf16[96,128]{1,0:T(8,128)(2,1)}, bf16[96,128]{1,0:T(8,128)(2,1)}) custom-call(bf16[16,96,128]{2,1,0:T(8,128)(2,1)} %reshape.190.sent_ref, bf16[96,128]{1,0:T(8,128)(2,1)} %copy-done.2), custom_call_target="tpu_custom_call" | custom-call | tf_op jit(solution)/shard_map/pallas_call | solution.py:132
  250.9 0.8 fusion.125
  (147 shorter events, 12.3 us)
Async XLA Ops:
  16.0 2.0 collective-permute-start
  19.2 8.2 %slice-start = ((s8[6291456]{0:T(1024)(128)(4,1)}), s8[4194304]{0:T(1024)(128)(4,1)S(1)}, s32[]{:S(2)}) async-start(s8[6291456]{0:T(1024)(128)(4,1)} %bitcast.214), calls=%async_computation | async-start | bytes 8388608
  23.3 4.2 %slice-start.1 = ((s8[6291456]{0:T(1024)(128)(4,1)}), s8[2097152]{0:T(1024)(128)(4,1)S(1)}, s32[]{:S(2)}) async-start(s8[6291456]{0:T(1024)(128)(4,1)} %bitcast.214), calls=%async_computation.1 | async-start | bytes 4194304
  27.4 20.0 %copy-start = (f32[1,3072]{1,0:T(1,128)S(1)}, f32[1,3072]{1,0:T(1,128)}, u32[]{:S(2)}) copy-start(f32[1,3072]{1,0:T(1,128)} %param.8) | copy-start | bytes 36868
  28.5 1.8 collective-permute-start.1
  47.1 18.0 %copy-start.3 = (bf16[96,128]{1,0:T(8,128)(2,1)}, bf16[96,128]{1,0:T(8,128)(2,1)S(1)}, u32[]{:S(2)}) copy-start(bf16[96,128]{1,0:T(8,128)(2,1)S(1)} %get-tuple-element.36.current_ref) | copy-start | bytes 73732
  57.7 2.0 collective-permute-start.2
  61.0 8.2 %slice-start.2 = ((s8[6291456]{0:T(1024)(128)(4,1)}), s8[4194304]{0:T(1024)(128)(4,1)S(1)}, s32[]{:S(2)}) async-start(s8[6291456]{0:T(1024)(128)(4,1)} %bitcast.217), calls=%async_computation.2 | async-start | bytes 8388608
  65.0 4.2 %slice-start.3 = ((s8[6291456]{0:T(1024)(128)(4,1)}), s8[2097152]{0:T(1024)(128)(4,1)S(1)}, s32[]{:S(2)}) async-start(s8[6291456]{0:T(1024)(128)(4,1)} %bitcast.217), calls=%async_computation.3 | async-start | bytes 4194304
  70.2 1.8 collective-permute-start.3
  88.4 17.9 %copy-start.4 = (bf16[96,128]{1,0:T(8,128)(2,1)}, bf16[96,128]{1,0:T(8,128)(2,1)S(1)}, u32[]{:S(2)}) copy-start(bf16[96,128]{1,0:T(8,128)(2,1)S(1)} %get-tuple-element.34.current_ref) | copy-start | bytes 73732
  99.0 2.0 collective-permute-start.4
  102.3 8.2 %slice-start.4 = ((s8[6291456]{0:T(1024)(128)(4,1)}), s8[4194304]{0:T(1024)(128)(4,1)S(1)}, s32[]{:S(2)}) async-start(s8[6291456]{0:T(1024)(128)(4,1)} %bitcast.220), calls=%async_computation.4 | async-start | bytes 8388608
  106.3 4.2 %slice-start.5 = ((s8[6291456]{0:T(1024)(128)(4,1)}), s8[2097152]{0:T(1024)(128)(4,1)S(1)}, s32[]{:S(2)}) async-start(s8[6291456]{0:T(1024)(128)(4,1)} %bitcast.220), calls=%async_computation.5 | async-start | bytes 4194304
  111.5 1.8 collective-permute-start.5
  129.7 17.9 %copy-start.5 = (bf16[96,128]{1,0:T(8,128)(2,1)}, bf16[96,128]{1,0:T(8,128)(2,1)S(1)}, u32[]{:S(2)}) copy-start(bf16[96,128]{1,0:T(8,128)(2,1)S(1)} %get-tuple-element.32.current_ref) | copy-start | bytes 73732
  140.3 2.0 collective-permute-start.6
  143.6 8.2 %slice-start.6 = ((s8[6291456]{0:T(1024)(128)(4,1)}), s8[4194304]{0:T(1024)(128)(4,1)S(1)}, s32[]{:S(2)}) async-start(s8[6291456]{0:T(1024)(128)(4,1)} %bitcast.223), calls=%async_computation.6 | async-start | bytes 8388608
  147.6 4.2 %slice-start.7 = ((s8[6291456]{0:T(1024)(128)(4,1)}), s8[2097152]{0:T(1024)(128)(4,1)S(1)}, s32[]{:S(2)}) async-start(s8[6291456]{0:T(1024)(128)(4,1)} %bitcast.223), calls=%async_computation.7 | async-start | bytes 4194304
  152.9 1.8 collective-permute-start.7
  170.3 18.1 %copy-start.1 = (bf16[96,128]{1,0:T(8,128)(2,1)}, bf16[96,128]{1,0:T(8,128)(2,1)S(1)}, u32[]{:S(2)}) copy-start(bf16[96,128]{1,0:T(8,128)(2,1)S(1)} %get-tuple-element.30.current_ref) | copy-start | bytes 73732
  180.9 2.2 collective-permute-start.8
  184.4 8.2 %slice-start.8 = ((s8[6291456]{0:T(1024)(128)(4,1)}), s8[4194304]{0:T(1024)(128)(4,1)S(1)}, s32[]{:S(2)}) async-start(s8[6291456]{0:T(1024)(128)(4,1)} %bitcast.226), calls=%async_computation.8 | async-start | bytes 8388608
  188.4 4.2 %slice-start.9 = ((s8[6291456]{0:T(1024)(128)(4,1)}), s8[2097152]{0:T(1024)(128)(4,1)S(1)}, s32[]{:S(2)}) async-start(s8[6291456]{0:T(1024)(128)(4,1)} %bitcast.226), calls=%async_computation.9 | async-start | bytes 4194304
  192.5 1.4 copy-start.6
  192.6 29.2 %copy-start.7 = (bf16[96,128]{1,0:T(8,128)(2,1)S(1)}, bf16[96,128]{1,0:T(8,128)(2,1)}, u32[]{:S(2)}) copy-start(bf16[96,128]{1,0:T(8,128)(2,1)} %get-tuple-element.18) | copy-start | bytes 73732
  192.6 29.3 %copy-start.8 = (bf16[96,128]{1,0:T(8,128)(2,1)S(1)}, bf16[96,128]{1,0:T(8,128)(2,1)}, u32[]{:S(2)}) copy-start(bf16[96,128]{1,0:T(8,128)(2,1)} %get-tuple-element.20) | copy-start | bytes 73732
  193.7 1.8 collective-permute-start.9
  211.2 17.9 %copy-start.2 = (bf16[96,128]{1,0:T(8,128)(2,1)}, bf16[96,128]{1,0:T(8,128)(2,1)S(1)}, u32[]{:S(2)}) copy-start(bf16[96,128]{1,0:T(8,128)(2,1)S(1)} %get-tuple-element.28.current_ref) | copy-start | bytes 73732
  221.7 2.0 collective-permute-start.10
  225.0 8.2 %slice-start.10 = ((s8[6291456]{0:T(1024)(128)(4,1)}), s8[4194304]{0:T(1024)(128)(4,1)S(1)}, s32[]{:S(2)}) async-start(s8[6291456]{0:T(1024)(128)(4,1)} %bitcast.229), calls=%async_computation.10 | async-start | bytes 8388608
  229.0 4.2 %slice-start.11 = ((s8[6291456]{0:T(1024)(128)(4,1)}), s8[2097152]{0:T(1024)(128)(4,1)S(1)}, s32[]{:S(2)}) async-start(s8[6291456]{0:T(1024)(128)(4,1)} %bitcast.229), calls=%async_computation.11 | async-start | bytes 4194304
  233.2 1.3 copy-start.9
  233.2 1.4 copy-start.10
  234.3 1.8 collective-permute-start.11
